TPU v7x, 128 devices: a whole 4x4x4 slice. The times are simulated.
128 devices in a mesh: region: 16 (over y, x_hi, core), ctx: 8 (over z, x_lo).
Axes of the slice: x: 4 (x_hi: 2, x_lo: 2; x = x_hi * 2 + x_lo), y: 4, z: 4, core: 2. Of those that a mesh axis runs over, the one named last changes fastest.
Arguments:
- tokens: bfloat16 [16, 4096, 1152], P('region', 'ctx'), may hold values from -6 to 6
- element_ids: int32 [16, 4096], P('region', 'ctx'), may hold values from 0 to 16383, as said below
- element_slot: int32 [16384], replicated, may hold values from 0 to 16383, as said below
- live_count: int32 [16, 8], P('region', 'ctx'), may hold values from 128 to 512
- cond_table: bfloat16 [16384, 1152], P(('region', 'ctx')), may hold values from -6 to 6
- w_ada: bfloat16 [1152, 3456], replicated, may hold values from -0.1875 to 0.1875
- b_ada: float32 [3456], replicated, may hold values from -3 to 3
- w_qkv: bfloat16 [1152, 3456], replicated, may hold values from -8 to 8
- w_out: bfloat16 [1152, 1152], replicated, may hold values from -0.1875 to 0.1875
Outputs:
- block_out: bfloat16 [16, 4096, 1152], P('region', 'ctx')
Inputs may be any that keep to these rules, and one draw needn't show every extreme that they name: element_ids: within each device's block of 512 patches (region r, positions c * 512 to (c + 1) * 512 - 1, device r * 8 + c of region+ctx), at most 6 patches name elements whose table row lies on one device (rows o * 128 to (o + 1) * 128 - 1); in every block some device is named by exactly 6 solid patches. element_slot is a permutation: element e is row element_slot[e] of cond_table.
All inputs are finite; a program needn't handle non-finite values.
Results may differ from a plain program's by a relative error of at most 0.027.
Values may be sent and summed in bfloat16 or wider, within the bound.
A program may use at most 192 MiB of HBM per device.

v0:
```python
import math

import jax
import jax.numpy as jnp
from jax import lax
from jax.sharding import PartitionSpec as P

HEADS = 16


def layer_modulate(device_tokens, mods, width):
    values = device_tokens.astype(jnp.float32)
    center = jnp.mean(values, axis=1, keepdims=True)
    spread = jnp.mean((values - center) ** 2, axis=1, keepdims=True)
    normed = (values - center) * lax.rsqrt(spread + 1e-06)
    shift = mods[:, :width]
    scale = mods[:, width : 2 * width]
    return (normed * (1.0 + scale) + shift).astype(jnp.bfloat16)


def per_device(
    tokens, element_ids, element_slot, live_count, cond_table, w_ada, b_ada, w_qkv, w_out
):
    device_tokens = tokens[0]
    tok_rows, width = device_tokens.shape
    owners = lax.axis_size(("region", "ctx"))
    elem_rows = cond_table.shape[0]
    capacity = max(2, 3 * tok_rows // (2 * owners))
    slots = element_slot[element_ids[0]]
    owner_index = slots // elem_rows
    local_row = slots % elem_rows
    position = jnp.arange(tok_rows, dtype=jnp.int32)
    solid = position < live_count[0, 0]
    earlier = (
        (owner_index[:, None] == owner_index[None, :])
        & (position[None, :] < position[:, None])
        & solid[None, :]
    )
    place_rank = jnp.sum(earlier.astype(jnp.int32), axis=1)
    target = jnp.where(solid, owner_index * capacity + place_rank, owners * capacity)
    requests = jnp.zeros((owners * capacity,), jnp.int32).at[target].set(local_row, mode="drop")
    asked = lax.all_to_all(
        requests.reshape(owners, capacity),
        ("region", "ctx"),
        split_axis=0,
        concat_axis=0,
        tiled=True,
    ).reshape(-1)
    pick_at = jnp.minimum(target, owners * capacity - 1)
    served = cond_table[asked].reshape(owners, capacity, width)
    replies = lax.all_to_all(served, ("region", "ctx"), split_axis=0, concat_axis=0, tiled=True)
    picked = replies.reshape(owners * capacity, width)[pick_at]
    activated = jnp.where(solid[:, None], jax.nn.silu(picked.astype(jnp.float32)), 0.0).astype(
        jnp.bfloat16
    )
    mods = (jnp.dot(activated, w_ada, preferred_element_type=jnp.float32) + b_ada).astype(
        jnp.bfloat16
    )
    mods = mods.astype(jnp.float32)
    modulated = layer_modulate(device_tokens, mods, width)
    qkv = jnp.dot(modulated, w_qkv, preferred_element_type=jnp.float32).astype(jnp.bfloat16)
    queries = qkv[:, :width]
    keys_here = qkv[:, width : 2 * width]
    values_here = qkv[:, 2 * width :]
    head_dim = width // HEADS
    inverse_root = 1.0 / math.sqrt(head_dim)
    query_heads = queries.reshape(tok_rows, HEADS, head_dim)
    initial = (
        jnp.full((HEADS, tok_rows), -1e30, jnp.float32),
        jnp.zeros((HEADS, tok_rows), jnp.float32),
        jnp.zeros((HEADS, tok_rows, head_dim), jnp.float32),
    )
    keys_piece = lax.all_gather(keys_here, "ctx", axis=0, tiled=True)
    values_piece = lax.all_gather(values_here, "ctx", axis=0, tiled=True)
    piece_rows = keys_piece.shape[0]
    block_rows = math.gcd(piece_rows, 512)
    key_blocks = keys_piece.reshape(piece_rows // block_rows, block_rows, HEADS, head_dim)
    value_blocks = values_piece.reshape(piece_rows // block_rows, block_rows, HEADS, head_dim)

    def advance(state, blocks):
        running_max, denominator, weighted = state
        key_block, value_block = blocks
        scores = (
            jnp.einsum("qhe,khe->hqk", query_heads, key_block, preferred_element_type=jnp.float32)
            * inverse_root
        )
        new_max = jnp.maximum(running_max, jnp.max(scores, axis=2))
        shrink = jnp.exp(running_max - new_max)
        expo = jnp.exp(scores - new_max[:, :, None])
        denominator = denominator * shrink + jnp.sum(expo, axis=2)
        weighted = weighted * shrink[:, :, None] + jnp.einsum(
            "hqk,khe->hqe",
            expo.astype(jnp.bfloat16),
            value_block,
            preferred_element_type=jnp.float32,
        )
        return ((new_max, denominator, weighted), None)

    result, _ = lax.scan(advance, initial, (key_blocks, value_blocks))
    final_max, denominator, weighted = result
    result = weighted / denominator[:, :, None]
    attended = jnp.transpose(result, (1, 0, 2)).reshape(tok_rows, width).astype(jnp.bfloat16)
    projected = jnp.dot(attended, w_out, preferred_element_type=jnp.float32)
    gate = mods[:, 2 * width :]
    output = (device_tokens.astype(jnp.float32) + gate * projected).astype(jnp.bfloat16)
    return output[None]


def solution(mesh):
    placed = (
        P("region", "ctx", None),
        P("region", "ctx"),
        P(),
        P("region", "ctx"),
        P(("region", "ctx"), None),
        P(),
        P(),
        P(),
        P(),
    )
    return jax.shard_map(
        per_device, mesh=mesh, in_specs=placed, out_specs=P("region", "ctx", None), check_vma=False
    )
```

profile of v0, /device:TPU:0, one launch (start us, length us, event | category | flops | bytes accessed | tf_op | source)
XLA Modules:
  0.0 790.5 jit_solution(2168846437949532841)
XLA Ops:
  14.5 20.5 %all_to_all.14 = s32[128,1,6]{2,1,0:T(1,128)S(1)} all-to-all(s32[128,1,6]{2,1,0:T(1,128)S(1)} %bitcast.77), channel_id=1, replica_groups=mesh['region'=16,'ctx'=8] {'region','ctx'}, dimensions={0} | all-to-all | bytes 6144 | tf_op jit(solution)/shard_map/all_to_all | solution.py:42
  53.3 29.6 %all-to-all-done.1 = bf16[128,6,1152]{2,1,0:T(8,128)(2,1)} async-done(((bf16[128,6,1152]{2,1,0:T(8,128)(2,1)}), bf16[128,6,1152]{2,1,0:T(8,128)(2,1)}, u32[]{:S(2)}, u32[]{:S(2)}) %all-to-all-start.1) | async-done | bytes 1769504 | tf_op jit(solution)/shard_map/all_to_all | solution.py:51
  100.2 11.4 %convolution_convert_fusion = bf16[512,3456]{1,0:T(8,128)(2,1)S(1)} fusion(bf16[1152,3456]{1,0:T(8,128)(2,1)} %param.18, bf16[1,512,1152]{2,1,0:T(8,128)(2,1)S(1)} %copy-done.2, f32[512,3456]{1,0:T(8,128)S(1)} %fusion.19, f32[512]{0:T(512)S(1)} %add_rsqrt_fusion, f32[512]{0:T(512)S(1)} %broadcast_multiply_fusion), kind=kOutput, calls=%fused_computation.28 | convolution fusion | flops 4082761728 | bytes 17403904 | tf_op jit(solution)/shard_map/dot_general | solution.py:61
  116.8 180.0 %all-gather.3.cloned.1.call-done = bf16[4096,1152]{1,0:T(8,128)(2,1)} async-done(((bf16[512,1152]{1,0:T(8,128)(2,1)}), bf16[4096,1152]{1,0:T(8,128)(2,1)}) %all-gather.3.cloned.1.call-update) | async-done | bytes 9437200 | tf_op jit(solution)/shard_map/all_gather | solution.py:73
  296.8 33.2 %reshape.260 = bf16[8,512,16,72]{3,2,1,0:T(8,128)(2,1)} reshape(bf16[4096,1152]{1,0:T(8,128)(2,1)} %all-gather.3.cloned.1.call-done) | data formatting | bytes 18874368 | tf_op jit(solution)/shard_map/reshape | solution.py:77
  330.0 21.5 %copy.32 = bf16[8,512,16,72]{1,3,2,0:T(8,128)(2,1)} copy(bf16[8,512,16,72]{3,2,1,0:T(8,128)(2,1)} %reshape.260) | data formatting | bytes 18874368
  351.5 136.0 %all-gather.5.cloned.1.call-done = bf16[4096,1152]{1,0:T(8,128)(2,1)} async-done(((bf16[512,1152]{1,0:T(8,128)(2,1)}), bf16[4096,1152]{1,0:T(8,128)(2,1)}) %all-gather.5.cloned.1.call-update) | async-done | bytes 9437200 | tf_op jit(solution)/shard_map/all_gather | solution.py:74
  487.5 33.2 %reshape.261 = bf16[8,512,16,72]{3,2,1,0:T(8,128)(2,1)} reshape(bf16[4096,1152]{1,0:T(8,128)(2,1)} %all-gather.5.cloned.1.call-done) | data formatting | bytes 18874368 | tf_op jit(solution)/shard_map/reshape | solution.py:78
  520.7 21.4 %copy.33 = bf16[8,512,16,72]{1,3,2,0:T(8,128)(2,1)} copy(bf16[8,512,16,72]{3,2,1,0:T(8,128)(2,1)} %reshape.261) | data formatting | bytes 18874368
  542.2 234.7 %while.15 = (s32[]{:T(128)}, f32[16,512]{1,0:T(8,128)S(1)}, f32[16,512]{1,0:T(8,128)S(1)}, f32[16,512,72]{1,2,0:T(8,128)}, bf16[8,512,16,72]{1,3,2,0:T(8,128)(2,...) while((s32[]{:T(128)}, f32[16,512]{1,0:T(8,128)S(1)}, ...), condition=%wide.region_7.8_spmd.clone, body=%wide.region_4.7_spmd.clone.sunk | while | flops 1243324416 | bytes 59114596 | solution.py:99
  560.5 10.4 %fusion.69 = f32[16,512,72]{1,2,0:T(8,128)} fusion(f32[16,512,72]{1,2,0:T(8,128)} %get-tuple-element.185, f32[16,512,512]{2,1,0:T(8,128)} %get-tuple-element.170, f32[16,512]{1,0:T(8,128)S(1)} %select_maximum_fusion.2, bf16[8,512,16,72]{1,3,2,0:T(8,128)(2,1)} %get-tuple-element.197, s32[]{:T(128)} %get-tuple-element.182, ...), kind=kOutput, calls=%fused_computation.13.clone.1 | convolution fusion | flops 618332160 | bytes 22741504 | tf_op jit(solution)/shard_map/while/body/eval_jaxpr/hqk,khe->hqe/dot_general | solution.py:91
  570.9 9.7 %bitcast_reduce_fusion.2 = (f32[16,512]{1,0:T(8,128)S(1)}, f32[16,512,512]{2,1,0:T(8,128)}) fusion(bf16[512,16,72]{0,2,1:T(8,128)(2,1)} %get-tuple-element.196, bf16[8,512,16,72]{1,3,2,0:T(8,128)(2,1)} %get-tuple-element.195, s32[]{:T(128)} %get-tuple-element.182), kind=kOutput, calls=%fused_computation.5.clone.1 | convolution fusion | flops 612360192 | bytes 19169792 | tf_op jit(solution)/shard_map/while/body/eval_jaxpr/qhe,khe->hqk/dot_general | solution.py:84
  589.2 11.1 %fusion.69 = f32[16,512,72]{1,2,0:T(8,128)} fusion(f32[16,512,72]{1,2,0:T(8,128)} %get-tuple-element.185, f32[16,512,512]{2,1,0:T(8,128)} %get-tuple-element.170, f32[16,512]{1,0:T(8,128)S(1)} %select_maximum_fusion.2, bf16[8,512,16,72]{1,3,2,0:T(8,128)(2,1)} %get-tuple-element.197, s32[]{:T(128)} %get-tuple-element.182, ...), kind=kOutput, calls=%fused_computation.13.clone.1 | convolution fusion | flops 618332160 | bytes 22741504 | tf_op jit(solution)/shard_map/while/body/eval_jaxpr/hqk,khe->hqe/dot_general | solution.py:91
  600.3 9.7 %bitcast_reduce_fusion.2 = (f32[16,512]{1,0:T(8,128)S(1)}, f32[16,512,512]{2,1,0:T(8,128)}) fusion(bf16[512,16,72]{0,2,1:T(8,128)(2,1)} %get-tuple-element.196, bf16[8,512,16,72]{1,3,2,0:T(8,128)(2,1)} %get-tuple-element.195, s32[]{:T(128)} %get-tuple-element.182), kind=kOutput, calls=%fused_computation.5.clone.1 | convolution fusion | flops 612360192 | bytes 19169792 | tf_op jit(solution)/shard_map/while/body/eval_jaxpr/qhe,khe->hqk/dot_general | solution.py:84
  618.6 11.1 %fusion.69 = f32[16,512,72]{1,2,0:T(8,128)} fusion(f32[16,512,72]{1,2,0:T(8,128)} %get-tuple-element.185, f32[16,512,512]{2,1,0:T(8,128)} %get-tuple-element.170, f32[16,512]{1,0:T(8,128)S(1)} %select_maximum_fusion.2, bf16[8,512,16,72]{1,3,2,0:T(8,128)(2,1)} %get-tuple-element.197, s32[]{:T(128)} %get-tuple-element.182, ...), kind=kOutput, calls=%fused_computation.13.clone.1 | convolution fusion | flops 618332160 | bytes 22741504 | tf_op jit(solution)/shard_map/while/body/eval_jaxpr/hqk,khe->hqe/dot_general | solution.py:91
  629.7 9.7 %bitcast_reduce_fusion.2 = (f32[16,512]{1,0:T(8,128)S(1)}, f32[16,512,512]{2,1,0:T(8,128)}) fusion(bf16[512,16,72]{0,2,1:T(8,128)(2,1)} %get-tuple-element.196, bf16[8,512,16,72]{1,3,2,0:T(8,128)(2,1)} %get-tuple-element.195, s32[]{:T(128)} %get-tuple-element.182), kind=kOutput, calls=%fused_computation.5.clone.1 | convolution fusion | flops 612360192 | bytes 19169792 | tf_op jit(solution)/shard_map/while/body/eval_jaxpr/qhe,khe->hqk/dot_general | solution.py:84
  648.1 11.1 %fusion.69 = f32[16,512,72]{1,2,0:T(8,128)} fusion(f32[16,512,72]{1,2,0:T(8,128)} %get-tuple-element.185, f32[16,512,512]{2,1,0:T(8,128)} %get-tuple-element.170, f32[16,512]{1,0:T(8,128)S(1)} %select_maximum_fusion.2, bf16[8,512,16,72]{1,3,2,0:T(8,128)(2,1)} %get-tuple-element.197, s32[]{:T(128)} %get-tuple-element.182, ...), kind=kOutput, calls=%fused_computation.13.clone.1 | convolution fusion | flops 618332160 | bytes 22741504 | tf_op jit(solution)/shard_map/while/body/eval_jaxpr/hqk,khe->hqe/dot_general | solution.py:91
  659.1 9.7 %bitcast_reduce_fusion.2 = (f32[16,512]{1,0:T(8,128)S(1)}, f32[16,512,512]{2,1,0:T(8,128)}) fusion(bf16[512,16,72]{0,2,1:T(8,128)(2,1)} %get-tuple-element.196, bf16[8,512,16,72]{1,3,2,0:T(8,128)(2,1)} %get-tuple-element.195, s32[]{:T(128)} %get-tuple-element.182), kind=kOutput, calls=%fused_computation.5.clone.1 | convolution fusion | flops 612360192 | bytes 19169792 | tf_op jit(solution)/shard_map/while/body/eval_jaxpr/qhe,khe->hqk/dot_general | solution.py:84
  677.5 11.1 %fusion.69 = f32[16,512,72]{1,2,0:T(8,128)} fusion(f32[16,512,72]{1,2,0:T(8,128)} %get-tuple-element.185, f32[16,512,512]{2,1,0:T(8,128)} %get-tuple-element.170, f32[16,512]{1,0:T(8,128)S(1)} %select_maximum_fusion.2, bf16[8,512,16,72]{1,3,2,0:T(8,128)(2,1)} %get-tuple-element.197, s32[]{:T(128)} %get-tuple-element.182, ...), kind=kOutput, calls=%fused_computation.13.clone.1 | convolution fusion | flops 618332160 | bytes 22741504 | tf_op jit(solution)/shard_map/while/body/eval_jaxpr/hqk,khe->hqe/dot_general | solution.py:91
  706.9 11.1 %fusion.69 = f32[16,512,72]{1,2,0:T(8,128)} fusion(f32[16,512,72]{1,2,0:T(8,128)} %get-tuple-element.185, f32[16,512,512]{2,1,0:T(8,128)} %get-tuple-element.170, f32[16,512]{1,0:T(8,128)S(1)} %select_maximum_fusion.2, bf16[8,512,16,72]{1,3,2,0:T(8,128)(2,1)} %get-tuple-element.197, s32[]{:T(128)} %get-tuple-element.182, ...), kind=kOutput, calls=%fused_computation.13.clone.1 | convolution fusion | flops 618332160 | bytes 22741504 | tf_op jit(solution)/shard_map/while/body/eval_jaxpr/hqk,khe->hqe/dot_general | solution.py:91
  718.0 9.7 %bitcast_reduce_fusion.2 = (f32[16,512]{1,0:T(8,128)S(1)}, f32[16,512,512]{2,1,0:T(8,128)}) fusion(bf16[512,16,72]{0,2,1:T(8,128)(2,1)} %get-tuple-element.196, bf16[8,512,16,72]{1,3,2,0:T(8,128)(2,1)} %get-tuple-element.195, s32[]{:T(128)} %get-tuple-element.182), kind=kOutput, calls=%fused_computation.5.clone.1 | convolution fusion | flops 612360192 | bytes 19169792 | tf_op jit(solution)/shard_map/while/body/eval_jaxpr/qhe,khe->hqk/dot_general | solution.py:84
  736.3 11.1 %fusion.69 = f32[16,512,72]{1,2,0:T(8,128)} fusion(f32[16,512,72]{1,2,0:T(8,128)} %get-tuple-element.185, f32[16,512,512]{2,1,0:T(8,128)} %get-tuple-element.170, f32[16,512]{1,0:T(8,128)S(1)} %select_maximum_fusion.2, bf16[8,512,16,72]{1,3,2,0:T(8,128)(2,1)} %get-tuple-element.197, s32[]{:T(128)} %get-tuple-element.182, ...), kind=kOutput, calls=%fused_computation.13.clone.1 | convolution fusion | flops 618332160 | bytes 22741504 | tf_op jit(solution)/shard_map/while/body/eval_jaxpr/hqk,khe->hqe/dot_general | solution.py:91
  747.4 9.7 %bitcast_reduce_fusion.2 = (f32[16,512]{1,0:T(8,128)S(1)}, f32[16,512,512]{2,1,0:T(8,128)}) fusion(bf16[512,16,72]{0,2,1:T(8,128)(2,1)} %get-tuple-element.196, bf16[8,512,16,72]{1,3,2,0:T(8,128)(2,1)} %get-tuple-element.195, s32[]{:T(128)} %get-tuple-element.182), kind=kOutput, calls=%fused_computation.5.clone.1 | convolution fusion | flops 612360192 | bytes 19169792 | tf_op jit(solution)/shard_map/while/body/eval_jaxpr/qhe,khe->hqk/dot_general | solution.py:84
  765.8 11.1 %fusion.69 = f32[16,512,72]{1,2,0:T(8,128)} fusion(f32[16,512,72]{1,2,0:T(8,128)} %get-tuple-element.185, f32[16,512,512]{2,1,0:T(8,128)} %get-tuple-element.170, f32[16,512]{1,0:T(8,128)S(1)} %select_maximum_fusion.2, bf16[8,512,16,72]{1,3,2,0:T(8,128)(2,1)} %get-tuple-element.197, s32[]{:T(128)} %get-tuple-element.182, ...), kind=kOutput, calls=%fused_computation.13.clone.1 | convolution fusion | flops 618332160 | bytes 22741504 | tf_op jit(solution)/shard_map/while/body/eval_jaxpr/hqk,khe->hqe/dot_general | solution.py:91
  (83 shorter events, 142.8 us)
Async XLA Ops:
  6.5 772.4 %copy-start = (bf16[1152,1152]{1,0:T(8,128)(2,1)S(1)}, bf16[1152,1152]{1,0:T(8,128)(2,1)}, u32[]{:S(2)}) copy-start(bf16[1152,1152]{1,0:T(8,128)(2,1)} %param.19) | copy-start | bytes 7962628
  6.5 30.0 %copy-start.1 = (bf16[128,1152]{1,0:T(8,128)(2,1)S(1)}, bf16[128,1152]{1,0:T(8,128)(2,1)}, u32[]{:S(2)}) copy-start(bf16[128,1152]{1,0:T(8,128)(2,1)} %param.15) | copy-start | bytes 884740
  44.1 38.8 %all-to-all-start.1 = ((bf16[128,6,1152]{2,1,0:T(8,128)(2,1)}), bf16[128,6,1152]{2,1,0:T(8,128)(2,1)}, u32[]{:S(2)}, u32[]{:S(2)}) async-start(bf16[128,6,1152]{2,1,0:T(8,128)(2,1)} %reshape.223), calls=%async_computation.1 | async-start | bytes 4718592 | tf_op jit(solution)/shard_map/all_to_all | solution.py:51
  49.8 247.0 %all-gather.3.cloned.1.call-start = ((), (), s32[]{:S(2)}) async-start(), calls=%async_computation.2 | async-start | bytes 10616832 | tf_op jit(solution)/shard_map/all_gather | solution.py:73
  86.7 5.4 copy-start.4
  92.2 8.0 %copy-start.2 = (bf16[1,512,1152]{2,1,0:T(8,128)(2,1)S(1)}, bf16[1,512,1152]{2,1,0:T(8,128)(2,1)}, u32[]{:S(2)}) copy-start(bf16[1,512,1152]{2,1,0:T(8,128)(2,1)} %param.11) | copy-start | bytes 3538948
  100.2 11.5 %copy-start.5 = (f32[512,3456]{1,0:T(8,128)}, f32[512,3456]{1,0:T(8,128)S(1)}, u32[]{:S(2)}) copy-start(f32[512,3456]{1,0:T(8,128)S(1)} %fusion.19) | copy-start | bytes 21233668
  113.6 373.9 %all-gather.5.cloned.1.call-start = ((), (), s32[]{:S(2)}) async-start(), calls=%async_computation.3 | async-start | bytes 10616832 | tf_op jit(solution)/shard_map/all_gather | solution.py:74
  776.9 2.1 copy-start.3
Sparse Core Ops, SparseCore 0:
  113.7 183.0 all-gather.2
  298.4 189.0 all-gather.4
where the time goes:
time: 794 us; the launch traced here: 790 us
  waiting for transfers between devices  346 us (44%)
  matrix products  190 us (24%)
  local copies, waits for them, and re-layouts  137 us (17%)
  other arithmetic  76 us (10%)
  blocking collectives  20.5 us (3%)
  between operations  14.2 us (2%)
    all_gather x1, waiting for transfers between devices, per_device(): keys_piece = lax.all_gather(keys_here, 'ctx', axis=0, tiled=True)  180 us
    all_gather x1, waiting for transfers between devices, per_device(): values_piece = lax.all_gather(values_here, 'ctx', axis=0, tiled=True)  136 us
    dot_general x8, matrix products, advance(): jnp.einsum('hqk,khe->hqe', expo.astype(jnp.bfloat16), value_block, prefer...  88 us
    dot_general x8, matrix products, advance(): jnp.einsum('qhe,khe->hqk', query_heads, key_block, preferred_element_type...  77.9 us
    reduce_sum x8, other arithmetic, advance(): denominator = denominator * shrink + jnp.sum(expo, axis=2)  68.4 us
    unnamed x14, local copies, waits for them, and re-layouts  43 us
    reshape x1, local copies, waits for them, and re-layouts, per_device(): values_piece.reshape(piece_rows // block_rows, block_rows, HEADS, head_dim)  33.2 us
    reshape x1, local copies, waits for them, and re-layouts, per_device(): keys_piece.reshape(piece_rows // block_rows, block_rows, HEADS, head_dim)  33.2 us
  transfers between devices with their start and end apart: 3, of which 3 were waited for; matrix products, arithmetic and copies ran while one was open for 8% of the time, Pallas kernels for 0%

commit v1 on v0

v1 whole, which is shorter than its diff:
```python
import functools
import math

import jax
import jax.numpy as jnp
from jax import lax
from jax.experimental import pallas as pl
from jax.experimental.pallas import tpu as pltpu
from jax.sharding import PartitionSpec as P

HEADS = 16


def layer_modulate(device_tokens, mods, width):
    values = device_tokens.astype(jnp.float32)
    center = jnp.mean(values, axis=1, keepdims=True)
    spread = jnp.mean((values - center) ** 2, axis=1, keepdims=True)
    normed = (values - center) * lax.rsqrt(spread + 1e-06)
    shift = mods[:, :width]
    scale = mods[:, width : 2 * width]
    return (normed * (1.0 + scale) + shift).astype(jnp.bfloat16)


def attend_kernel(qt_ref, k_ref, vt_ref, o_ref, s_scr, *, inv_root, chunks):
    qt = qt_ref[0, 0]
    q_rows = qt.shape[1]

    def score(c, m):
        s = jnp.dot(k_ref[c, 0], qt, preferred_element_type=jnp.float32) * inv_root
        s_scr[c] = s
        return jnp.maximum(m, jnp.max(s, axis=0, keepdims=True))

    m = lax.fori_loop(0, chunks, score, jnp.full((1, q_rows), -jnp.inf, jnp.float32))

    def accumulate(c, carry):
        total, acc = carry
        expo = jnp.exp(s_scr[c] - m)
        total = total + jnp.sum(expo, axis=0, keepdims=True)
        acc = acc + jnp.dot(
            vt_ref[c, 0], expo.astype(jnp.bfloat16), preferred_element_type=jnp.float32
        )
        return total, acc

    head_dim = qt.shape[0]
    total, acc = lax.fori_loop(
        0,
        chunks,
        accumulate,
        (
            jnp.zeros((1, q_rows), jnp.float32),
            jnp.zeros((head_dim, q_rows), jnp.float32),
        ),
    )
    o_ref[0, 0] = (acc / total).astype(o_ref.dtype)


def attend(q_t, k_tok, v_t, inv_root):
    blocks, pair, head_dim, rows = q_t.shape
    kernel = functools.partial(attend_kernel, inv_root=inv_root, chunks=blocks)
    return pl.pallas_call(
        kernel,
        out_shape=jax.ShapeDtypeStruct(q_t.shape, jnp.bfloat16),
        grid=(pair, blocks),
        in_specs=[
            pl.BlockSpec((1, 1, head_dim, rows), lambda h, b: (b, h, 0, 0)),
            pl.BlockSpec((blocks, 1, rows, head_dim), lambda h, b: (0, h, 0, 0)),
            pl.BlockSpec((blocks, 1, head_dim, rows), lambda h, b: (0, h, 0, 0)),
        ],
        out_specs=pl.BlockSpec((1, 1, head_dim, rows), lambda h, b: (b, h, 0, 0)),
        scratch_shapes=[pltpu.VMEM((blocks, rows, rows), jnp.float32)],
        compiler_params=pltpu.CompilerParams(vmem_limit_bytes=48 * 1024 * 1024),
    )(q_t, k_tok, v_t)


def per_device(
    tokens, element_ids, element_slot, live_count, cond_table, w_ada, b_ada, w_qkv, w_out
):
    device_tokens = tokens[0]
    tok_rows, width = device_tokens.shape
    owners = lax.axis_size(("region", "ctx"))
    shards = lax.axis_size("ctx")
    elem_rows = cond_table.shape[0]
    capacity = max(2, 3 * tok_rows // (2 * owners))
    slots = element_slot[element_ids[0]]
    owner_index = slots // elem_rows
    local_row = slots % elem_rows
    position = jnp.arange(tok_rows, dtype=jnp.int32)
    solid = position < live_count[0, 0]
    earlier = (
        (owner_index[:, None] == owner_index[None, :])
        & (position[None, :] < position[:, None])
        & solid[None, :]
    )
    place_rank = jnp.sum(earlier.astype(jnp.int32), axis=1)
    target = jnp.where(solid, owner_index * capacity + place_rank, owners * capacity)
    requests = jnp.zeros((owners * capacity,), jnp.int32).at[target].set(local_row, mode="drop")
    asked = lax.all_to_all(
        requests.reshape(owners, capacity),
        ("region", "ctx"),
        split_axis=0,
        concat_axis=0,
        tiled=True,
    ).reshape(-1)
    pick_at = jnp.minimum(target, owners * capacity - 1)
    served = cond_table[asked].reshape(owners, capacity, width)
    replies = lax.all_to_all(served, ("region", "ctx"), split_axis=0, concat_axis=0, tiled=True)
    picked = replies.reshape(owners * capacity, width)[pick_at]
    activated = jnp.where(solid[:, None], jax.nn.silu(picked.astype(jnp.float32)), 0.0).astype(
        jnp.bfloat16
    )
    mods = (jnp.dot(activated, w_ada, preferred_element_type=jnp.float32) + b_ada).astype(
        jnp.bfloat16
    )
    mods = mods.astype(jnp.float32)
    modulated = layer_modulate(device_tokens, mods, width)

    head_dim = width // HEADS
    pair = HEADS // shards
    inverse_root = 1.0 / math.sqrt(head_dim)
    w_parts = w_qkv.reshape(width, 3, shards, pair, head_dim)
    q_send = jnp.einsum(
        "td,dphe->phet", modulated, w_parts[:, 0], preferred_element_type=jnp.float32
    ).astype(jnp.bfloat16)
    k_send = jnp.einsum(
        "td,dphe->phte", modulated, w_parts[:, 1], preferred_element_type=jnp.float32
    ).astype(jnp.bfloat16)
    v_send = jnp.einsum(
        "td,dphe->phet", modulated, w_parts[:, 2], preferred_element_type=jnp.float32
    ).astype(jnp.bfloat16)
    q_got = lax.all_to_all(q_send, "ctx", split_axis=0, concat_axis=0, tiled=True)
    k_got = lax.all_to_all(k_send, "ctx", split_axis=0, concat_axis=0, tiled=True)
    v_got = lax.all_to_all(v_send, "ctx", split_axis=0, concat_axis=0, tiled=True)
    out_t = attend(q_got, k_got, v_got, inverse_root)
    back = lax.all_to_all(out_t, "ctx", split_axis=0, concat_axis=0, tiled=True)
    projected = jnp.einsum(
        "phet,pheD->tD",
        back,
        w_out.reshape(shards, pair, head_dim, width),
        preferred_element_type=jnp.float32,
    )
    gate = mods[:, 2 * width :]
    output = (device_tokens.astype(jnp.float32) + gate * projected).astype(jnp.bfloat16)
    return output[None]


def solution(mesh):
    placed = (
        P("region", "ctx", None),
        P("region", "ctx"),
        P(),
        P("region", "ctx"),
        P(("region", "ctx"), None),
        P(),
        P(),
        P(),
        P(),
    )
    return jax.shard_map(
        per_device, mesh=mesh, in_specs=placed, out_specs=P("region", "ctx", None), check_vma=False
    )
```

time: 794 us -> 266 us (0.34)
  waiting for transfers between devices: 346 us -> 46.4 us
  matrix products: 190 us -> 22.1 us
  local copies, waits for them, and re-layouts: 137 us -> 49.1 us
  Pallas kernels: 0 us -> 77.6 us
  other arithmetic: 76 us -> 9.38 us
  blocking collectives: 20.5 us -> 38.1 us
  between operations: 14.2 us -> 1.02 us
  starting transfers between devices: 6.2 us -> 18.7 us
    all_gather x2 -> x0, waiting for transfers between devices: 316 us -> none  [the longest x1 180 us: per_device(): keys_piece = lax.all_gather(keys_here, 'ctx', axis=0, tiled=True)]
    dot_general x18 -> x1, matrix products: 182 us -> 4.65 us  [per_device(): jnp.einsum('phet,pheD->tD', back, w_out.reshape(shards, pair, head_dim, w...]
    pallas_call x0 -> x1, Pallas kernels: none -> 77.6 us  [attend(): pl.pallas_call(kernel, out_shape=jax.ShapeDtypeStruct(q_t.shape, jnp.bflo...]
    reduce_sum x8 -> x0, other arithmetic: 68.4 us -> none  [advance(): denominator = denominator * shrink + jnp.sum(expo, axis=2)]
    reshape x2 -> x0, local copies, waits for them, and re-layouts: 66.4 us -> none  [the longest x1 33.2 us: per_device(): values_piece.reshape(piece_rows // block_rows, block_rows, HEADS, head_dim)]
    all_to_all x0 -> x3, waiting for transfers between devices: none -> 33.9 us  [the longest x1 11.7 us: per_device(): lax.all_to_all(k_send, 'ctx', split_axis=0, concat_axis=0, tiled=True)]
    unnamed x14 -> x19, local copies, waits for them, and re-layouts: 43 us -> 16.2 us
    all_to_all x0 -> x1, blocking collectives: none -> 17.7 us  [per_device(): back = lax.all_to_all(out_t, 'ctx', split_axis=0, concat_axis=0, tiled=True)]
  transfers between devices with their start and end apart: 3 -> 4, of which waited for: 3 -> 4; matrix products, arithmetic and copies ran while one was open for 8% -> 13% of each run, Pallas kernels for 0% -> 0%
where the time goes in v1:
time: 266 us; the launch traced here: 262 us
  Pallas kernels  77.6 us (29%)
  local copies, waits for them, and re-layouts  49.1 us (18%)
  waiting for transfers between devices  46.4 us (17%)
  blocking collectives  38.1 us (14%)
  matrix products  22.1 us (8%)
  starting transfers between devices  18.7 us (7%)
  other arithmetic  9.38 us (4%)
    pallas_call x1, Pallas kernels, attend(): pl.pallas_call(kernel, out_shape=jax.ShapeDtypeStruct(q_t.shape, jnp.bflo...  77.6 us
    all_to_all x1, blocking collectives, per_device(): lax.all_to_all(requests.reshape(owners, capacity), ('region', 'ctx'), spl...  20.5 us
    all_to_all x1, blocking collectives, per_device(): back = lax.all_to_all(out_t, 'ctx', split_axis=0, concat_axis=0, tiled=True)  17.7 us
    unnamed x19, local copies, waits for them, and re-layouts  16.2 us
    all_to_all x1, waiting for transfers between devices, per_device(): lax.all_to_all(served, ('region', 'ctx'), split_axis=0, concat_axis=0, ti...  12.5 us
    all_to_all x1, waiting for transfers between devices, per_device(): lax.all_to_all(k_send, 'ctx', split_axis=0, concat_axis=0, tiled=True)  11.7 us
    all_to_all x1, waiting for transfers between devices, per_device(): lax.all_to_all(v_send, 'ctx', split_axis=0, concat_axis=0, tiled=True)  11.4 us
    all_to_all x1, waiting for transfers between devices, per_device(): lax.all_to_all(q_send, 'ctx', split_axis=0, concat_axis=0, tiled=True)  10.8 us
  transfers between devices with their start and end apart: 4, of which 4 were waited for; matrix products, arithmetic and copies ran while one was open for 13% of the time, Pallas kernels for 0%

profile of v1, /device:TPU:0, one launch (start us, length us, event | category | flops | bytes accessed | tf_op | source)
XLA Modules:
  0.0 262.4 jit_solution(1252843296321075432)
XLA Ops:
  1.6 3.5 %gather_fusion = s32[512]{0:T(512)S(1)} fusion(s32[16384]{0:T(1024)} %param.11, s32[1024]{0:T(1024)S(1)} %pad_clamp_fusion.2), kind=kCustom, calls=%fused_computation | custom fusion | bytes 6144 | tf_op jit(solution)/shard_map/gather | solution.py:84
  8.0 20.5 %all_to_all.34 = s32[128,1,6]{2,1,0:T(1,128)S(1)} all-to-all(s32[128,1,6]{2,1,0:T(1,128)S(1)} %bitcast.81), channel_id=1, replica_groups=mesh['region'=16,'ctx'=8] {'region','ctx'}, dimensions={0} | all-to-all | bytes 6144 | tf_op jit(solution)/shard_map/all_to_all | solution.py:97
  30.0 3.7 %gather_fusion.1 = bf16[768,1152]{1,0:T(8,128)(2,1)} fusion(bf16[128,1152]{1,0:T(8,128)(2,1)S(1)} %copy-done.2, s32[1024]{0:T(1024)S(1)} %pad_clamp_fusion.1), kind=kCustom, calls=%fused_computation.1 | custom fusion | bytes 3542016 | tf_op jit(solution)/shard_map/gather | solution.py:105
  33.7 3.9 %reshape.215 = bf16[128,6,1152]{2,1,0:T(8,128)(2,1)} reshape(bf16[768,1152]{1,0:T(8,128)(2,1)} %gather_fusion.1) | data formatting | bytes 3538944 | tf_op jit(solution)/shard_map/reshape | solution.py:105
  37.6 5.9 %all-to-all-start.1 = ((bf16[128,6,1152]{2,1,0:T(8,128)(2,1)}), bf16[128,6,1152]{2,1,0:T(8,128)(2,1)}, u32[]{:S(2)}, u32[]{:S(2)}) async-start(bf16[128,6,1152]{2,1,0:T(8,128)(2,1)} %reshape.215), calls=%async_computation.1 | async-start | bytes 4718592 | tf_op jit(solution)/shard_map/all_to_all | solution.py:106
  43.5 11.5 %copy.21 = bf16[1152,3456]{0,1:T(8,128)(2,1)} copy(bf16[1152,3456]{1,0:T(8,128)(2,1)} %param.16) | data formatting | bytes 15925248 | tf_op args[7]
  58.2 5.7 %fusion.31 = (bf16[1152,1,8,2,72]{0,4,3,2,1:T(8,128)(2,1)}, bf16[1152,1,8,2,72]{0,4,3,2,1:T(8,128)(2,1)}, bf16[1152,1,8,2,72]{0,4,3,2,1:T(8,128)(2,1)}) fusion(bf16[1152,3,8,2,72]{0,4,3,2,1:T(8,128)(2,1)} %bitcast.74), kind=kLoop, calls=%fused_computation.68 | loop fusion | bytes 15925248 | tf_op jit(solution)/shard_map/slice | solution.py:128
  63.9 12.5 %all-to-all-done.1 = bf16[128,6,1152]{2,1,0:T(8,128)(2,1)} async-done(((bf16[128,6,1152]{2,1,0:T(8,128)(2,1)}), bf16[128,6,1152]{2,1,0:T(8,128)(2,1)}, u32[]{:S(2)}, u32[]{:S(2)}) %all-to-all-start.1) | async-done | bytes 1769504 | tf_op jit(solution)/shard_map/all_to_all | solution.py:106
  76.4 3.9 %reshape.216 = bf16[768,1152]{1,0:T(8,128)(2,1)} reshape(bf16[128,6,1152]{2,1,0:T(8,128)(2,1)} %all-to-all-done.1) | data formatting | bytes 3538944 | tf_op jit(solution)/shard_map/reshape | solution.py:107
  80.2 5.4 %gather_fusion.2 = bf16[512,1152]{1,0:T(8,128)(2,1)} fusion(bf16[768,1152]{1,0:T(8,128)(2,1)} %reshape.216, s32[1024]{0:T(1024)S(1)} %pad_clamp_fusion), kind=kCustom, calls=%fused_computation.2 | custom fusion | bytes 2361344 | tf_op jit(solution)/shard_map/gather | solution.py:107
  85.7 8.0 %fusion = f32[512,3456]{1,0:T(8,128)S(1)} fusion(bf16[1152,3456]{1,0:T(8,128)(2,1)} %param.14, f32[3456]{0:T(1024)S(1)} %copy-done.8, bf16[512,1152]{1,0:T(8,128)(2,1)} %gather_fusion.2, pred[512]{0:T(512)(128)(4,1)S(1)} %iota_compare_fusion.1), kind=kOutput, calls=%fused_computation.5 | convolution fusion | flops 4086300672 | bytes 16234496 | tf_op jit(solution)/shard_map/dot_general | solution.py:111
  94.3 2.7 %copy-done.5 = f32[512,3456]{1,0:T(8,128)} copy-done((f32[512,3456]{1,0:T(8,128)}, f32[512,3456]{1,0:T(8,128)S(1)}, u32[]{:S(2)}) %copy-start.5) | copy-done | bytes 7077912
  100.4 4.3 %all-to-all-start.3 = ((bf16[8,2,512,72]{2,3,1,0:T(8,128)(2,1)}), bf16[8,2,512,72]{2,3,1,0:T(8,128)(2,1)}, u32[]{:S(2)}, u32[]{:S(2)}) async-start(bf16[8,2,512,72]{2,3,1,0:T(8,128)(2,1)} %convert_bitcast_fusion.2), calls=%async_computation.3 | async-start | bytes 2359296 | tf_op jit(solution)/shard_map/all_to_all | solution.py:131
  104.6 3.8 %fusion.32 = f32[512,1152]{0,1:S(1)} fusion(bf16[512,1152]{1,0:T(8,128)(2,1)} %copy-done.7, bf16[1152,1152]{0,1:T(8,128)(2,1)} %bitcast.76), kind=kOutput, calls=%fused_computation.69 | convolution fusion | flops 1358954496 | bytes 6193152
  109.7 11.7 %all-to-all-done.3 = bf16[8,2,512,72]{2,3,1,0:T(8,128)(2,1)} async-done(((bf16[8,2,512,72]{2,3,1,0:T(8,128)(2,1)}), bf16[8,2,512,72]{2,3,1,0:T(8,128)(2,1)}, u32[]{:S(2)}, u32[]{:S(2)}) %all-to-all-start.3) | async-done | bytes 1179680 | tf_op jit(solution)/shard_map/all_to_all | solution.py:131
  121.5 4.3 %all-to-all-start.2 = ((bf16[8,2,72,512]{3,2,1,0:T(8,128)(2,1)}), bf16[8,2,72,512]{3,2,1,0:T(8,128)(2,1)}, u32[]{:S(2)}, u32[]{:S(2)}) async-start(bf16[8,2,72,512]{3,2,1,0:T(8,128)(2,1)} %convert_bitcast_fusion.3), calls=%async_computation.2 | async-start | bytes 2359296 | tf_op jit(solution)/shard_map/all_to_all | solution.py:130
  125.7 3.8 %fusion.34 = f32[512,1152]{0,1:S(1)} fusion(bf16[512,1152]{1,0:T(8,128)(2,1)} %copy-done.7, bf16[1152,1152]{0,1:T(8,128)(2,1)} %bitcast.75), kind=kOutput, calls=%fused_computation.71 | convolution fusion | flops 1358954496 | bytes 6193152
  130.8 10.8 %all-to-all-done.2.qt_ref = bf16[8,2,72,512]{3,2,1,0:T(8,128)(2,1)} async-done(((bf16[8,2,72,512]{3,2,1,0:T(8,128)(2,1)}), bf16[8,2,72,512]{3,2,1,0:T(8,128)(2,1)}, u32[]{:S(2)}, u32[]{:S(2)}) %all-to-all-start.2) | async-done | bytes 1179680 | tf_op jit(solution)/shard_map/all_to_all | solution.py:130
  141.5 4.3 %all-to-all-start.4 = ((bf16[8,2,72,512]{3,2,1,0:T(8,128)(2,1)}), bf16[8,2,72,512]{3,2,1,0:T(8,128)(2,1)}, u32[]{:S(2)}, u32[]{:S(2)}) async-start(bf16[8,2,72,512]{3,2,1,0:T(8,128)(2,1)} %convert_bitcast_fusion.1), calls=%async_computation.4 | async-start | bytes 2359296 | tf_op jit(solution)/shard_map/all_to_all | solution.py:132
  145.8 3.6 %copy.22.k_ref = bf16[8,2,512,72]{3,2,1,0:T(8,128)(2,1)} copy(bf16[8,2,512,72]{2,3,1,0:T(8,128)(2,1)} %all-to-all-done.3) | data formatting | bytes 2359296 | tf_op jit(solution)/shard_map/all_to_all | solution.py:131
  149.4 11.4 %all-to-all-done.4.vt_ref = bf16[8,2,72,512]{3,2,1,0:T(8,128)(2,1)} async-done(((bf16[8,2,72,512]{3,2,1,0:T(8,128)(2,1)}), bf16[8,2,72,512]{3,2,1,0:T(8,128)(2,1)}, u32[]{:S(2)}, u32[]{:S(2)}) %all-to-all-start.4) | async-done | bytes 1179680 | tf_op jit(solution)/shard_map/all_to_all | solution.py:132
  162.4 77.6 %shard_map.91 = bf16[8,2,72,512]{3,2,1,0:T(8,128)(2,1)S(1)} custom-call(bf16[8,2,72,512]{3,2,1,0:T(8,128)(2,1)} %all-to-all-done.2.qt_ref, bf16[8,2,512,72]{3,2,1,0:T(8,128)(2,1)S(1)} %copy-done.1, bf16[8,2,72,512]{3,2,1,0:T(8,128)(2,1)} %all-to-all-done.4.vt_ref), custom_call_target="tpu_custom_call" | custom-call | tf_op jit(solution)/shard_map/pallas_call | solution.py:60
  240.0 17.7 %all_to_all.35 = bf16[8,2,72,512]{3,2,1,0:T(8,128)(2,1)S(1)} all-to-all(bf16[8,2,72,512]{3,2,1,0:T(8,128)(2,1)S(1)} %shard_map.91), channel_id=1, replica_groups=mesh['region'=16,'ctx'=8] {'ctx'}, dimensions={0} | all-to-all | bytes 2359296 | tf_op jit(solution)/shard_map/all_to_all | solution.py:134
  257.7 4.7 %fusion.7 = bf16[1,512,1152]{2,1,0:T(8,128)(2,1)} fusion(bf16[1,512,1152]{2,1,0:T(8,128)(2,1)S(1)} %copy-done.4, bf16[8,2,72,1152]{3,2,1,0:T(8,128)(2,1)S(1)} %bitcast.73, f32[512,3456]{1,0:T(8,128)} %copy-done.5, bf16[8,2,72,512]{3,2,1,0:T(8,128)(2,1)S(1)} %all_to_all.35), kind=kOutput, calls=%fused_computation.17 | convolution fusion | flops 1361313792 | bytes 8552448 | tf_op jit(solution)/shard_map/phet,pheD->tD/dot_general | solution.py:135
  (41 shorter events, 16.4 us)
Async XLA Ops:
  0.0 257.7 %copy-start = (bf16[1152,1152]{1,0:T(8,128)(2,1)S(1)}, bf16[1152,1152]{1,0:T(8,128)(2,1)}, u32[]{:S(2)}) copy-start(bf16[1152,1152]{1,0:T(8,128)(2,1)} %param.17) | copy-start | bytes 7962628
  0.0 30.0 %copy-start.2 = (bf16[128,1152]{1,0:T(8,128)(2,1)S(1)}, bf16[128,1152]{1,0:T(8,128)(2,1)}, u32[]{:S(2)}) copy-start(bf16[128,1152]{1,0:T(8,128)(2,1)} %param.13) | copy-start | bytes 884740
  37.6 38.8 %all-to-all-start.1 = ((bf16[128,6,1152]{2,1,0:T(8,128)(2,1)}), bf16[128,6,1152]{2,1,0:T(8,128)(2,1)}, u32[]{:S(2)}, u32[]{:S(2)}) async-start(bf16[128,6,1152]{2,1,0:T(8,128)(2,1)} %reshape.215), calls=%async_computation.1 | async-start | bytes 4718592 | tf_op jit(solution)/shard_map/all_to_all | solution.py:106
  80.2 5.4 %copy-start.8 = (f32[3456]{0:T(1024)S(1)}, f32[3456]{0:T(1024)}, u32[]{:S(2)}) copy-start(f32[3456]{0:T(1024)} %param.15) | copy-start | bytes 41476
  85.7 8.0 %copy-start.3 = (bf16[1,512,1152]{2,1,0:T(8,128)(2,1)S(1)}, bf16[1,512,1152]{2,1,0:T(8,128)(2,1)}, u32[]{:S(2)}) copy-start(bf16[1,512,1152]{2,1,0:T(8,128)(2,1)} %param.9) | copy-start | bytes 3538948
  93.7 3.3 %copy-start.5 = (f32[512,3456]{1,0:T(8,128)}, f32[512,3456]{1,0:T(8,128)S(1)}, u32[]{:S(2)}) copy-start(f32[512,3456]{1,0:T(8,128)S(1)} %fusion) | copy-start | bytes 21233668
  93.7 3.7 %copy-start.6 = (bf16[1152,1,8,2,72]{0,4,3,2,1:T(8,128)(2,1)S(1)}, bf16[1152,1,8,2,72]{0,4,3,2,1:T(8,128)(2,1)}, u32[]{:S(2)}) copy-start(bf16[1152,1,8,2,72]{0,4,3,2,1:T(8,128)(2,1)} %get-tuple-element.8) | copy-start | bytes 7962628
  97.0 2.2 copy-start.7
  100.4 21.1 %all-to-all-start.3 = ((bf16[8,2,512,72]{2,3,1,0:T(8,128)(2,1)}), bf16[8,2,512,72]{2,3,1,0:T(8,128)(2,1)}, u32[]{:S(2)}, u32[]{:S(2)}) async-start(bf16[8,2,512,72]{2,3,1,0:T(8,128)(2,1)} %convert_bitcast_fusion.2), calls=%async_computation.3 | async-start | bytes 2359296 | tf_op jit(solution)/shard_map/all_to_all | solution.py:131
  121.5 20.1 %all-to-all-start.2 = ((bf16[8,2,72,512]{3,2,1,0:T(8,128)(2,1)}), bf16[8,2,72,512]{3,2,1,0:T(8,128)(2,1)}, u32[]{:S(2)}, u32[]{:S(2)}) async-start(bf16[8,2,72,512]{3,2,1,0:T(8,128)(2,1)} %convert_bitcast_fusion.3), calls=%async_computation.2 | async-start | bytes 2359296 | tf_op jit(solution)/shard_map/all_to_all | solution.py:130
  141.5 19.3 %all-to-all-start.4 = ((bf16[8,2,72,512]{3,2,1,0:T(8,128)(2,1)}), bf16[8,2,72,512]{3,2,1,0:T(8,128)(2,1)}, u32[]{:S(2)}, u32[]{:S(2)}) async-start(bf16[8,2,72,512]{3,2,1,0:T(8,128)(2,1)} %convert_bitcast_fusion.1), calls=%async_computation.4 | async-start | bytes 2359296 | tf_op jit(solution)/shard_map/all_to_all | solution.py:132
  160.8 1.6 copy-start.1
  240.0 17.7 %copy-start.4 = (bf16[1,512,1152]{2,1,0:T(8,128)(2,1)S(1)}, bf16[1,512,1152]{2,1,0:T(8,128)(2,1)}, u32[]{:S(2)}) copy-start(bf16[1,512,1152]{2,1,0:T(8,128)(2,1)} %param.9) | copy-start | bytes 3538948

commit v2 on v1

--- a/solution.py
+++ b/solution.py
@@ -70,6 +70,60 @@
         scratch_shapes=[pltpu.VMEM((blocks, rows, rows), jnp.float32)],
         compiler_params=pltpu.CompilerParams(vmem_limit_bytes=48 * 1024 * 1024),
     )(q_t, k_tok, v_t)
+
+
+def exchange_kernel(*refs, count, shards):
+    sends = refs[:count]
+    gots = refs[count : 2 * count]
+    send_sem, recv_sem, local_sem = refs[2 * count :]
+    me = lax.axis_index("ctx")
+    region = lax.axis_index("region")
+    mesh_id = pl.DeviceIdType.MESH
+    barrier = pltpu.get_barrier_semaphore()
+    for d in range(1, shards):
+        peer = lax.rem(me + d, shards)
+        pl.semaphore_signal(barrier, 1, device_id=(region, peer), device_id_type=mesh_id)
+    pl.semaphore_wait(barrier, shards - 1)
+    copies = []
+    for a in range(count):
+        local = pltpu.make_async_copy(sends[a].at[me], gots[a].at[me], local_sem.at[a])
+        local.start()
+        copies.append(local)
+    for d in range(1, shards):
+        peer = lax.rem(me + d, shards)
+        for a in range(count):
+            remote = pltpu.make_async_remote_copy(
+                src_ref=sends[a].at[peer],
+                dst_ref=gots[a].at[me],
+                send_sem=send_sem.at[a, d - 1],
+                recv_sem=recv_sem.at[a, d - 1],
+                device_id=(region, peer),
+                device_id_type=mesh_id,
+            )
+            remote.start()
+            copies.append(remote)
+    for copy in copies:
+        copy.wait()
+
+
+def exchange(arrays, shards, collective_id):
+    count = len(arrays)
+    kernel = functools.partial(exchange_kernel, count=count, shards=shards)
+    any_spec = pl.BlockSpec(memory_space=pl.ANY)
+    return pl.pallas_call(
+        kernel,
+        out_shape=[jax.ShapeDtypeStruct(x.shape, x.dtype) for x in arrays],
+        in_specs=[any_spec] * count,
+        out_specs=[any_spec] * count,
+        scratch_shapes=[
+            pltpu.SemaphoreType.DMA((count, shards - 1)),
+            pltpu.SemaphoreType.DMA((count, shards - 1)),
+            pltpu.SemaphoreType.DMA((count,)),
+        ],
+        compiler_params=pltpu.CompilerParams(
+            collective_id=collective_id, has_side_effects=True
+        ),
+    )(*arrays)
 
 
 def per_device(
@@ -127,11 +181,9 @@
     v_send = jnp.einsum(
         "td,dphe->phet", modulated, w_parts[:, 2], preferred_element_type=jnp.float32
     ).astype(jnp.bfloat16)
-    q_got = lax.all_to_all(q_send, "ctx", split_axis=0, concat_axis=0, tiled=True)
-    k_got = lax.all_to_all(k_send, "ctx", split_axis=0, concat_axis=0, tiled=True)
-    v_got = lax.all_to_all(v_send, "ctx", split_axis=0, concat_axis=0, tiled=True)
+    q_got, k_got, v_got = exchange([q_send, k_send, v_send], shards, 0)
     out_t = attend(q_got, k_got, v_got, inverse_root)
-    back = lax.all_to_all(out_t, "ctx", split_axis=0, concat_axis=0, tiled=True)
+    (back,) = exchange([out_t], shards, 1)
     projected = jnp.einsum(
         "phet,pheD->tD",
         back,

time: 266 us -> 271 us (1.019)
  Pallas kernels: 77.6 us -> 145 us
  waiting for transfers between devices: 46.4 us -> 12.4 us
  blocking collectives: 38.1 us -> 20.5 us
  starting transfers between devices: 18.7 us -> 5.9 us
  local copies, waits for them, and re-layouts: 49.1 us -> 52.6 us
    pallas_call x0 -> x2, Pallas kernels: none -> 68.3 us  [exchange(): pl.pallas_call(kernel, out_shape=[jax.ShapeDtypeStruct(x.shape, x.dtype)...]
    all_to_all x3 -> x0, waiting for transfers between devices: 33.9 us -> none  [the longest x1 11.7 us: per_device(): lax.all_to_all(k_send, 'ctx', split_axis=0, concat_axis=0, tiled=True)]
    all_to_all x1 -> x0, blocking collectives: 17.7 us -> none  [per_device(): back = lax.all_to_all(out_t, 'ctx', split_axis=0, concat_axis=0, tiled=True)]
    all_to_all x3 -> x0, starting transfers between devices: 12.8 us -> none  [the longest x1 4.27 us: per_device(): lax.all_to_all(v_send, 'ctx', split_axis=0, concat_axis=0, tiled=True)]
    all_to_all x1 -> x0, local copies, waits for them, and re-layouts: 3.61 us -> none  [per_device(): lax.all_to_all(k_send, 'ctx', split_axis=0, concat_axis=0, tiled=True)]
    unnamed x19 -> x25, local copies, waits for them, and re-layouts: 16.2 us -> 19.8 us
    convert_element_type x0 -> x1, local copies, waits for them, and re-layouts: none -> 3.56 us  [per_device(): k_send = jnp.einsum('td,dphe->phte', modulated, w_parts[:, 1], preferred_...]
    convert_element_type x1, other arithmetic: 1.2 us -> 4.17 us  [per_device(): v_send = jnp.einsum('td,dphe->phet', modulated, w_parts[:, 2], preferred_...]
  transfers between devices with their start and end apart: 4 -> 1, of which waited for: 4 -> 1; matrix products, arithmetic and copies ran while one was open for 13% -> 8% of each run, Pallas kernels for 0% -> 0%
where the time goes in v2:
time: 271 us; the launch traced here: 270 us
  Pallas kernels  145 us (54%)
  local copies, waits for them, and re-layouts  52.6 us (19%)
  matrix products  21.4 us (8%)
  blocking collectives  20.5 us (8%)
  waiting for transfers between devices  12.4 us (5%)
  other arithmetic  11.1 us (4%)
  starting transfers between devices  5.9 us (2%)
    pallas_call x1, Pallas kernels, attend(): pl.pallas_call(kernel, out_shape=jax.ShapeDtypeStruct(q_t.shape, jnp.bflo...  76.8 us
    pallas_call x2, Pallas kernels, exchange(): pl.pallas_call(kernel, out_shape=[jax.ShapeDtypeStruct(x.shape, x.dtype)...  68.3 us
    all_to_all x1, blocking collectives, per_device(): lax.all_to_all(requests.reshape(owners, capacity), ('region', 'ctx'), spl...  20.5 us
    unnamed x25, local copies, waits for them, and re-layouts  19.8 us
    all_to_all x1, waiting for transfers between devices, per_device(): lax.all_to_all(served, ('region', 'ctx'), split_axis=0, concat_axis=0, ti...  12.4 us
    unnamed x3, matrix products  8.06 us
    dot_general x1, matrix products, per_device(): jnp.dot(activated, w_ada, preferred_element_type=jnp.float32) + b_ada  8.01 us
    all_to_all x1, starting transfers between devices, per_device(): lax.all_to_all(served, ('region', 'ctx'), split_axis=0, concat_axis=0, ti...  5.9 us
  transfers between devices with their start and end apart: 1, of which 1 were waited for; matrix products, arithmetic and copies ran while one was open for 8% of the time, Pallas kernels for 0%

profile of v2, /device:TPU:0, one launch (start us, length us, event | category | flops | bytes accessed | tf_op | source)
XLA Modules:
  0.0 270.1 jit_solution(2116050410654259105)
XLA Ops:
  1.6 3.5 %gather_fusion = s32[512]{0:T(512)S(1)} fusion(s32[16384]{0:T(1024)} %param.11, s32[1024]{0:T(1024)S(1)} %pad_clamp_fusion.2), kind=kCustom, calls=%fused_computation | custom fusion | bytes 6144 | tf_op jit(solution)/shard_map/gather | solution.py:138
  5.4 2.4 scatter_custom_fusion
  8.0 20.5 %all_to_all.14 = s32[128,1,6]{2,1,0:T(1,128)S(1)} all-to-all(s32[128,1,6]{2,1,0:T(1,128)S(1)} %bitcast.81), channel_id=1, replica_groups=mesh['region'=16,'ctx'=8] {'region','ctx'}, dimensions={0} | all-to-all | bytes 6144 | tf_op jit(solution)/shard_map/all_to_all | solution.py:151
  30.0 3.7 %gather_fusion.1 = bf16[768,1152]{1,0:T(8,128)(2,1)} fusion(bf16[128,1152]{1,0:T(8,128)(2,1)S(1)} %copy-done.5, s32[1024]{0:T(1024)S(1)} %pad_clamp_fusion.1), kind=kCustom, calls=%fused_computation.1 | custom fusion | bytes 3542016 | tf_op jit(solution)/shard_map/gather | solution.py:159
  33.7 3.9 %reshape.215 = bf16[128,6,1152]{2,1,0:T(8,128)(2,1)} reshape(bf16[768,1152]{1,0:T(8,128)(2,1)} %gather_fusion.1) | data formatting | bytes 3538944 | tf_op jit(solution)/shard_map/reshape | solution.py:159
  37.6 5.9 %all-to-all-start.1 = ((bf16[128,6,1152]{2,1,0:T(8,128)(2,1)}), bf16[128,6,1152]{2,1,0:T(8,128)(2,1)}, u32[]{:S(2)}, u32[]{:S(2)}) async-start(bf16[128,6,1152]{2,1,0:T(8,128)(2,1)} %reshape.215), calls=%async_computation.1 | async-start | bytes 4718592 | tf_op jit(solution)/shard_map/all_to_all | solution.py:160
  43.5 11.5 %copy.29 = bf16[1152,3456]{0,1:T(8,128)(2,1)} copy(bf16[1152,3456]{1,0:T(8,128)(2,1)} %param.16) | data formatting | bytes 15925248 | tf_op args[7]
  56.5 1.7 fusion.9
  58.3 5.7 %fusion.31 = (bf16[1152,1,8,2,72]{0,4,3,2,1:T(8,128)(2,1)}, bf16[1152,1,8,2,72]{0,4,3,2,1:T(8,128)(2,1)}, bf16[1152,1,8,2,72]{0,4,3,2,1:T(8,128)(2,1)}) fusion(bf16[1152,3,8,2,72]{0,4,3,2,1:T(8,128)(2,1)} %bitcast.73), kind=kLoop, calls=%fused_computation.67 | loop fusion | bytes 15925248 | tf_op jit(solution)/shard_map/slice | solution.py:182
  63.9 12.4 %all-to-all-done.1 = bf16[128,6,1152]{2,1,0:T(8,128)(2,1)} async-done(((bf16[128,6,1152]{2,1,0:T(8,128)(2,1)}), bf16[128,6,1152]{2,1,0:T(8,128)(2,1)}, u32[]{:S(2)}, u32[]{:S(2)}) %all-to-all-start.1) | async-done | bytes 1769504 | tf_op jit(solution)/shard_map/all_to_all | solution.py:160
  76.4 3.9 %reshape.216 = bf16[768,1152]{1,0:T(8,128)(2,1)} reshape(bf16[128,6,1152]{2,1,0:T(8,128)(2,1)} %all-to-all-done.1) | data formatting | bytes 3538944 | tf_op jit(solution)/shard_map/reshape | solution.py:161
  80.3 5.4 %gather_fusion.2 = bf16[512,1152]{1,0:T(8,128)(2,1)} fusion(bf16[768,1152]{1,0:T(8,128)(2,1)} %reshape.216, s32[1024]{0:T(1024)S(1)} %pad_clamp_fusion), kind=kCustom, calls=%fused_computation.2 | custom fusion | bytes 2361344 | tf_op jit(solution)/shard_map/gather | solution.py:161
  85.7 8.0 %fusion = f32[512,3456]{1,0:T(8,128)S(1)} fusion(bf16[1152,3456]{1,0:T(8,128)(2,1)} %param.14, f32[3456]{0:T(1024)S(1)} %copy-done.11, bf16[512,1152]{1,0:T(8,128)(2,1)} %gather_fusion.2, pred[512]{0:T(512)(128)(4,1)S(1)} %iota_compare_fusion.1), kind=kOutput, calls=%fused_computation.5 | convolution fusion | flops 4086300672 | bytes 16234496 | tf_op jit(solution)/shard_map/dot_general | solution.py:165
  94.4 2.7 copy-done.7
  97.4 3.1 %fusion.34 = f32[512,1152]{0,1} fusion(bf16[512,1152]{1,0:T(8,128)(2,1)S(1)} %fusion.12, bf16[1152,1152]{0,1:T(8,128)(2,1)S(1)} %bitcast.77), kind=kOutput, calls=%fused_computation.70 | convolution fusion | flops 1358954496 | bytes 6193152
  100.6 1.7 fusion.33
  102.3 3.2 %fusion.32 = f32[512,1152]{0,1} fusion(bf16[512,1152]{1,0:T(8,128)(2,1)S(1)} %fusion.12, bf16[1152,1152]{0,1:T(8,128)(2,1)S(1)} %bitcast.75), kind=kOutput, calls=%fused_computation.68 | convolution fusion | flops 1358954496 | bytes 6193152
  106.7 3.6 %copy.30 = bf16[512,8,2,72]{3,0,2,1:T(8,128)(2,1)} copy(bf16[512,8,2,72]{0,3,2,1:T(8,128)(2,1)} %convert_element_type.53) | data formatting | bytes 2359296 | tf_op jit(solution)/shard_map/convert_element_type | solution.py:180
  110.3 4.2 %convert_bitcast_fusion.1 = (bf16[8,2,72,512]{3,2,1,0:T(8,128)(2,1)}, bf16[8,2,72,512]{3,2,1,0:T(8,128)(2,1)}) fusion(f32[512,8,2,72]{0,3,2,1:T(8,128)} %bitcast.78, f32[512,8,2,72]{0,3,2,1:T(8,128)} %bitcast.79), kind=kLoop, calls=%fused_computation.30 | loop fusion | flops 1179648 | bytes 7077888 | tf_op jit(solution)/shard_map/convert_element_type | solution.py:183
  114.5 51.9 %shard_map.91 = (bf16[8,2,72,512]{3,2,1,0:T(8,128)(2,1)}, bf16[8,2,512,72]{3,2,1,0:T(8,128)(2,1)}, bf16[8,2,72,512]{3,2,1,0:T(8,128)(2,1)}) custom-call(bf16[8,2,72,512]{3,2,1,0:T(8,128)(2,1)} %get-tuple-element.19.refs_0_, bf16[8,2,512,72]{3,2,1,0:T(8,128)(2,1)} %bitcast.74, bf16[8,2,72,512]{3,2,1,0:T(8,128)(2,1)} %get-tuple-element.18.refs_2_), custom_call_target="tpu_custom_call" | custom-call | tf_op jit(solution)/shard_map/pallas_call | solution.py:113
  166.3 1.6 copy-done.2
  170.5 76.8 %shard_map.92.refs_0_ = bf16[8,2,72,512]{3,2,1,0:T(8,128)(2,1)S(1)} custom-call(bf16[8,2,72,512]{3,2,1,0:T(8,128)(2,1)S(1)} %copy-done.3, bf16[8,2,512,72]{3,2,1,0:T(8,128)(2,1)S(1)} %copy-done.2, bf16[8,2,72,512]{3,2,1,0:T(8,128)(2,1)S(1)} %copy-done.4), custom_call_target="tpu_custom_call" | custom-call | tf_op jit(solution)/shard_map/pallas_call | solution.py:60
  248.3 16.4 %shard_map.93 = bf16[8,2,72,512]{3,2,1,0:T(8,128)(2,1)} custom-call(bf16[8,2,72,512]{3,2,1,0:T(8,128)(2,1)} %copy-done.1), custom_call_target="tpu_custom_call" | custom-call | tf_op jit(solution)/shard_map/pallas_call | solution.py:113
  264.8 5.3 %fusion.7 = bf16[1,512,1152]{2,1,0:T(8,128)(2,1)} fusion(bf16[1,512,1152]{2,1,0:T(8,128)(2,1)} %param.9, bf16[8,2,72,1152]{3,2,1,0:T(8,128)(2,1)S(1)} %bitcast.72, f32[512,3456]{1,0:T(8,128)} %copy-done.7, bf16[8,2,72,512]{3,2,1,0:T(8,128)(2,1)} %shard_map.93), kind=kOutput, calls=%fused_computation.17 | convolution fusion | flops 1361313792 | bytes 8552448 | tf_op jit(solution)/shard_map/phet,pheD->tD/dot_general | solution.py:187
  (41 shorter events, 10.0 us)
Async XLA Ops:
  0.0 264.8 %copy-start = (bf16[1152,1152]{1,0:T(8,128)(2,1)S(1)}, bf16[1152,1152]{1,0:T(8,128)(2,1)}, u32[]{:S(2)}) copy-start(bf16[1152,1152]{1,0:T(8,128)(2,1)} %param.17) | copy-start | bytes 7962628
  0.0 30.0 %copy-start.5 = (bf16[128,1152]{1,0:T(8,128)(2,1)S(1)}, bf16[128,1152]{1,0:T(8,128)(2,1)}, u32[]{:S(2)}) copy-start(bf16[128,1152]{1,0:T(8,128)(2,1)} %param.13) | copy-start | bytes 884740
  37.6 38.8 %all-to-all-start.1 = ((bf16[128,6,1152]{2,1,0:T(8,128)(2,1)}), bf16[128,6,1152]{2,1,0:T(8,128)(2,1)}, u32[]{:S(2)}, u32[]{:S(2)}) async-start(bf16[128,6,1152]{2,1,0:T(8,128)(2,1)} %reshape.215), calls=%async_computation.1 | async-start | bytes 4718592 | tf_op jit(solution)/shard_map/all_to_all | solution.py:160
  80.3 5.4 %copy-start.11 = (f32[3456]{0:T(1024)S(1)}, f32[3456]{0:T(1024)}, u32[]{:S(2)}) copy-start(f32[3456]{0:T(1024)} %param.15) | copy-start | bytes 41476
  85.7 8.0 %copy-start.6 = (bf16[1,512,1152]{2,1,0:T(8,128)(2,1)S(1)}, bf16[1,512,1152]{2,1,0:T(8,128)(2,1)}, u32[]{:S(2)}) copy-start(bf16[1,512,1152]{2,1,0:T(8,128)(2,1)} %param.9) | copy-start | bytes 3538948
  93.7 3.3 %copy-start.7 = (f32[512,3456]{1,0:T(8,128)}, f32[512,3456]{1,0:T(8,128)S(1)}, u32[]{:S(2)}) copy-start(f32[512,3456]{1,0:T(8,128)S(1)} %fusion) | copy-start | bytes 21233668
  93.7 3.7 %copy-start.10 = (bf16[1152,1,8,2,72]{0,4,3,2,1:T(8,128)(2,1)S(1)}, bf16[1152,1,8,2,72]{0,4,3,2,1:T(8,128)(2,1)}, u32[]{:S(2)}) copy-start(bf16[1152,1,8,2,72]{0,4,3,2,1:T(8,128)(2,1)} %get-tuple-element.13) | copy-start | bytes 7962628
  97.4 3.1 %copy-start.9 = (bf16[1152,1,8,2,72]{0,4,3,2,1:T(8,128)(2,1)S(1)}, bf16[1152,1,8,2,72]{0,4,3,2,1:T(8,128)(2,1)}, u32[]{:S(2)}) copy-start(bf16[1152,1,8,2,72]{0,4,3,2,1:T(8,128)(2,1)} %get-tuple-element.14) | copy-start | bytes 7962628
  100.6 1.8 copy-start.8
  166.3 1.6 copy-start.2
  167.9 1.3 copy-start.3
  169.2 1.3 copy-start.4
  247.3 1.0 copy-start.1

commit v3 on v2

--- a/solution.py
+++ b/solution.py
@@ -21,61 +21,7 @@
     return (normed * (1.0 + scale) + shift).astype(jnp.bfloat16)
 
 
-def attend_kernel(qt_ref, k_ref, vt_ref, o_ref, s_scr, *, inv_root, chunks):
-    qt = qt_ref[0, 0]
-    q_rows = qt.shape[1]
-
-    def score(c, m):
-        s = jnp.dot(k_ref[c, 0], qt, preferred_element_type=jnp.float32) * inv_root
-        s_scr[c] = s
-        return jnp.maximum(m, jnp.max(s, axis=0, keepdims=True))
-
-    m = lax.fori_loop(0, chunks, score, jnp.full((1, q_rows), -jnp.inf, jnp.float32))
-
-    def accumulate(c, carry):
-        total, acc = carry
-        expo = jnp.exp(s_scr[c] - m)
-        total = total + jnp.sum(expo, axis=0, keepdims=True)
-        acc = acc + jnp.dot(
-            vt_ref[c, 0], expo.astype(jnp.bfloat16), preferred_element_type=jnp.float32
-        )
-        return total, acc
-
-    head_dim = qt.shape[0]
-    total, acc = lax.fori_loop(
-        0,
-        chunks,
-        accumulate,
-        (
-            jnp.zeros((1, q_rows), jnp.float32),
-            jnp.zeros((head_dim, q_rows), jnp.float32),
-        ),
-    )
-    o_ref[0, 0] = (acc / total).astype(o_ref.dtype)
-
-
-def attend(q_t, k_tok, v_t, inv_root):
-    blocks, pair, head_dim, rows = q_t.shape
-    kernel = functools.partial(attend_kernel, inv_root=inv_root, chunks=blocks)
-    return pl.pallas_call(
-        kernel,
-        out_shape=jax.ShapeDtypeStruct(q_t.shape, jnp.bfloat16),
-        grid=(pair, blocks),
-        in_specs=[
-            pl.BlockSpec((1, 1, head_dim, rows), lambda h, b: (b, h, 0, 0)),
-            pl.BlockSpec((blocks, 1, rows, head_dim), lambda h, b: (0, h, 0, 0)),
-            pl.BlockSpec((blocks, 1, head_dim, rows), lambda h, b: (0, h, 0, 0)),
-        ],
-        out_specs=pl.BlockSpec((1, 1, head_dim, rows), lambda h, b: (b, h, 0, 0)),
-        scratch_shapes=[pltpu.VMEM((blocks, rows, rows), jnp.float32)],
-        compiler_params=pltpu.CompilerParams(vmem_limit_bytes=48 * 1024 * 1024),
-    )(q_t, k_tok, v_t)
-
-
-def exchange_kernel(*refs, count, shards):
-    sends = refs[:count]
-    gots = refs[count : 2 * count]
-    send_sem, recv_sem, local_sem = refs[2 * count :]
+def start_sends(sends, gots, send_sem, recv_sem, local_sem, shards):
     me = lax.axis_index("ctx")
     region = lax.axis_index("region")
     mesh_id = pl.DeviceIdType.MESH
@@ -85,13 +31,13 @@
         pl.semaphore_signal(barrier, 1, device_id=(region, peer), device_id_type=mesh_id)
     pl.semaphore_wait(barrier, shards - 1)
     copies = []
-    for a in range(count):
+    for a in range(len(sends)):
         local = pltpu.make_async_copy(sends[a].at[me], gots[a].at[me], local_sem.at[a])
         local.start()
         copies.append(local)
     for d in range(1, shards):
         peer = lax.rem(me + d, shards)
-        for a in range(count):
+        for a in range(len(sends)):
             remote = pltpu.make_async_remote_copy(
                 src_ref=sends[a].at[peer],
                 dst_ref=gots[a].at[me],
@@ -102,8 +48,23 @@
             )
             remote.start()
             copies.append(remote)
+    return copies
+
+
+def exchange_kernel(*refs, count, shards):
+    sends = refs[:count]
+    gots = refs[count : 2 * count]
+    copies = start_sends(sends, gots, *refs[2 * count :], shards)
     for copy in copies:
         copy.wait()
+
+
+def send_scratch(count, shards):
+    return [
+        pltpu.SemaphoreType.DMA((count, shards - 1)),
+        pltpu.SemaphoreType.DMA((count, shards - 1)),
+        pltpu.SemaphoreType.DMA((count,)),
+    ]
 
 
 def exchange(arrays, shards, collective_id):
@@ -115,15 +76,106 @@
         out_shape=[jax.ShapeDtypeStruct(x.shape, x.dtype) for x in arrays],
         in_specs=[any_spec] * count,
         out_specs=[any_spec] * count,
-        scratch_shapes=[
-            pltpu.SemaphoreType.DMA((count, shards - 1)),
-            pltpu.SemaphoreType.DMA((count, shards - 1)),
-            pltpu.SemaphoreType.DMA((count,)),
-        ],
+        scratch_shapes=send_scratch(count, shards),
         compiler_params=pltpu.CompilerParams(
             collective_id=collective_id, has_side_effects=True
         ),
     )(*arrays)
+
+
+def attend_body(qt_ref, k_ref, vt_ref, o_ref, s_scr, inv_root):
+    blocks, head_dim, q_rows = qt_ref.shape
+
+    def one_block(b, carry):
+        qt = qt_ref[b]
+
+        def score(c, m):
+            s = jnp.dot(k_ref[c], qt, preferred_element_type=jnp.float32) * inv_root
+            s_scr[c] = s
+            return jnp.maximum(m, jnp.max(s, axis=0, keepdims=True))
+
+        m = lax.fori_loop(0, blocks, score, jnp.full((1, q_rows), -jnp.inf, jnp.float32))
+
+        def accumulate(c, inner):
+            total, acc = inner
+            expo = jnp.exp(s_scr[c] - m)
+            total = total + jnp.sum(expo, axis=0, keepdims=True)
+            acc = acc + jnp.dot(
+                vt_ref[c], expo.astype(jnp.bfloat16), preferred_element_type=jnp.float32
+            )
+            return total, acc
+
+        total, acc = lax.fori_loop(
+            0,
+            blocks,
+            accumulate,
+            (
+                jnp.zeros((1, q_rows), jnp.float32),
+                jnp.zeros((head_dim, q_rows), jnp.float32),
+            ),
+        )
+        o_ref[b] = (acc / total).astype(o_ref.dtype)
+        return carry
+
+    lax.fori_loop(0, blocks, one_block, 0)
+
+
+def attend_send_kernel(*refs, count, shards, inv_root):
+    qt_ref, k_ref, vt_ref = refs[:3]
+    sends = refs[3 : 3 + count]
+    o_ref = refs[3 + count]
+    gots = refs[4 + count : 4 + 2 * count]
+    s_scr = refs[4 + 2 * count]
+    copies = start_sends(sends, gots, *refs[5 + 2 * count :], shards)
+    attend_body(qt_ref, k_ref, vt_ref, o_ref, s_scr, inv_root)
+    for copy in copies:
+        copy.wait()
+
+
+def attend_send(q_t, k_tok, v_t, sends, shards, inv_root, collective_id):
+    blocks, head_dim, rows = q_t.shape
+    count = len(sends)
+    kernel = functools.partial(
+        attend_send_kernel, count=count, shards=shards, inv_root=inv_root
+    )
+    any_spec = pl.BlockSpec(memory_space=pl.ANY)
+    vmem_spec = pl.BlockSpec(memory_space=pltpu.VMEM)
+    outs = pl.pallas_call(
+        kernel,
+        out_shape=[jax.ShapeDtypeStruct(q_t.shape, jnp.bfloat16)]
+        + [jax.ShapeDtypeStruct(x.shape, x.dtype) for x in sends],
+        in_specs=[vmem_spec] * 3 + [any_spec] * count,
+        out_specs=[vmem_spec] + [any_spec] * count,
+        scratch_shapes=[pltpu.VMEM((blocks, rows, rows), jnp.float32)]
+        + send_scratch(count, shards),
+        compiler_params=pltpu.CompilerParams(
+            collective_id=collective_id,
+            has_side_effects=True,
+            vmem_limit_bytes=48 * 1024 * 1024,
+        ),
+    )(q_t, k_tok, v_t, *sends)
+    return outs[0], outs[1:]
+
+
+def head_pipeline(q_all, k_all, v_all, shards, inverse_root):
+    pair = q_all.shape[0]
+    got = exchange([q_all[0], k_all[0], v_all[0]], shards, 0)
+    backs = []
+    for h in range(pair):
+        if h + 1 < pair:
+            sends = [q_all[h + 1], k_all[h + 1], v_all[h + 1]]
+        else:
+            sends = []
+        if h > 0:
+            sends = sends + [out_prev]
+        out_prev, sent = attend_send(*got, sends, shards, inverse_root, 1 + h)
+        if h + 1 < pair:
+            got = sent[:3]
+            sent = sent[3:]
+        backs.extend(sent)
+    (last_back,) = exchange([out_prev], shards, 1 + pair)
+    backs.append(last_back)
+    return jnp.stack(backs, axis=1)
 
 
 def per_device(
@@ -172,22 +224,21 @@
     pair = HEADS // shards
     inverse_root = 1.0 / math.sqrt(head_dim)
     w_parts = w_qkv.reshape(width, 3, shards, pair, head_dim)
-    q_send = jnp.einsum(
-        "td,dphe->phet", modulated, w_parts[:, 0], preferred_element_type=jnp.float32
+    q_all = jnp.einsum(
+        "td,dphe->hpet", modulated, w_parts[:, 0], preferred_element_type=jnp.float32
     ).astype(jnp.bfloat16)
-    k_send = jnp.einsum(
-        "td,dphe->phte", modulated, w_parts[:, 1], preferred_element_type=jnp.float32
+    k_all = jnp.einsum(
+        "td,dphe->hpte", modulated, w_parts[:, 1], preferred_element_type=jnp.float32
     ).astype(jnp.bfloat16)
-    v_send = jnp.einsum(
-        "td,dphe->phet", modulated, w_parts[:, 2], preferred_element_type=jnp.float32
+    v_all = jnp.einsum(
+        "td,dphe->hpet", modulated, w_parts[:, 2], preferred_element_type=jnp.float32
     ).astype(jnp.bfloat16)
-    q_got, k_got, v_got = exchange([q_send, k_send, v_send], shards, 0)
-    out_t = attend(q_got, k_got, v_got, inverse_root)
-    (back,) = exchange([out_t], shards, 1)
+    backs = head_pipeline(q_all, k_all, v_all, shards, inverse_root)
+    w_out_parts = w_out.reshape(shards, pair, head_dim, width)
     projected = jnp.einsum(
         "phet,pheD->tD",
-        back,
-        w_out.reshape(shards, pair, head_dim, width),
+        backs,
+        w_out_parts,
         preferred_element_type=jnp.float32,
     )
     gate = mods[:, 2 * width :]

time: 271 us -> 246 us (0.908)
  Pallas kernels: 145 us -> 119 us
  local copies, waits for them, and re-layouts: 52.6 us -> 60.5 us
  other arithmetic: 11.1 us -> 6.96 us
  matrix products: 21.4 us -> 18.3 us
    pallas_call x2, Pallas kernels: 68.3 us -> 37.6 us  [exchange(): pl.pallas_call(kernel, out_shape=[jax.ShapeDtypeStruct(x.shape, x.dtype)...]
    pallas_call x1 -> x2, Pallas kernels: 76.8 us -> 81.9 us  [attend_send(): pl.pallas_call(kernel, out_shape=[jax.ShapeDtypeStruct(q_t.shape, jnp.bfl...]
    squeeze x0 -> x2, local copies, waits for them, and re-layouts: none -> 4.53 us  [head_pipeline(): sends = [q_all[h + 1], k_all[h + 1], v_all[h + 1]]]
    convert_element_type x2 -> x1, other arithmetic: 5.37 us -> 1.2 us  [per_device(): k_all = jnp.einsum('td,dphe->hpte', modulated, w_parts[:, 1], preferred_e...]
    unnamed x3, matrix products: 8.06 us -> 5.18 us
    unnamed x25 -> x31, local copies, waits for them, and re-layouts: 19.8 us -> 20.9 us
where the time goes in v3:
time: 246 us; the launch traced here: 245 us
  Pallas kernels  119 us (48%)
  local copies, waits for them, and re-layouts  60.5 us (25%)
  blocking collectives  20.5 us (8%)
  matrix products  18.3 us (7%)
  waiting for transfers between devices  12.5 us (5%)
  other arithmetic  6.96 us (3%)
  starting transfers between devices  5.9 us (2%)
    pallas_call x2, Pallas kernels, attend_send(): pl.pallas_call(kernel, out_shape=[jax.ShapeDtypeStruct(q_t.shape, jnp.bfl...  81.9 us
    pallas_call x2, Pallas kernels, exchange(): pl.pallas_call(kernel, out_shape=[jax.ShapeDtypeStruct(x.shape, x.dtype)...  37.6 us
    unnamed x31, local copies, waits for them, and re-layouts  20.9 us
    all_to_all x1, blocking collectives, per_device(): lax.all_to_all(requests.reshape(owners, capacity), ('region', 'ctx'), spl...  20.5 us
    all_to_all x1, waiting for transfers between devices, per_device(): lax.all_to_all(served, ('region', 'ctx'), split_axis=0, concat_axis=0, ti...  12.5 us
    dot_general x1, matrix products, per_device(): jnp.dot(activated, w_ada, preferred_element_type=jnp.float32) + b_ada  8.01 us
    all_to_all x1, starting transfers between devices, per_device(): lax.all_to_all(served, ('region', 'ctx'), split_axis=0, concat_axis=0, ti...  5.9 us
    slice x1, local copies, waits for them, and re-layouts, per_device(): w_parts[:, 2]  5.62 us
  transfers between devices with their start and end apart: 1, of which 1 were waited for; matrix products, arithmetic and copies ran while one was open for 8% of the time, Pallas kernels for 0%

profile of v3, /device:TPU:0, one launch (start us, length us, event | category | flops | bytes accessed | tf_op | source)
XLA Modules:
  0.0 245.2 jit_solution(16714568821875691780)
XLA Ops:
  1.6 3.5 %gather_fusion = s32[512]{0:T(512)S(1)} fusion(s32[16384]{0:T(1024)} %param.11, s32[1024]{0:T(1024)S(1)} %pad_clamp_fusion.2), kind=kCustom, calls=%fused_computation | custom fusion | bytes 6144 | tf_op jit(solution)/shard_map/gather | solution.py:190
  5.4 2.4 scatter_custom_fusion
  8.0 20.5 %all_to_all.14 = s32[128,1,6]{2,1,0:T(1,128)S(1)} all-to-all(s32[128,1,6]{2,1,0:T(1,128)S(1)} %bitcast.101), channel_id=1, replica_groups=mesh['region'=16,'ctx'=8] {'region','ctx'}, dimensions={0} | all-to-all | bytes 6144 | tf_op jit(solution)/shard_map/all_to_all | solution.py:203
  30.0 3.7 %gather_fusion.1 = bf16[768,1152]{1,0:T(8,128)(2,1)} fusion(bf16[128,1152]{1,0:T(8,128)(2,1)S(1)} %copy-done.6, s32[1024]{0:T(1024)S(1)} %pad_clamp_fusion.1), kind=kCustom, calls=%fused_computation.1 | custom fusion | bytes 3542016 | tf_op jit(solution)/shard_map/gather | solution.py:211
  33.7 3.9 %reshape.215 = bf16[128,6,1152]{2,1,0:T(8,128)(2,1)} reshape(bf16[768,1152]{1,0:T(8,128)(2,1)} %gather_fusion.1) | data formatting | bytes 3538944 | tf_op jit(solution)/shard_map/reshape | solution.py:211
  37.6 5.9 %all-to-all-start.1 = ((bf16[128,6,1152]{2,1,0:T(8,128)(2,1)}), bf16[128,6,1152]{2,1,0:T(8,128)(2,1)}, u32[]{:S(2)}, u32[]{:S(2)}) async-start(bf16[128,6,1152]{2,1,0:T(8,128)(2,1)} %reshape.215), calls=%async_computation.1 | async-start | bytes 4718592 | tf_op jit(solution)/shard_map/all_to_all | solution.py:212
  43.5 11.5 %copy.33 = bf16[1152,3456]{0,1:T(8,128)(2,1)} copy(bf16[1152,3456]{1,0:T(8,128)(2,1)} %param.16) | data formatting | bytes 15925248 | tf_op args[7]
  56.5 1.7 fusion.9
  58.2 5.6 %fusion.36 = (bf16[1152,1,8,2,72]{0,4,3,2,1:T(8,128)(2,1)}, bf16[1152,1,8,2,72]{0,4,3,2,1:T(8,128)(2,1)}, bf16[1152,1,8,2,72]{0,4,3,2,1:T(8,128)(2,1)}) fusion(bf16[1152,3,8,2,72]{0,4,3,2,1:T(8,128)(2,1)} %bitcast.90), kind=kLoop, calls=%fused_computation.78 | loop fusion | bytes 15925248 | tf_op jit(solution)/shard_map/slice | solution.py:234
  63.8 12.5 %all-to-all-done.1 = bf16[128,6,1152]{2,1,0:T(8,128)(2,1)} async-done(((bf16[128,6,1152]{2,1,0:T(8,128)(2,1)}), bf16[128,6,1152]{2,1,0:T(8,128)(2,1)}, u32[]{:S(2)}, u32[]{:S(2)}) %all-to-all-start.1) | async-done | bytes 1769504 | tf_op jit(solution)/shard_map/all_to_all | solution.py:212
  76.3 3.9 %reshape.216 = bf16[768,1152]{1,0:T(8,128)(2,1)} reshape(bf16[128,6,1152]{2,1,0:T(8,128)(2,1)} %all-to-all-done.1) | data formatting | bytes 3538944 | tf_op jit(solution)/shard_map/reshape | solution.py:213
  80.2 5.4 %gather_fusion.2 = bf16[512,1152]{1,0:T(8,128)(2,1)} fusion(bf16[768,1152]{1,0:T(8,128)(2,1)} %reshape.216, s32[1024]{0:T(1024)S(1)} %pad_clamp_fusion), kind=kCustom, calls=%fused_computation.2 | custom fusion | bytes 2361344 | tf_op jit(solution)/shard_map/gather | solution.py:213
  85.7 8.0 %fusion = f32[512,3456]{1,0:T(8,128)S(1)} fusion(bf16[1152,3456]{1,0:T(8,128)(2,1)} %param.14, f32[3456]{0:T(1024)S(1)} %copy-done.14, bf16[512,1152]{1,0:T(8,128)(2,1)} %gather_fusion.2, pred[512]{0:T(512)(128)(4,1)S(1)} %iota_compare_fusion.1), kind=kOutput, calls=%fused_computation.5 | convolution fusion | flops 4086300672 | bytes 16234496 | tf_op jit(solution)/shard_map/dot_general | solution.py:217
  94.3 2.7 %copy-done.10 = f32[512,3456]{1,0:T(8,128)} copy-done((f32[512,3456]{1,0:T(8,128)}, f32[512,3456]{1,0:T(8,128)S(1)}, u32[]{:S(2)}) %copy-start.10) | copy-done | bytes 7077912
  97.4 1.7 fusion.39
  101.3 1.7 fusion.38
  103.1 1.7 fusion.37
  107.2 3.6 %copy.35 = bf16[512,8,2,72]{3,0,1,2:T(8,128)(2,1)} copy(bf16[512,8,2,72]{0,3,2,1:T(8,128)(2,1)} %convert_element_type.56) | data formatting | bytes 2359296 | tf_op jit(solution)/shard_map/convert_element_type | solution.py:232
  110.8 3.2 %slice_bitcast_fusion = (bf16[8,512,72]{2,1,0:T(8,128)(2,1)}, bf16[8,512,72]{2,1,0:T(8,128)(2,1)}) fusion(bf16[2,8,512,72]{3,2,1,0:T(8,128)(2,1)} %bitcast.91), kind=kLoop, calls=%fused_computation.39 | loop fusion | bytes 2359296 | tf_op jit(solution)/shard_map/squeeze | solution.py:166
  115.3 28.0 %shard_map.91 = (bf16[8,72,512]{2,1,0:T(8,128)(2,1)}, bf16[8,512,72]{2,1,0:T(8,128)(2,1)}, bf16[8,72,512]{2,1,0:T(8,128)(2,1)}) custom-call(bf16[8,72,512]{2,1,0:T(8,128)(2,1)} %get-tuple-element.36.refs_0_, bf16[8,512,72]{2,1,0:T(8,128)(2,1)} %get-tuple-element.29.refs_1_, bf16[8,72,512]{2,1,0:T(8,128)(2,1)} %get-tuple-element.31.refs_2_), custom_call_target="tpu_custom_call" | custom-call | tf_op jit(solution)/shard_map/pallas_call | solution.py:74
  147.7 41.0 %shard_map.92 = (bf16[8,72,512]{2,1,0:T(8,128)(2,1)S(1)}, bf16[8,72,512]{2,1,0:T(8,128)(2,1)S(1)}, bf16[8,512,72]{2,1,0:T(8,128)(2,1)S(1)}, bf16[8,72,512]{2,1,0:T(8,128)(2,1)S(1)}) custom-call(bf16[8,72,512]{2,1,0:T(8,128)(2,1)S(1)} %copy-done.3, bf16[8,512,72]{2,1,0:T(8,128)(2,1)S(1)} %copy-done.2, bf16[8,72,512]{2,1,0:T(8,128)(2,1)S(1)} %copy-done.4, ...), custom_call_target="tpu_custom_call" | custom-call | tf_op jit(solution)/shard_map/pallas_call | solution.py:143
  188.7 40.9 %shard_map.93 = (bf16[8,72,512]{2,1,0:T(8,128)(2,1)S(1)}, bf16[8,72,512]{2,1,0:T(8,128)(2,1)S(1)}) custom-call(bf16[8,72,512]{2,1,0:T(8,128)(2,1)S(1)} %get-tuple-element.17.refs_0_, bf16[8,512,72]{2,1,0:T(8,128)(2,1)S(1)} %get-tuple-element.18.refs_1_, bf16[8,72,512]{2,1,0:T(8,128)(2,1)S(1)} %get-tuple-element.19.refs_2_, ...), custom_call_target="tpu_custom_call" | custom-call | tf_op jit(solution)/shard_map/pallas_call | solution.py:143
  230.5 9.6 %shard_map.94 = bf16[8,72,512]{2,1,0:T(8,128)(2,1)} custom-call(bf16[8,72,512]{2,1,0:T(8,128)(2,1)} %copy-done.5), custom_call_target="tpu_custom_call" | custom-call | tf_op jit(solution)/shard_map/pallas_call | solution.py:74
  240.0 5.1 %fusion.7 = bf16[1,512,1152]{2,1,0:T(8,128)(2,1)} fusion(bf16[1,512,1152]{2,1,0:T(8,128)(2,1)} %param.9, bf16[8,2,72,1152]{3,2,1,0:T(8,128)(2,1)S(1)} %bitcast.88, f32[512,3456]{1,0:T(8,128)} %copy-done.10, bf16[8,1,72,512]{3,2,0,1:T(8,128)(2,1)} %bitcast.100, bf16[8,1,72,512]{3,2,0,1:T(8,128)(2,1)S(1)} %bitcast.89), kind=kOutput, calls=%fused_computation.17 | convolution fusion | flops 1361903616 | bytes 8552448 | tf_op jit(solution)/shard_map/phet,pheD->tD/dot_general | solution.py:238
  (51 shorter events, 16.4 us)
Async XLA Ops:
  0.0 240.0 %copy-start = (bf16[1152,1152]{1,0:T(8,128)(2,1)S(1)}, bf16[1152,1152]{1,0:T(8,128)(2,1)}, u32[]{:S(2)}) copy-start(bf16[1152,1152]{1,0:T(8,128)(2,1)} %param.17) | copy-start | bytes 7962628
  0.0 30.0 %copy-start.6 = (bf16[128,1152]{1,0:T(8,128)(2,1)S(1)}, bf16[128,1152]{1,0:T(8,128)(2,1)}, u32[]{:S(2)}) copy-start(bf16[128,1152]{1,0:T(8,128)(2,1)} %param.13) | copy-start | bytes 884740
  37.6 38.8 %all-to-all-start.1 = ((bf16[128,6,1152]{2,1,0:T(8,128)(2,1)}), bf16[128,6,1152]{2,1,0:T(8,128)(2,1)}, u32[]{:S(2)}, u32[]{:S(2)}) async-start(bf16[128,6,1152]{2,1,0:T(8,128)(2,1)} %reshape.215), calls=%async_computation.1 | async-start | bytes 4718592 | tf_op jit(solution)/shard_map/all_to_all | solution.py:212
  80.2 5.4 %copy-start.14 = (f32[3456]{0:T(1024)S(1)}, f32[3456]{0:T(1024)}, u32[]{:S(2)}) copy-start(f32[3456]{0:T(1024)} %param.15) | copy-start | bytes 41476
  85.7 8.0 %copy-start.7 = (bf16[1,512,1152]{2,1,0:T(8,128)(2,1)S(1)}, bf16[1,512,1152]{2,1,0:T(8,128)(2,1)}, u32[]{:S(2)}) copy-start(bf16[1,512,1152]{2,1,0:T(8,128)(2,1)} %param.9) | copy-start | bytes 3538948
  93.7 3.3 %copy-start.10 = (f32[512,3456]{1,0:T(8,128)}, f32[512,3456]{1,0:T(8,128)S(1)}, u32[]{:S(2)}) copy-start(f32[512,3456]{1,0:T(8,128)S(1)} %fusion) | copy-start | bytes 21233668
  93.7 3.7 %copy-start.13 = (bf16[1152,1,8,2,72]{0,4,3,2,1:T(8,128)(2,1)S(1)}, bf16[1152,1,8,2,72]{0,4,3,2,1:T(8,128)(2,1)}, u32[]{:S(2)}) copy-start(bf16[1152,1,8,2,72]{0,4,3,2,1:T(8,128)(2,1)} %get-tuple-element.25) | copy-start | bytes 7962628
  99.1 2.2 copy-start.12
  101.3 1.7 copy-start.11
  110.7 3.2 %copy-start.8 = (bf16[512,8,2,72]{0,3,1,2:T(8,128)(2,1)S(1)}, bf16[512,8,2,72]{0,3,1,2:T(8,128)(2,1)}, u32[]{:S(2)}) copy-start(bf16[512,8,2,72]{0,3,1,2:T(8,128)(2,1)} %copy.48) | copy-start | bytes 3538948
  110.8 3.2 %copy-start.9 = (bf16[512,8,2,72]{0,3,1,2:T(8,128)(2,1)S(1)}, bf16[512,8,2,72]{0,3,1,2:T(8,128)(2,1)}, u32[]{:S(2)}) copy-start(bf16[512,8,2,72]{0,3,1,2:T(8,128)(2,1)} %copy.47) | copy-start | bytes 3538948
  143.3 1.1 copy-start.1
  144.4 1.2 copy-start.2
  145.6 1.1 copy-start.3
  146.6 1.1 copy-start.4
  229.6 0.8 copy-start.5

commit v4 on v3

--- a/solution.py
+++ b/solution.py
@@ -94,7 +94,9 @@
             s_scr[c] = s
             return jnp.maximum(m, jnp.max(s, axis=0, keepdims=True))
 
-        m = lax.fori_loop(0, blocks, score, jnp.full((1, q_rows), -jnp.inf, jnp.float32))
+        m = lax.fori_loop(
+            0, blocks, score, jnp.full((1, q_rows), -jnp.inf, jnp.float32), unroll=2
+        )
 
         def accumulate(c, inner):
             total, acc = inner
@@ -113,6 +115,7 @@
                 jnp.zeros((1, q_rows), jnp.float32),
                 jnp.zeros((head_dim, q_rows), jnp.float32),
             ),
+            unroll=2,
         )
         o_ref[b] = (acc / total).astype(o_ref.dtype)
         return carry

time: 246 us -> 229 us (0.931)
  Pallas kernels: 119 us -> 102 us
    pallas_call x2, Pallas kernels: 81.9 us -> 64.2 us  [attend_send(): pl.pallas_call(kernel, out_shape=[jax.ShapeDtypeStruct(q_t.shape, jnp.bfl...]
  transfers between devices with their start and end apart: 1 -> 1, of which waited for: 1 -> 1; matrix products, arithmetic and copies ran while one was open for 8% -> 9% of each run, Pallas kernels for 0% -> 0%
where the time goes in v4:
time: 229 us; the launch traced here: 228 us
  Pallas kernels  102 us (45%)
  local copies, waits for them, and re-layouts  60.5 us (26%)
  blocking collectives  20.5 us (9%)
  matrix products  18.3 us (8%)
  waiting for transfers between devices  12.5 us (5%)
  other arithmetic  6.96 us (3%)
  starting transfers between devices  5.9 us (3%)
    pallas_call x2, Pallas kernels, attend_send(): pl.pallas_call(kernel, out_shape=[jax.ShapeDtypeStruct(q_t.shape, jnp.bfl...  64.2 us
    pallas_call x2, Pallas kernels, exchange(): pl.pallas_call(kernel, out_shape=[jax.ShapeDtypeStruct(x.shape, x.dtype)...  37.6 us
    unnamed x31, local copies, waits for them, and re-layouts  20.9 us
    all_to_all x1, blocking collectives, per_device(): lax.all_to_all(requests.reshape(owners, capacity), ('region', 'ctx'), spl...  20.5 us
    all_to_all x1, waiting for transfers between devices, per_device(): lax.all_to_all(served, ('region', 'ctx'), split_axis=0, concat_axis=0, ti...  12.5 us
    dot_general x1, matrix products, per_device(): jnp.dot(activated, w_ada, preferred_element_type=jnp.float32) + b_ada  8.01 us
    all_to_all x1, starting transfers between devices, per_device(): lax.all_to_all(served, ('region', 'ctx'), split_axis=0, concat_axis=0, ti...  5.9 us
    slice x1, local copies, waits for them, and re-layouts, per_device(): w_parts[:, 2]  5.62 us
  transfers between devices with their start and end apart: 1, of which 1 were waited for; matrix products, arithmetic and copies ran while one was open for 9% of the time, Pallas kernels for 0%

profile of v4, /device:TPU:0, one launch (start us, length us, event | category | flops | bytes accessed | tf_op | source)
XLA Modules:
  0.0 227.5 jit_solution(1119250951365357295)
XLA Ops:
  1.6 3.5 %gather_fusion = s32[512]{0:T(512)S(1)} fusion(s32[16384]{0:T(1024)} %param.11, s32[1024]{0:T(1024)S(1)} %pad_clamp_fusion.2), kind=kCustom, calls=%fused_computation | custom fusion | bytes 6144 | tf_op jit(solution)/shard_map/gather | solution.py:193
  5.4 2.4 %scatter_custom_fusion = s32[768]{0:T(1024)S(1)} fusion(s32[512]{0:T(512)S(1)} %bitcast.106, s32[512]{0:T(512)S(1)} %get-tuple-element.34, s32[]{:T(128)} %constant.24.clone.1), kind=kCustom, calls=%fused_computation.69 | custom fusion | bytes 3076 | tf_op jit(solution)/shard_map/scatter | solution.py:205
  8.0 20.5 %all_to_all.14 = s32[128,1,6]{2,1,0:T(1,128)S(1)} all-to-all(s32[128,1,6]{2,1,0:T(1,128)S(1)} %bitcast.101), channel_id=1, replica_groups=mesh['region'=16,'ctx'=8] {'region','ctx'}, dimensions={0} | all-to-all | bytes 6144 | tf_op jit(solution)/shard_map/all_to_all | solution.py:206
  30.0 3.7 %gather_fusion.1 = bf16[768,1152]{1,0:T(8,128)(2,1)} fusion(bf16[128,1152]{1,0:T(8,128)(2,1)S(1)} %copy-done.6, s32[1024]{0:T(1024)S(1)} %pad_clamp_fusion.1), kind=kCustom, calls=%fused_computation.1 | custom fusion | bytes 3542016 | tf_op jit(solution)/shard_map/gather | solution.py:214
  33.7 3.9 %reshape.215 = bf16[128,6,1152]{2,1,0:T(8,128)(2,1)} reshape(bf16[768,1152]{1,0:T(8,128)(2,1)} %gather_fusion.1) | data formatting | bytes 3538944 | tf_op jit(solution)/shard_map/reshape | solution.py:214
  37.6 5.9 %all-to-all-start.1 = ((bf16[128,6,1152]{2,1,0:T(8,128)(2,1)}), bf16[128,6,1152]{2,1,0:T(8,128)(2,1)}, u32[]{:S(2)}, u32[]{:S(2)}) async-start(bf16[128,6,1152]{2,1,0:T(8,128)(2,1)} %reshape.215), calls=%async_computation.1 | async-start | bytes 4718592 | tf_op jit(solution)/shard_map/all_to_all | solution.py:215
  43.5 11.5 %copy.33 = bf16[1152,3456]{0,1:T(8,128)(2,1)} copy(bf16[1152,3456]{1,0:T(8,128)(2,1)} %param.16) | data formatting | bytes 15925248 | tf_op args[7]
  56.5 1.7 fusion.9
  58.2 5.6 %fusion.36 = (bf16[1152,1,8,2,72]{0,4,3,2,1:T(8,128)(2,1)}, bf16[1152,1,8,2,72]{0,4,3,2,1:T(8,128)(2,1)}, bf16[1152,1,8,2,72]{0,4,3,2,1:T(8,128)(2,1)}) fusion(bf16[1152,3,8,2,72]{0,4,3,2,1:T(8,128)(2,1)} %bitcast.90), kind=kLoop, calls=%fused_computation.78 | loop fusion | bytes 15925248 | tf_op jit(solution)/shard_map/slice | solution.py:237
  63.8 12.5 %all-to-all-done.1 = bf16[128,6,1152]{2,1,0:T(8,128)(2,1)} async-done(((bf16[128,6,1152]{2,1,0:T(8,128)(2,1)}), bf16[128,6,1152]{2,1,0:T(8,128)(2,1)}, u32[]{:S(2)}, u32[]{:S(2)}) %all-to-all-start.1) | async-done | bytes 1769504 | tf_op jit(solution)/shard_map/all_to_all | solution.py:215
  76.3 3.9 %reshape.216 = bf16[768,1152]{1,0:T(8,128)(2,1)} reshape(bf16[128,6,1152]{2,1,0:T(8,128)(2,1)} %all-to-all-done.1) | data formatting | bytes 3538944 | tf_op jit(solution)/shard_map/reshape | solution.py:216
  80.2 5.4 %gather_fusion.2 = bf16[512,1152]{1,0:T(8,128)(2,1)} fusion(bf16[768,1152]{1,0:T(8,128)(2,1)} %reshape.216, s32[1024]{0:T(1024)S(1)} %pad_clamp_fusion), kind=kCustom, calls=%fused_computation.2 | custom fusion | bytes 2361344 | tf_op jit(solution)/shard_map/gather | solution.py:216
  85.7 8.0 %fusion = f32[512,3456]{1,0:T(8,128)S(1)} fusion(bf16[1152,3456]{1,0:T(8,128)(2,1)} %param.14, f32[3456]{0:T(1024)S(1)} %copy-done.14, bf16[512,1152]{1,0:T(8,128)(2,1)} %gather_fusion.2, pred[512]{0:T(512)(128)(4,1)S(1)} %iota_compare_fusion.1), kind=kOutput, calls=%fused_computation.5 | convolution fusion | flops 4086300672 | bytes 16234496 | tf_op jit(solution)/shard_map/dot_general | solution.py:220
  94.3 2.7 %copy-done.10 = f32[512,3456]{1,0:T(8,128)} copy-done((f32[512,3456]{1,0:T(8,128)}, f32[512,3456]{1,0:T(8,128)S(1)}, u32[]{:S(2)}) %copy-start.10) | copy-done | bytes 7077912
  97.4 1.7 fusion.39
  101.3 1.7 fusion.38
  103.1 1.7 fusion.37
  107.2 3.6 %copy.35 = bf16[512,8,2,72]{3,0,1,2:T(8,128)(2,1)} copy(bf16[512,8,2,72]{0,3,2,1:T(8,128)(2,1)} %convert_element_type.56) | data formatting | bytes 2359296 | tf_op jit(solution)/shard_map/convert_element_type | solution.py:235
  110.8 3.2 %slice_bitcast_fusion = (bf16[8,512,72]{2,1,0:T(8,128)(2,1)}, bf16[8,512,72]{2,1,0:T(8,128)(2,1)}) fusion(bf16[2,8,512,72]{3,2,1,0:T(8,128)(2,1)} %bitcast.91), kind=kLoop, calls=%fused_computation.39 | loop fusion | bytes 2359296 | tf_op jit(solution)/shard_map/squeeze | solution.py:169
  115.3 28.0 %shard_map.91 = (bf16[8,72,512]{2,1,0:T(8,128)(2,1)}, bf16[8,512,72]{2,1,0:T(8,128)(2,1)}, bf16[8,72,512]{2,1,0:T(8,128)(2,1)}) custom-call(bf16[8,72,512]{2,1,0:T(8,128)(2,1)} %get-tuple-element.36.refs_0_, bf16[8,512,72]{2,1,0:T(8,128)(2,1)} %get-tuple-element.29.refs_1_, bf16[8,72,512]{2,1,0:T(8,128)(2,1)} %get-tuple-element.31.refs_2_), custom_call_target="tpu_custom_call" | custom-call | tf_op jit(solution)/shard_map/pallas_call | solution.py:74
  147.7 32.4 %shard_map.92 = (bf16[8,72,512]{2,1,0:T(8,128)(2,1)S(1)}, bf16[8,72,512]{2,1,0:T(8,128)(2,1)S(1)}, bf16[8,512,72]{2,1,0:T(8,128)(2,1)S(1)}, bf16[8,72,512]{2,1,0:T(8,128)(2,1)S(1)}) custom-call(bf16[8,72,512]{2,1,0:T(8,128)(2,1)S(1)} %copy-done.3, bf16[8,512,72]{2,1,0:T(8,128)(2,1)S(1)} %copy-done.2, bf16[8,72,512]{2,1,0:T(8,128)(2,1)S(1)} %copy-done.4, ...), custom_call_target="tpu_custom_call" | custom-call | tf_op jit(solution)/shard_map/pallas_call | solution.py:146
  180.1 31.9 %shard_map.93 = (bf16[8,72,512]{2,1,0:T(8,128)(2,1)S(1)}, bf16[8,72,512]{2,1,0:T(8,128)(2,1)S(1)}) custom-call(bf16[8,72,512]{2,1,0:T(8,128)(2,1)S(1)} %get-tuple-element.17.refs_0_, bf16[8,512,72]{2,1,0:T(8,128)(2,1)S(1)} %get-tuple-element.18.refs_1_, bf16[8,72,512]{2,1,0:T(8,128)(2,1)S(1)} %get-tuple-element.19.refs_2_, ...), custom_call_target="tpu_custom_call" | custom-call | tf_op jit(solution)/shard_map/pallas_call | solution.py:146
  212.8 9.6 %shard_map.94 = bf16[8,72,512]{2,1,0:T(8,128)(2,1)} custom-call(bf16[8,72,512]{2,1,0:T(8,128)(2,1)} %copy-done.5), custom_call_target="tpu_custom_call" | custom-call | tf_op jit(solution)/shard_map/pallas_call | solution.py:74
  222.4 5.1 %fusion.7 = bf16[1,512,1152]{2,1,0:T(8,128)(2,1)} fusion(bf16[1,512,1152]{2,1,0:T(8,128)(2,1)} %param.9, bf16[8,2,72,1152]{3,2,1,0:T(8,128)(2,1)S(1)} %bitcast.88, f32[512,3456]{1,0:T(8,128)} %copy-done.10, bf16[8,1,72,512]{3,2,0,1:T(8,128)(2,1)} %bitcast.100, bf16[8,1,72,512]{3,2,0,1:T(8,128)(2,1)S(1)} %bitcast.89), kind=kOutput, calls=%fused_computation.17 | convolution fusion | flops 1361903616 | bytes 8552448 | tf_op jit(solution)/shard_map/phet,pheD->tD/dot_general | solution.py:241
  (51 shorter events, 16.4 us)
Async XLA Ops:
  0.0 222.4 %copy-start = (bf16[1152,1152]{1,0:T(8,128)(2,1)S(1)}, bf16[1152,1152]{1,0:T(8,128)(2,1)}, u32[]{:S(2)}) copy-start(bf16[1152,1152]{1,0:T(8,128)(2,1)} %param.17) | copy-start | bytes 7962628
  0.0 30.0 %copy-start.6 = (bf16[128,1152]{1,0:T(8,128)(2,1)S(1)}, bf16[128,1152]{1,0:T(8,128)(2,1)}, u32[]{:S(2)}) copy-start(bf16[128,1152]{1,0:T(8,128)(2,1)} %param.13) | copy-start | bytes 884740
  37.6 38.8 %all-to-all-start.1 = ((bf16[128,6,1152]{2,1,0:T(8,128)(2,1)}), bf16[128,6,1152]{2,1,0:T(8,128)(2,1)}, u32[]{:S(2)}, u32[]{:S(2)}) async-start(bf16[128,6,1152]{2,1,0:T(8,128)(2,1)} %reshape.215), calls=%async_computation.1 | async-start | bytes 4718592 | tf_op jit(solution)/shard_map/all_to_all | solution.py:215
  80.2 5.4 %copy-start.14 = (f32[3456]{0:T(1024)S(1)}, f32[3456]{0:T(1024)}, u32[]{:S(2)}) copy-start(f32[3456]{0:T(1024)} %param.15) | copy-start | bytes 41476
  85.6 8.0 %copy-start.7 = (bf16[1,512,1152]{2,1,0:T(8,128)(2,1)S(1)}, bf16[1,512,1152]{2,1,0:T(8,128)(2,1)}, u32[]{:S(2)}) copy-start(bf16[1,512,1152]{2,1,0:T(8,128)(2,1)} %param.9) | copy-start | bytes 3538948
  93.7 3.3 %copy-start.10 = (f32[512,3456]{1,0:T(8,128)}, f32[512,3456]{1,0:T(8,128)S(1)}, u32[]{:S(2)}) copy-start(f32[512,3456]{1,0:T(8,128)S(1)} %fusion) | copy-start | bytes 21233668
  93.7 3.7 %copy-start.13 = (bf16[1152,1,8,2,72]{0,4,3,2,1:T(8,128)(2,1)S(1)}, bf16[1152,1,8,2,72]{0,4,3,2,1:T(8,128)(2,1)}, u32[]{:S(2)}) copy-start(bf16[1152,1,8,2,72]{0,4,3,2,1:T(8,128)(2,1)} %get-tuple-element.25) | copy-start | bytes 7962628
  99.1 2.2 copy-start.12
  101.3 1.7 copy-start.11
  110.7 3.2 %copy-start.8 = (bf16[512,8,2,72]{0,3,1,2:T(8,128)(2,1)S(1)}, bf16[512,8,2,72]{0,3,1,2:T(8,128)(2,1)}, u32[]{:S(2)}) copy-start(bf16[512,8,2,72]{0,3,1,2:T(8,128)(2,1)} %copy.48) | copy-start | bytes 3538948
  110.8 3.2 %copy-start.9 = (bf16[512,8,2,72]{0,3,1,2:T(8,128)(2,1)S(1)}, bf16[512,8,2,72]{0,3,1,2:T(8,128)(2,1)}, u32[]{:S(2)}) copy-start(bf16[512,8,2,72]{0,3,1,2:T(8,128)(2,1)} %copy.47) | copy-start | bytes 3538948
  143.3 1.1 copy-start.1
  144.3 1.2 copy-start.2
  145.6 1.1 copy-start.3
  146.6 1.1 copy-start.4
  212.0 0.8 copy-start.5

commit v5 on v4

--- a/solution.py
+++ b/solution.py
@@ -161,7 +161,7 @@
 
 
 def head_pipeline(q_all, k_all, v_all, shards, inverse_root):
-    pair = q_all.shape[0]
+    pair = len(q_all)
     got = exchange([q_all[0], k_all[0], v_all[0]], shards, 0)
     backs = []
     for h in range(pair):
@@ -189,7 +189,7 @@
     owners = lax.axis_size(("region", "ctx"))
     shards = lax.axis_size("ctx")
     elem_rows = cond_table.shape[0]
-    capacity = max(2, 3 * tok_rows // (2 * owners))
+    capacity = -(-max(2, 3 * tok_rows // (2 * owners)) // 8) * 8
     slots = element_slot[element_ids[0]]
     owner_index = slots // elem_rows
     local_row = slots % elem_rows
@@ -227,15 +227,14 @@
     pair = HEADS // shards
     inverse_root = 1.0 / math.sqrt(head_dim)
     w_parts = w_qkv.reshape(width, 3, shards, pair, head_dim)
-    q_all = jnp.einsum(
-        "td,dphe->hpet", modulated, w_parts[:, 0], preferred_element_type=jnp.float32
-    ).astype(jnp.bfloat16)
-    k_all = jnp.einsum(
-        "td,dphe->hpte", modulated, w_parts[:, 1], preferred_element_type=jnp.float32
-    ).astype(jnp.bfloat16)
-    v_all = jnp.einsum(
-        "td,dphe->hpet", modulated, w_parts[:, 2], preferred_element_type=jnp.float32
-    ).astype(jnp.bfloat16)
+    def project(i, h, pattern):
+        return jnp.einsum(
+            pattern, modulated, w_parts[:, i, :, h], preferred_element_type=jnp.float32
+        ).astype(jnp.bfloat16)
+
+    q_all = [project(0, h, "td,dpe->pet") for h in range(pair)]
+    k_all = [project(1, h, "td,dpe->pte") for h in range(pair)]
+    v_all = [project(2, h, "td,dpe->pet") for h in range(pair)]
     backs = head_pipeline(q_all, k_all, v_all, shards, inverse_root)
     w_out_parts = w_out.reshape(shards, pair, head_dim, width)
     projected = jnp.einsum(

time: 229 us -> 223 us (0.974)
  local copies, waits for them, and re-layouts: 60.5 us -> 45.6 us
  matrix products: 18.3 us -> 24.9 us
    reshape x2 -> x0, local copies, waits for them, and re-layouts: 7.75 us -> none  [the longest x1 3.88 us: per_device(): picked = replies.reshape(owners * capacity, width)[pick_at]]
    unnamed x3 -> x6, matrix products: 5.18 us -> 11.8 us
    squeeze x2 -> x0, local copies, waits for them, and re-layouts: 4.53 us -> none  [head_pipeline(): sends = [q_all[h + 1], k_all[h + 1], v_all[h + 1]]]
    convert_element_type x1 -> x4, other arithmetic: 1.2 us -> 4.13 us  [project(): return jnp.einsum(pattern, modulated, w_parts[:, i, :, h], preferred_elem...]
    dot_general x2 -> x0, local copies, waits for them, and re-layouts: 2.32 us -> none  [the longest x1 1.16 us: per_device(): jnp.einsum('td,dphe->hpet', modulated, w_parts[:, 2], preferred_element_t...]
    unnamed x31 -> x41, local copies, waits for them, and re-layouts: 20.9 us -> 19.4 us
where the time goes in v5:
time: 223 us; the launch traced here: 222 us
  Pallas kernels  102 us (46%)
  local copies, waits for them, and re-layouts  45.6 us (20%)
  matrix products  24.9 us (11%)
  blocking collectives  20.5 us (9%)
  waiting for transfers between devices  13.5 us (6%)
  other arithmetic  8.71 us (4%)
  starting transfers between devices  5.9 us (3%)
    pallas_call x2, Pallas kernels, attend_send(): pl.pallas_call(kernel, out_shape=[jax.ShapeDtypeStruct(q_t.shape, jnp.bfl...  64.2 us
    pallas_call x2, Pallas kernels, exchange(): pl.pallas_call(kernel, out_shape=[jax.ShapeDtypeStruct(x.shape, x.dtype)...  37.6 us
    all_to_all x1, blocking collectives, per_device(): lax.all_to_all(requests.reshape(owners, capacity), ('region', 'ctx'), spl...  20.5 us
    unnamed x41, local copies, waits for them, and re-layouts  19.4 us
    all_to_all x1, waiting for transfers between devices, per_device(): lax.all_to_all(served, ('region', 'ctx'), split_axis=0, concat_axis=0, ti...  13.5 us
    unnamed x6, matrix products  11.8 us
    dot_general x1, matrix products, per_device(): jnp.dot(activated, w_ada, preferred_element_type=jnp.float32) + b_ada  8.01 us
    all_to_all x1, starting transfers between devices, per_device(): lax.all_to_all(served, ('region', 'ctx'), split_axis=0, concat_axis=0, ti...  5.9 us
  transfers between devices with their start and end apart: 1, of which 1 were waited for; matrix products, arithmetic and copies ran while one was open for 9% of the time, Pallas kernels for 0%

profile of v5, /device:TPU:0, one launch (start us, length us, event | category | flops | bytes accessed | tf_op | source)
XLA Modules:
  0.0 221.9 jit_solution(7095886501312236137)
XLA Ops:
  1.6 3.5 %gather_fusion = s32[512]{0:T(512)S(1)} fusion(s32[16384]{0:T(1024)} %param.11, s32[1024]{0:T(1024)S(1)} %pad_clamp_fusion.1), kind=kCustom, calls=%fused_computation | custom fusion | bytes 6144 | tf_op jit(solution)/shard_map/gather | solution.py:193
  5.4 2.4 %scatter_custom_fusion = s32[1024]{0:T(1024)S(1)} fusion(s32[512]{0:T(512)S(1)} %bitcast.137, s32[512]{0:T(512)S(1)} %get-tuple-element.31, s32[]{:T(128)} %constant.24.clone.1), kind=kCustom, calls=%fused_computation.62 | custom fusion | bytes 4100 | tf_op jit(solution)/shard_map/scatter | solution.py:205
  8.0 20.5 %all_to_all.14 = s32[128,1,8]{2,1,0:T(1,128)S(1)} all-to-all(s32[128,1,8]{2,1,0:T(1,128)S(1)} %bitcast.131), channel_id=1, replica_groups=mesh['region'=16,'ctx'=8] {'region','ctx'}, dimensions={0} | all-to-all | bytes 8192 | tf_op jit(solution)/shard_map/all_to_all | solution.py:206
  29.9 5.4 %gather_fusion.1 = bf16[1024,1152]{1,0:T(8,128)(2,1)} fusion(bf16[128,1152]{1,0:T(8,128)(2,1)S(1)} %copy-done.6, s32[1024]{0:T(1024)S(1)} %broadcast_clamp_fusion), kind=kCustom, calls=%fused_computation.1 | custom fusion | bytes 4722688 | tf_op jit(solution)/shard_map/gather | solution.py:214
  35.4 5.9 %all-to-all-start.1 = ((bf16[128,8,1152]{2,1,0:T(8,128)(2,1)}), bf16[128,8,1152]{2,1,0:T(8,128)(2,1)}, u32[]{:S(2)}, u32[]{:S(2)}) async-start(bf16[128,8,1152]{2,1,0:T(8,128)(2,1)} %bitcast.115), calls=%async_computation.1 | async-start | bytes 4718592 | tf_op jit(solution)/shard_map/all_to_all | solution.py:215
  41.3 11.5 %copy.46 = bf16[1152,3456]{0,1:T(8,128)(2,1)} copy(bf16[1152,3456]{1,0:T(8,128)(2,1)} %param.16) | data formatting | bytes 15925248 | tf_op args[7]
  52.8 1.6 convert_reduce_fusion
  54.9 5.8 %fusion.33 = (bf16[1152,1,8,1,72]{0,4,3,2,1:T(8,128)(2,1)}, bf16[1152,1,8,1,72]{0,4,3,2,1:T(8,128)(2,1)}, bf16[1152,1,8,1,72]{0,4,3,2,1:T(8,128)(2,1)}, bf16[115...) fusion(bf16[1152,3,8,2,72]{0,4,3,2,1:T(8,128)(2,1)} %bitcast.114), kind=kLoop, calls=%fused_computation.71 | loop fusion | bytes 15925248 | tf_op jit(solution)/shard_map/slice | solution.py:232
  60.7 13.5 %all-to-all-done.1 = bf16[128,8,1152]{2,1,0:T(8,128)(2,1)} async-done(((bf16[128,8,1152]{2,1,0:T(8,128)(2,1)}), bf16[128,8,1152]{2,1,0:T(8,128)(2,1)}, u32[]{:S(2)}, u32[]{:S(2)}) %all-to-all-start.1) | async-done | bytes 2359328 | tf_op jit(solution)/shard_map/all_to_all | solution.py:215
  74.2 5.7 %gather_fusion.2 = bf16[512,1152]{1,0:T(8,128)(2,1)} fusion(bf16[1024,1152]{1,0:T(8,128)(2,1)} %bitcast.10, s32[1024]{0:T(1024)S(1)} %pad_clamp_fusion), kind=kCustom, calls=%fused_computation.2 | custom fusion | bytes 2361344 | tf_op jit(solution)/shard_map/gather | solution.py:216
  79.8 8.0 %fusion = f32[512,3456]{1,0:T(8,128)S(1)} fusion(bf16[1152,3456]{1,0:T(8,128)(2,1)} %param.14, f32[3456]{0:T(1024)S(1)} %copy-done.19, bf16[512,1152]{1,0:T(8,128)(2,1)} %gather_fusion.2, pred[512]{0:T(512)(128)(4,1)S(1)} %iota_compare_fusion.1), kind=kOutput, calls=%fused_computation.5 | convolution fusion | flops 4086300672 | bytes 16234496 | tf_op jit(solution)/shard_map/dot_general | solution.py:220
  88.5 2.2 %copy-done.9 = f32[512,3456]{1,0:T(8,128)} copy-done((f32[512,3456]{1,0:T(8,128)}, f32[512,3456]{1,0:T(8,128)S(1)}, u32[]{:S(2)}) %copy-start.9) | copy-done | bytes 7077912
  90.8 2.0 fusion.39
  93.8 1.3 copy.53
  95.1 3.9 %fusion.37 = f32[512,576]{0,1} fusion(bf16[512,1152]{1,0:T(8,128)(2,1)} %copy-done.17, bf16[1152,576]{0,1:T(8,128)(2,1)} %bitcast.121), kind=kOutput, calls=%fused_computation.75 | convolution fusion | flops 679477248 | bytes 3686400
  99.0 2.0 fusion.36
  102.3 2.0 fusion.34
  104.4 1.3 copy.49
  105.7 2.8 %convert_bitcast_fusion.1 = (bf16[8,72,512]{2,1,0:T(8,128)(2,1)S(1)}, bf16[8,72,512]{2,1,0:T(8,128)(2,1)}) fusion(f32[512,8,72]{0,2,1:T(8,128)} %bitcast.124, f32[512,8,72]{0,2,1:T(8,128)} %bitcast.126), kind=kLoop, calls=%fused_computation.39 | loop fusion | flops 589824 | bytes 3538944 | tf_op jit(solution)/shard_map/convert_element_type | solution.py:233
  109.7 28.0 %shard_map.91 = (bf16[8,72,512]{2,1,0:T(8,128)(2,1)}, bf16[8,512,72]{2,1,0:T(8,128)(2,1)}, bf16[8,72,512]{2,1,0:T(8,128)(2,1)}) custom-call(bf16[8,72,512]{2,1,0:T(8,128)(2,1)} %get-tuple-element.34.refs_0_, bf16[8,512,72]{2,1,0:T(8,128)(2,1)} %bitcast.117, bf16[8,72,512]{2,1,0:T(8,128)(2,1)} %get-tuple-element.33.refs_2_), custom_call_target="tpu_custom_call" | custom-call | tf_op jit(solution)/shard_map/pallas_call | solution.py:74
  142.1 32.2 %shard_map.92 = (bf16[8,72,512]{2,1,0:T(8,128)(2,1)S(1)}, bf16[8,72,512]{2,1,0:T(8,128)(2,1)S(1)}, bf16[8,512,72]{2,1,0:T(8,128)(2,1)S(1)}, bf16[8,72,512]{2,1,0:T(8,128)(2,1)S(1)}) custom-call(bf16[8,72,512]{2,1,0:T(8,128)(2,1)S(1)} %copy-done.3, bf16[8,512,72]{2,1,0:T(8,128)(2,1)S(1)} %copy-done.2, bf16[8,72,512]{2,1,0:T(8,128)(2,1)S(1)} %copy-done.4, ...), custom_call_target="tpu_custom_call" | custom-call | tf_op jit(solution)/shard_map/pallas_call | solution.py:146
  174.3 32.1 %shard_map.93 = (bf16[8,72,512]{2,1,0:T(8,128)(2,1)S(1)}, bf16[8,72,512]{2,1,0:T(8,128)(2,1)S(1)}) custom-call(bf16[8,72,512]{2,1,0:T(8,128)(2,1)S(1)} %get-tuple-element.17.refs_0_, bf16[8,512,72]{2,1,0:T(8,128)(2,1)S(1)} %get-tuple-element.18.refs_1_, bf16[8,72,512]{2,1,0:T(8,128)(2,1)S(1)} %get-tuple-element.19.refs_2_, ...), custom_call_target="tpu_custom_call" | custom-call | tf_op jit(solution)/shard_map/pallas_call | solution.py:146
  207.2 9.6 %shard_map.94 = bf16[8,72,512]{2,1,0:T(8,128)(2,1)} custom-call(bf16[8,72,512]{2,1,0:T(8,128)(2,1)} %copy-done.5), custom_call_target="tpu_custom_call" | custom-call | tf_op jit(solution)/shard_map/pallas_call | solution.py:74
  216.8 5.1 %fusion.7 = bf16[1,512,1152]{2,1,0:T(8,128)(2,1)} fusion(bf16[1,512,1152]{2,1,0:T(8,128)(2,1)} %param.9, bf16[8,2,72,1152]{3,2,1,0:T(8,128)(2,1)S(1)} %bitcast.112, f32[512,3456]{1,0:T(8,128)} %copy-done.9, bf16[8,1,72,512]{3,2,0,1:T(8,128)(2,1)} %bitcast.130, bf16[8,1,72,512]{3,2,0,1:T(8,128)(2,1)S(1)} %bitcast.113), kind=kOutput, calls=%fused_computation.17 | convolution fusion | flops 1361903616 | bytes 8552448 | tf_op jit(solution)/shard_map/phet,pheD->tD/dot_general | solution.py:240
  (62 shorter events, 12.6 us)
Async XLA Ops:
  0.0 216.8 %copy-start = (bf16[1152,1152]{1,0:T(8,128)(2,1)S(1)}, bf16[1152,1152]{1,0:T(8,128)(2,1)}, u32[]{:S(2)}) copy-start(bf16[1152,1152]{1,0:T(8,128)(2,1)} %param.17) | copy-start | bytes 7962628
  0.0 29.9 %copy-start.6 = (bf16[128,1152]{1,0:T(8,128)(2,1)S(1)}, bf16[128,1152]{1,0:T(8,128)(2,1)}, u32[]{:S(2)}) copy-start(bf16[128,1152]{1,0:T(8,128)(2,1)} %param.13) | copy-start | bytes 884740
  35.4 38.8 %all-to-all-start.1 = ((bf16[128,8,1152]{2,1,0:T(8,128)(2,1)}), bf16[128,8,1152]{2,1,0:T(8,128)(2,1)}, u32[]{:S(2)}, u32[]{:S(2)}) async-start(bf16[128,8,1152]{2,1,0:T(8,128)(2,1)} %bitcast.115), calls=%async_computation.1 | async-start | bytes 4718592 | tf_op jit(solution)/shard_map/all_to_all | solution.py:215
  52.8 1.6 copy-start.7
  74.1 5.7 %copy-start.19 = (f32[3456]{0:T(1024)S(1)}, f32[3456]{0:T(1024)}, u32[]{:S(2)}) copy-start(f32[3456]{0:T(1024)} %param.15) | copy-start | bytes 41476
  79.8 8.0 %copy-start.8 = (bf16[1,512,1152]{2,1,0:T(8,128)(2,1)S(1)}, bf16[1,512,1152]{2,1,0:T(8,128)(2,1)}, u32[]{:S(2)}) copy-start(bf16[1,512,1152]{2,1,0:T(8,128)(2,1)} %param.9) | copy-start | bytes 3538948
  87.9 2.9 %copy-start.9 = (f32[512,3456]{1,0:T(8,128)}, f32[512,3456]{1,0:T(8,128)S(1)}, u32[]{:S(2)}) copy-start(f32[512,3456]{1,0:T(8,128)S(1)} %fusion) | copy-start | bytes 21233668
  87.9 2.9 %copy-start.14 = (bf16[1152,1,8,1,72]{0,4,3,2,1:T(8,128)(2,1)S(1)}, bf16[1152,1,8,1,72]{0,4,3,2,1:T(8,128)(2,1)}, u32[]{:S(2)}) copy-start(bf16[1152,1,8,1,72]{0,4,3,2,1:T(8,128)(2,1)} %get-tuple-element.25) | copy-start | bytes 3981316
  90.8 2.0 copy-start.17
  90.8 2.0 copy-start.13
  95.1 3.9 %copy-start.12 = (bf16[1152,1,8,1,72]{0,4,3,2,1:T(8,128)(2,1)S(1)}, bf16[1152,1,8,1,72]{0,4,3,2,1:T(8,128)(2,1)}, u32[]{:S(2)}) copy-start(bf16[1152,1,8,1,72]{0,4,3,2,1:T(8,128)(2,1)} %get-tuple-element.28) | copy-start | bytes 3981316
  95.1 3.9 %copy-start.18 = (bf16[512,1152]{1,0:T(8,128)(2,1)S(1)}, bf16[512,1152]{1,0:T(8,128)(2,1)}, u32[]{:S(2)}) copy-start(bf16[512,1152]{1,0:T(8,128)(2,1)} %copy-done.17) | copy-start | bytes 3538948
  99.0 2.0 copy-start.11
  101.0 1.3 copy-start.10
  105.7 2.8 %copy-start.15 = (f32[512,576]{0,1:S(1)}, f32[512,576]{0,1}, u32[]{:S(2)}) copy-start(f32[512,576]{0,1} %fusion.36) | copy-start | bytes 3538948
  105.7 2.8 %copy-start.16 = (f32[512,576]{0,1:S(1)}, f32[512,576]{0,1}, u32[]{:S(2)}) copy-start(f32[512,576]{0,1} %fusion.34) | copy-start | bytes 3538948
  137.7 1.1 copy-start.1
  138.7 1.2 copy-start.2
  140.0 1.1 copy-start.3
  141.0 1.1 copy-start.4
  206.3 0.8 copy-start.5

commit v6 on v5

--- a/solution.py
+++ b/solution.py
@@ -83,7 +83,7 @@
     )(*arrays)
 
 
-def attend_body(qt_ref, k_ref, vt_ref, o_ref, s_scr, inv_root):
+def attend_body(qt_ref, k_ref, vt_ref, o_ref, s_scr, inv_root, after_block=None):
     blocks, head_dim, q_rows = qt_ref.shape
 
     def one_block(b, carry):
@@ -118,39 +118,100 @@
             unroll=2,
         )
         o_ref[b] = (acc / total).astype(o_ref.dtype)
+        if after_block is not None:
+            after_block(b)
         return carry
 
     lax.fori_loop(0, blocks, one_block, 0)
 
 
-def attend_send_kernel(*refs, count, shards, inv_root):
+def attend_send_kernel(*refs, count, shards, inv_root, stream):
     qt_ref, k_ref, vt_ref = refs[:3]
     sends = refs[3 : 3 + count]
     o_ref = refs[3 + count]
     gots = refs[4 + count : 4 + 2 * count]
-    s_scr = refs[4 + 2 * count]
-    copies = start_sends(sends, gots, *refs[5 + 2 * count :], shards)
-    attend_body(qt_ref, k_ref, vt_ref, o_ref, s_scr, inv_root)
+    rest = refs[4 + 2 * count :]
+    if stream:
+        back_ref = rest[0]
+        rest = rest[1:]
+    s_scr = rest[0]
+    copies = start_sends(sends, gots, *rest[1:4], shards)
+    after_block = None
+    if stream:
+        block_send, block_recv, block_local = rest[4:7]
+        me = lax.axis_index("ctx")
+        region = lax.axis_index("region")
+
+        def remote_block(b):
+            return pltpu.make_async_remote_copy(
+                src_ref=o_ref.at[b],
+                dst_ref=back_ref.at[me],
+                send_sem=block_send.at[b],
+                recv_sem=block_recv.at[me],
+                device_id=(region, b),
+                device_id_type=pl.DeviceIdType.MESH,
+            )
+
+        def local_block(b):
+            return pltpu.make_async_copy(o_ref.at[b], back_ref.at[b], block_local.at[0])
+
+        def after_block(b):
+            @pl.when(b == me)
+            def _():
+                local_block(b).start()
+
+            @pl.when(b != me)
+            def _():
+                remote_block(b).start()
+
+    attend_body(qt_ref, k_ref, vt_ref, o_ref, s_scr, inv_root, after_block)
     for copy in copies:
         copy.wait()
-
-
-def attend_send(q_t, k_tok, v_t, sends, shards, inv_root, collective_id):
+    if stream:
+        for b in range(shards):
+            @pl.when(b == me)
+            def _():
+                local_block(b).wait()
+
+            @pl.when(b != me)
+            def _():
+                remote_block(b).wait_send()
+                pltpu.make_async_remote_copy(
+                    src_ref=o_ref.at[b],
+                    dst_ref=back_ref.at[b],
+                    send_sem=block_send.at[b],
+                    recv_sem=block_recv.at[b],
+                    device_id=(region, b),
+                    device_id_type=pl.DeviceIdType.MESH,
+                ).wait_recv()
+
+
+def attend_send(q_t, k_tok, v_t, sends, shards, inv_root, collective_id, stream=False):
     blocks, head_dim, rows = q_t.shape
     count = len(sends)
     kernel = functools.partial(
-        attend_send_kernel, count=count, shards=shards, inv_root=inv_root
+        attend_send_kernel, count=count, shards=shards, inv_root=inv_root, stream=stream
     )
     any_spec = pl.BlockSpec(memory_space=pl.ANY)
     vmem_spec = pl.BlockSpec(memory_space=pltpu.VMEM)
+    out_shape = [jax.ShapeDtypeStruct(q_t.shape, jnp.bfloat16)]
+    out_shape += [jax.ShapeDtypeStruct(x.shape, x.dtype) for x in sends]
+    out_specs = [vmem_spec] + [any_spec] * count
+    scratch = [pltpu.VMEM((blocks, rows, rows), jnp.float32)] + send_scratch(count, shards)
+    if stream:
+        out_shape.append(jax.ShapeDtypeStruct(q_t.shape, jnp.bfloat16))
+        out_specs.append(any_spec)
+        scratch += [
+            pltpu.SemaphoreType.DMA((shards,)),
+            pltpu.SemaphoreType.DMA((shards,)),
+            pltpu.SemaphoreType.DMA((1,)),
+        ]
     outs = pl.pallas_call(
         kernel,
-        out_shape=[jax.ShapeDtypeStruct(q_t.shape, jnp.bfloat16)]
-        + [jax.ShapeDtypeStruct(x.shape, x.dtype) for x in sends],
+        out_shape=out_shape,
         in_specs=[vmem_spec] * 3 + [any_spec] * count,
-        out_specs=[vmem_spec] + [any_spec] * count,
-        scratch_shapes=[pltpu.VMEM((blocks, rows, rows), jnp.float32)]
-        + send_scratch(count, shards),
+        out_specs=out_specs,
+        scratch_shapes=scratch,
         compiler_params=pltpu.CompilerParams(
             collective_id=collective_id,
             has_side_effects=True,
@@ -165,19 +226,17 @@
     got = exchange([q_all[0], k_all[0], v_all[0]], shards, 0)
     backs = []
     for h in range(pair):
-        if h + 1 < pair:
-            sends = [q_all[h + 1], k_all[h + 1], v_all[h + 1]]
-        else:
-            sends = []
+        last = h + 1 == pair
+        sends = [] if last else [q_all[h + 1], k_all[h + 1], v_all[h + 1]]
         if h > 0:
             sends = sends + [out_prev]
-        out_prev, sent = attend_send(*got, sends, shards, inverse_root, 1 + h)
-        if h + 1 < pair:
+        out_prev, sent = attend_send(
+            *got, sends, shards, inverse_root, 1 + h, stream=last
+        )
+        if not last:
             got = sent[:3]
             sent = sent[3:]
         backs.extend(sent)
-    (last_back,) = exchange([out_prev], shards, 1 + pair)
-    backs.append(last_back)
     return jnp.stack(backs, axis=1)
 
 

time: 223 us -> 217 us (0.973)
  Pallas kernels: 102 us -> 95.2 us
    pallas_call x2 -> x1, Pallas kernels: 37.6 us -> 28 us  [exchange(): pl.pallas_call(kernel, out_shape=[jax.ShapeDtypeStruct(x.shape, x.dtype)...]
    pallas_call x2, Pallas kernels: 64.2 us -> 67.3 us  [attend_send(): pl.pallas_call(kernel, out_shape=out_shape, in_specs=[vmem_spec] * 3 + [a...]
where the time goes in v6:
time: 217 us; the launch traced here: 214 us
  Pallas kernels  95.2 us (44%)
  local copies, waits for them, and re-layouts  44.8 us (21%)
  matrix products  24.4 us (11%)
  blocking collectives  20.5 us (9%)
  waiting for transfers between devices  13.5 us (6%)
  other arithmetic  8.71 us (4%)
  starting transfers between devices  5.9 us (3%)
    pallas_call x2, Pallas kernels, attend_send(): pl.pallas_call(kernel, out_shape=out_shape, in_specs=[vmem_spec] * 3 + [a...  67.3 us
    pallas_call x1, Pallas kernels, exchange(): pl.pallas_call(kernel, out_shape=[jax.ShapeDtypeStruct(x.shape, x.dtype)...  28 us
    all_to_all x1, blocking collectives, per_device(): lax.all_to_all(requests.reshape(owners, capacity), ('region', 'ctx'), spl...  20.5 us
    unnamed x41, local copies, waits for them, and re-layouts  18.6 us
    all_to_all x1, waiting for transfers between devices, per_device(): lax.all_to_all(served, ('region', 'ctx'), split_axis=0, concat_axis=0, ti...  13.5 us
    unnamed x6, matrix products  11.8 us
    dot_general x1, matrix products, per_device(): jnp.dot(activated, w_ada, preferred_element_type=jnp.float32) + b_ada  8.01 us
    all_to_all x1, starting transfers between devices, per_device(): lax.all_to_all(served, ('region', 'ctx'), split_axis=0, concat_axis=0, ti...  5.9 us
  transfers between devices with their start and end apart: 1, of which 1 were waited for; matrix products, arithmetic and copies ran while one was open for 9% of the time, Pallas kernels for 0%

profile of v6, /device:TPU:0, one launch (start us, length us, event | category | flops | bytes accessed | tf_op | source)
XLA Modules:
  0.0 214.0 jit_solution(13421060322053300344)
XLA Ops:
  1.6 3.5 %gather_fusion = s32[512]{0:T(512)S(1)} fusion(s32[16384]{0:T(1024)} %param.11, s32[1024]{0:T(1024)S(1)} %pad_clamp_fusion.1), kind=kCustom, calls=%fused_computation | custom fusion | bytes 6144 | tf_op jit(solution)/shard_map/gather | solution.py:252
  5.4 2.4 %scatter_custom_fusion = s32[1024]{0:T(1024)S(1)} fusion(s32[512]{0:T(512)S(1)} %bitcast.137, s32[512]{0:T(512)S(1)} %get-tuple-element.31, s32[]{:T(128)} %constant.24.clone.1), kind=kCustom, calls=%fused_computation.62 | custom fusion | bytes 4100 | tf_op jit(solution)/shard_map/scatter | solution.py:264
  8.0 20.5 %all_to_all.14 = s32[128,1,8]{2,1,0:T(1,128)S(1)} all-to-all(s32[128,1,8]{2,1,0:T(1,128)S(1)} %bitcast.131), channel_id=1, replica_groups=mesh['region'=16,'ctx'=8] {'region','ctx'}, dimensions={0} | all-to-all | bytes 8192 | tf_op jit(solution)/shard_map/all_to_all | solution.py:265
  29.9 5.4 %gather_fusion.1 = bf16[1024,1152]{1,0:T(8,128)(2,1)} fusion(bf16[128,1152]{1,0:T(8,128)(2,1)S(1)} %copy-done.5, s32[1024]{0:T(1024)S(1)} %broadcast_clamp_fusion), kind=kCustom, calls=%fused_computation.1 | custom fusion | bytes 4722688 | tf_op jit(solution)/shard_map/gather | solution.py:273
  35.4 5.9 %all-to-all-start.1 = ((bf16[128,8,1152]{2,1,0:T(8,128)(2,1)}), bf16[128,8,1152]{2,1,0:T(8,128)(2,1)}, u32[]{:S(2)}, u32[]{:S(2)}) async-start(bf16[128,8,1152]{2,1,0:T(8,128)(2,1)} %bitcast.116), calls=%async_computation.1 | async-start | bytes 4718592 | tf_op jit(solution)/shard_map/all_to_all | solution.py:274
  41.3 11.5 %copy.46 = bf16[1152,3456]{0,1:T(8,128)(2,1)} copy(bf16[1152,3456]{1,0:T(8,128)(2,1)} %param.16) | data formatting | bytes 15925248 | tf_op args[7]
  52.8 1.6 convert_reduce_fusion
  54.9 5.8 %fusion.33 = (bf16[1152,1,8,1,72]{0,4,3,2,1:T(8,128)(2,1)}, bf16[1152,1,8,1,72]{0,4,3,2,1:T(8,128)(2,1)}, bf16[1152,1,8,1,72]{0,4,3,2,1:T(8,128)(2,1)}, bf16[115...) fusion(bf16[1152,3,8,2,72]{0,4,3,2,1:T(8,128)(2,1)} %bitcast.115), kind=kLoop, calls=%fused_computation.71 | loop fusion | bytes 15925248 | tf_op jit(solution)/shard_map/slice | solution.py:291
  60.7 13.5 %all-to-all-done.1 = bf16[128,8,1152]{2,1,0:T(8,128)(2,1)} async-done(((bf16[128,8,1152]{2,1,0:T(8,128)(2,1)}), bf16[128,8,1152]{2,1,0:T(8,128)(2,1)}, u32[]{:S(2)}, u32[]{:S(2)}) %all-to-all-start.1) | async-done | bytes 2359328 | tf_op jit(solution)/shard_map/all_to_all | solution.py:274
  74.2 5.7 %gather_fusion.2 = bf16[512,1152]{1,0:T(8,128)(2,1)} fusion(bf16[1024,1152]{1,0:T(8,128)(2,1)} %bitcast.10, s32[1024]{0:T(1024)S(1)} %pad_clamp_fusion), kind=kCustom, calls=%fused_computation.2 | custom fusion | bytes 2361344 | tf_op jit(solution)/shard_map/gather | solution.py:275
  79.8 8.0 %fusion = f32[512,3456]{1,0:T(8,128)S(1)} fusion(bf16[1152,3456]{1,0:T(8,128)(2,1)} %param.14, f32[3456]{0:T(1024)S(1)} %copy-done.19, bf16[512,1152]{1,0:T(8,128)(2,1)} %gather_fusion.2, pred[512]{0:T(512)(128)(4,1)S(1)} %iota_compare_fusion.1), kind=kOutput, calls=%fused_computation.5 | convolution fusion | flops 4086300672 | bytes 16234496 | tf_op jit(solution)/shard_map/dot_general | solution.py:279
  88.5 2.2 %copy-done.9 = f32[512,3456]{1,0:T(8,128)} copy-done((f32[512,3456]{1,0:T(8,128)}, f32[512,3456]{1,0:T(8,128)S(1)}, u32[]{:S(2)}) %copy-start.9) | copy-done | bytes 7077912
  90.8 2.0 fusion.39
  93.8 1.3 copy.53
  95.1 3.9 %fusion.37 = f32[512,576]{0,1} fusion(bf16[512,1152]{1,0:T(8,128)(2,1)} %copy-done.17, bf16[1152,576]{0,1:T(8,128)(2,1)} %bitcast.122), kind=kOutput, calls=%fused_computation.75 | convolution fusion | flops 679477248 | bytes 3686400
  99.0 2.0 fusion.36
  102.3 2.0 fusion.34
  104.4 1.3 copy.49
  105.7 2.8 %convert_bitcast_fusion.1 = (bf16[8,72,512]{2,1,0:T(8,128)(2,1)S(1)}, bf16[8,72,512]{2,1,0:T(8,128)(2,1)}) fusion(f32[512,8,72]{0,2,1:T(8,128)} %bitcast.125, f32[512,8,72]{0,2,1:T(8,128)} %bitcast.127), kind=kLoop, calls=%fused_computation.39 | loop fusion | flops 589824 | bytes 3538944 | tf_op jit(solution)/shard_map/convert_element_type | solution.py:292
  109.7 28.0 %shard_map.91 = (bf16[8,72,512]{2,1,0:T(8,128)(2,1)}, bf16[8,512,72]{2,1,0:T(8,128)(2,1)}, bf16[8,72,512]{2,1,0:T(8,128)(2,1)}) custom-call(bf16[8,72,512]{2,1,0:T(8,128)(2,1)} %get-tuple-element.34.refs_0_, bf16[8,512,72]{2,1,0:T(8,128)(2,1)} %bitcast.118, bf16[8,72,512]{2,1,0:T(8,128)(2,1)} %get-tuple-element.33.refs_2_), custom_call_target="tpu_custom_call" | custom-call | tf_op jit(solution)/shard_map/pallas_call | solution.py:74
  138.7 1.2 copy-done.2
  142.1 32.2 %shard_map.92 = (bf16[8,72,512]{2,1,0:T(8,128)(2,1)S(1)}, bf16[8,72,512]{2,1,0:T(8,128)(2,1)S(1)}, bf16[8,512,72]{2,1,0:T(8,128)(2,1)S(1)}, bf16[8,72,512]{2,1,0:T(8,128)(2,1)S(1)}) custom-call(bf16[8,72,512]{2,1,0:T(8,128)(2,1)S(1)} %copy-done.3, bf16[8,512,72]{2,1,0:T(8,128)(2,1)S(1)} %copy-done.2, bf16[8,72,512]{2,1,0:T(8,128)(2,1)S(1)} %copy-done.4, ...), custom_call_target="tpu_custom_call" | custom-call | tf_op jit(solution)/shard_map/pallas_call | solution.py:209
  174.3 35.1 %shard_map.93 = (bf16[8,72,512]{2,1,0:T(8,128)(2,1)}, bf16[8,72,512]{2,1,0:T(8,128)(2,1)S(1)}, bf16[8,72,512]{2,1,0:T(8,128)(2,1)S(1)}) custom-call(bf16[8,72,512]{2,1,0:T(8,128)(2,1)S(1)} %get-tuple-element.17.refs_0_, bf16[8,512,72]{2,1,0:T(8,128)(2,1)S(1)} %get-tuple-element.18.refs_1_, bf16[8,72,512]{2,1,0:T(8,128)(2,1)S(1)} %get-tuple-element.19.refs_2_, ...), custom_call_target="tpu_custom_call" | custom-call | tf_op jit(solution)/shard_map/pallas_call | solution.py:209
  209.4 4.6 %fusion.7 = bf16[1,512,1152]{2,1,0:T(8,128)(2,1)} fusion(bf16[1,512,1152]{2,1,0:T(8,128)(2,1)S(1)} %copy-done.8, bf16[8,2,72,1152]{3,2,1,0:T(8,128)(2,1)S(1)} %bitcast.112, f32[512,3456]{1,0:T(8,128)} %copy-done.9, bf16[8,1,72,512]{3,2,0,1:T(8,128)(2,1)S(1)} %bitcast.114, bf16[8,1,72,512]{3,2,0,1:T(8,128)(2,1)S(1)} %bitcast.113), kind=kOutput, calls=%fused_computation.17 | convolution fusion | flops 1361903616 | bytes 8552448 | tf_op jit(solution)/shard_map/phet,pheD->tD/dot_general | solution.py:299
  (61 shorter events, 10.5 us)
Async XLA Ops:
  0.0 209.4 %copy-start = (bf16[1152,1152]{1,0:T(8,128)(2,1)S(1)}, bf16[1152,1152]{1,0:T(8,128)(2,1)}, u32[]{:S(2)}) copy-start(bf16[1152,1152]{1,0:T(8,128)(2,1)} %param.17) | copy-start | bytes 7962628
  0.0 29.9 %copy-start.5 = (bf16[128,1152]{1,0:T(8,128)(2,1)S(1)}, bf16[128,1152]{1,0:T(8,128)(2,1)}, u32[]{:S(2)}) copy-start(bf16[128,1152]{1,0:T(8,128)(2,1)} %param.13) | copy-start | bytes 884740
  35.4 38.8 %all-to-all-start.1 = ((bf16[128,8,1152]{2,1,0:T(8,128)(2,1)}), bf16[128,8,1152]{2,1,0:T(8,128)(2,1)}, u32[]{:S(2)}, u32[]{:S(2)}) async-start(bf16[128,8,1152]{2,1,0:T(8,128)(2,1)} %bitcast.116), calls=%async_computation.1 | async-start | bytes 4718592 | tf_op jit(solution)/shard_map/all_to_all | solution.py:274
  52.8 1.6 copy-start.6
  74.1 5.7 %copy-start.19 = (f32[3456]{0:T(1024)S(1)}, f32[3456]{0:T(1024)}, u32[]{:S(2)}) copy-start(f32[3456]{0:T(1024)} %param.15) | copy-start | bytes 41476
  79.8 8.0 %copy-start.7 = (bf16[1,512,1152]{2,1,0:T(8,128)(2,1)S(1)}, bf16[1,512,1152]{2,1,0:T(8,128)(2,1)}, u32[]{:S(2)}) copy-start(bf16[1,512,1152]{2,1,0:T(8,128)(2,1)} %param.9) | copy-start | bytes 3538948
  87.9 2.9 %copy-start.9 = (f32[512,3456]{1,0:T(8,128)}, f32[512,3456]{1,0:T(8,128)S(1)}, u32[]{:S(2)}) copy-start(f32[512,3456]{1,0:T(8,128)S(1)} %fusion) | copy-start | bytes 21233668
  87.9 2.9 %copy-start.14 = (bf16[1152,1,8,1,72]{0,4,3,2,1:T(8,128)(2,1)S(1)}, bf16[1152,1,8,1,72]{0,4,3,2,1:T(8,128)(2,1)}, u32[]{:S(2)}) copy-start(bf16[1152,1,8,1,72]{0,4,3,2,1:T(8,128)(2,1)} %get-tuple-element.25) | copy-start | bytes 3981316
  90.8 2.0 copy-start.17
  90.8 2.0 copy-start.13
  95.1 3.9 %copy-start.12 = (bf16[1152,1,8,1,72]{0,4,3,2,1:T(8,128)(2,1)S(1)}, bf16[1152,1,8,1,72]{0,4,3,2,1:T(8,128)(2,1)}, u32[]{:S(2)}) copy-start(bf16[1152,1,8,1,72]{0,4,3,2,1:T(8,128)(2,1)} %get-tuple-element.28) | copy-start | bytes 3981316
  95.1 3.9 %copy-start.18 = (bf16[512,1152]{1,0:T(8,128)(2,1)S(1)}, bf16[512,1152]{1,0:T(8,128)(2,1)}, u32[]{:S(2)}) copy-start(bf16[512,1152]{1,0:T(8,128)(2,1)} %copy-done.17) | copy-start | bytes 3538948
  99.0 2.0 copy-start.11
  101.0 1.3 copy-start.10
  105.7 2.8 %copy-start.15 = (f32[512,576]{0,1:S(1)}, f32[512,576]{0,1}, u32[]{:S(2)}) copy-start(f32[512,576]{0,1} %fusion.36) | copy-start | bytes 3538948
  105.7 2.8 %copy-start.16 = (f32[512,576]{0,1:S(1)}, f32[512,576]{0,1}, u32[]{:S(2)}) copy-start(f32[512,576]{0,1} %fusion.34) | copy-start | bytes 3538948
  137.7 1.1 copy-start.1
  138.7 1.2 copy-start.2
  140.0 1.1 copy-start.3
  141.0 1.1 copy-start.4
  174.2 35.1 %copy-start.8 = (bf16[1,512,1152]{2,1,0:T(8,128)(2,1)S(1)}, bf16[1,512,1152]{2,1,0:T(8,128)(2,1)}, u32[]{:S(2)}) copy-start(bf16[1,512,1152]{2,1,0:T(8,128)(2,1)} %param.9) | copy-start | bytes 3538948

commit v7 on v6

--- a/solution.py
+++ b/solution.py
@@ -221,13 +221,67 @@
     return outs[0], outs[1:]
 
 
-def head_pipeline(q_all, k_all, v_all, shards, inverse_root):
-    pair = len(q_all)
-    got = exchange([q_all[0], k_all[0], v_all[0]], shards, 0)
+def project_kernel(mod_ref, w_ref, *refs, shards, pair, head_dim):
+    got0 = refs[:3]
+    later = refs[3 : 3 * pair]
+    send0 = refs[3 * pair : 3 * pair + 3]
+    sems = refs[3 * pair + 3 :]
+    modulated = mod_ref[...]
+
+    def fill(h, dests):
+        for i in range(3):
+            out_t = lax.dot_general(
+                w_ref[i, h],
+                modulated,
+                (((1,), (1,)), ((), ())),
+                preferred_element_type=jnp.float32,
+            )
+            for p in range(shards):
+                piece = out_t[p * head_dim : (p + 1) * head_dim]
+                if i == 1:
+                    piece = piece.T
+                dests[i][p] = piece.astype(jnp.bfloat16)
+
+    fill(0, send0)
+    copies = start_sends(send0, got0, *sems, shards)
+    for h in range(1, pair):
+        fill(h, later[3 * (h - 1) : 3 * h])
+    for copy in copies:
+        copy.wait()
+
+
+def project_send(modulated, w_t, shards, pair, head_dim):
+    rows, width = modulated.shape
+    q_shape = jax.ShapeDtypeStruct((shards, head_dim, rows), jnp.bfloat16)
+    k_shape = jax.ShapeDtypeStruct((shards, rows, head_dim), jnp.bfloat16)
+    shapes = [q_shape, k_shape, q_shape]
+    kernel = functools.partial(
+        project_kernel, shards=shards, pair=pair, head_dim=head_dim
+    )
+    any_spec = pl.BlockSpec(memory_space=pl.ANY)
+    vmem_spec = pl.BlockSpec(memory_space=pltpu.VMEM)
+    outs = pl.pallas_call(
+        kernel,
+        out_shape=shapes * pair,
+        in_specs=[vmem_spec, vmem_spec],
+        out_specs=[any_spec] * 3 + [vmem_spec] * (3 * (pair - 1)),
+        scratch_shapes=[pltpu.VMEM(x.shape, x.dtype) for x in shapes]
+        + send_scratch(3, shards),
+        compiler_params=pltpu.CompilerParams(
+            collective_id=pair + 1,
+            has_side_effects=True,
+            vmem_limit_bytes=48 * 1024 * 1024,
+        ),
+    )(modulated, w_t)
+    return outs[:3], [outs[3 * h : 3 * h + 3] for h in range(1, pair)]
+
+
+def head_pipeline(modulated, w_t, shards, pair, head_dim, inverse_root):
+    got, later = project_send(modulated, w_t, shards, pair, head_dim)
     backs = []
     for h in range(pair):
         last = h + 1 == pair
-        sends = [] if last else [q_all[h + 1], k_all[h + 1], v_all[h + 1]]
+        sends = [] if last else list(later[h])
         if h > 0:
             sends = sends + [out_prev]
         out_prev, sent = attend_send(
@@ -285,16 +339,12 @@
     head_dim = width // HEADS
     pair = HEADS // shards
     inverse_root = 1.0 / math.sqrt(head_dim)
-    w_parts = w_qkv.reshape(width, 3, shards, pair, head_dim)
-    def project(i, h, pattern):
-        return jnp.einsum(
-            pattern, modulated, w_parts[:, i, :, h], preferred_element_type=jnp.float32
-        ).astype(jnp.bfloat16)
-
-    q_all = [project(0, h, "td,dpe->pet") for h in range(pair)]
-    k_all = [project(1, h, "td,dpe->pte") for h in range(pair)]
-    v_all = [project(2, h, "td,dpe->pet") for h in range(pair)]
-    backs = head_pipeline(q_all, k_all, v_all, shards, inverse_root)
+    w_t = (
+        w_qkv.reshape(width, 3, shards, pair, head_dim)
+        .transpose(1, 3, 2, 4, 0)
+        .reshape(3, pair, shards * head_dim, width)
+    )
+    backs = head_pipeline(modulated, w_t, shards, pair, head_dim, inverse_root)
     w_out_parts = w_out.reshape(shards, pair, head_dim, width)
     projected = jnp.einsum(
         "phet,pheD->tD",

time: 217 us -> 200 us (0.922)
  matrix products: 24.4 us -> 12.6 us
  Pallas kernels: 95.2 us -> 101 us
  other arithmetic: 8.71 us -> 3.23 us
  local copies, waits for them, and re-layouts: 44.8 us -> 39.8 us
    unnamed x6 -> x0, matrix products: 11.8 us -> none
    transpose x0 -> x1, local copies, waits for them, and re-layouts: none -> 7.21 us  [per_device(): w_t = w_qkv.reshape(width, 3, shards, pair, head_dim).transpose(1, 3, 2,...]
    slice x1 -> x0, local copies, waits for them, and re-layouts: 5.81 us -> none  [project(): w_parts[:, i, :, h]]
    pallas_call x1, Pallas kernels: 28 us -> 33.8 us  [project_send(): pl.pallas_call(kernel, out_shape=shapes * pair, in_specs=[vmem_spec, vmem...]
    convert_element_type x4 -> x0, other arithmetic: 4.13 us -> none  [project(): return jnp.einsum(pattern, modulated, w_parts[:, i, :, h], preferred_elem...]
    unnamed x41 -> x15, local copies, waits for them, and re-layouts: 18.6 us -> 14.8 us
    convert_element_type x2 -> x0, local copies, waits for them, and re-layouts: 2.6 us -> none  [project(): return jnp.einsum(pattern, modulated, w_parts[:, i, :, h], preferred_elem...]
  transfers between devices with their start and end apart: 1 -> 1, of which waited for: 1 -> 1; matrix products, arithmetic and copies ran while one was open for 9% -> 10% of each run, Pallas kernels for 0% -> 0%
where the time goes in v7:
time: 200 us; the launch traced here: 197 us
  Pallas kernels  101 us (50%)
  local copies, waits for them, and re-layouts  39.8 us (20%)
  blocking collectives  20.5 us (10%)
  waiting for transfers between devices  13.5 us (7%)
  matrix products  12.6 us (6%)
  starting transfers between devices  5.9 us (3%)
  other arithmetic  3.23 us (2%)
    pallas_call x2, Pallas kernels, attend_send(): pl.pallas_call(kernel, out_shape=out_shape, in_specs=[vmem_spec] * 3 + [a...  67.1 us
    pallas_call x1, Pallas kernels, project_send(): pl.pallas_call(kernel, out_shape=shapes * pair, in_specs=[vmem_spec, vmem...  33.8 us
    all_to_all x1, blocking collectives, per_device(): lax.all_to_all(requests.reshape(owners, capacity), ('region', 'ctx'), spl...  20.5 us
    unnamed x15, local copies, waits for them, and re-layouts  14.8 us
    all_to_all x1, waiting for transfers between devices, per_device(): lax.all_to_all(served, ('region', 'ctx'), split_axis=0, concat_axis=0, ti...  13.5 us
    dot_general x1, matrix products, per_device(): jnp.dot(activated, w_ada, preferred_element_type=jnp.float32) + b_ada  8.01 us
    transpose x1, local copies, waits for them, and re-layouts, per_device(): w_t = w_qkv.reshape(width, 3, shards, pair, head_dim).transpose(1, 3, 2,...  7.21 us
    all_to_all x1, starting transfers between devices, per_device(): lax.all_to_all(served, ('region', 'ctx'), split_axis=0, concat_axis=0, ti...  5.9 us
  transfers between devices with their start and end apart: 1, of which 1 were waited for; matrix products, arithmetic and copies ran while one was open for 10% of the time, Pallas kernels for 0%

profile of v7, /device:TPU:0, one launch (start us, length us, event | category | flops | bytes accessed | tf_op | source)
XLA Modules:
  0.0 197.3 jit_solution(14535740840294043945)
XLA Ops:
  0.8 0.8 compare_select_fusion.3
  1.6 3.5 %gather_fusion = s32[512]{0:T(512)S(1)} fusion(s32[16384]{0:T(1024)} %param.11, s32[1024]{0:T(1024)S(1)} %pad_clamp_fusion.1), kind=kCustom, calls=%fused_computation | custom fusion | bytes 6144 | tf_op jit(solution)/shard_map/gather | solution.py:306
  5.1 0.3 convert_reduce_fusion.1
  5.4 2.4 %scatter_custom_fusion = s32[1024]{0:T(1024)S(1)} fusion(s32[512]{0:T(512)S(1)} %bitcast.69, s32[512]{0:T(512)S(1)} %get-tuple-element.31, s32[]{:T(128)} %constant.24.clone.1), kind=kCustom, calls=%fused_computation.58 | custom fusion | bytes 4100 | tf_op jit(solution)/shard_map/scatter | solution.py:318
  8.0 20.5 %all_to_all.14 = s32[128,1,8]{2,1,0:T(1,128)S(1)} all-to-all(s32[128,1,8]{2,1,0:T(1,128)S(1)} %bitcast.63), channel_id=1, replica_groups=mesh['region'=16,'ctx'=8] {'region','ctx'}, dimensions={0} | all-to-all | bytes 8192 | tf_op jit(solution)/shard_map/all_to_all | solution.py:319
  28.5 0.5 broadcast.299
  29.0 0.8 reduce.4
  29.8 0.1 reshape.217
  29.9 5.5 %gather_fusion.1 = bf16[1024,1152]{1,0:T(8,128)(2,1)} fusion(bf16[128,1152]{1,0:T(8,128)(2,1)S(1)} %copy-done.2, s32[1024]{0:T(1024)S(1)} %broadcast_clamp_fusion), kind=kCustom, calls=%fused_computation.1 | custom fusion | bytes 4722688 | tf_op jit(solution)/shard_map/gather | solution.py:327
  35.4 5.9 %all-to-all-start.1 = ((bf16[128,8,1152]{2,1,0:T(8,128)(2,1)}), bf16[128,8,1152]{2,1,0:T(8,128)(2,1)}, u32[]{:S(2)}, u32[]{:S(2)}) async-start(bf16[128,8,1152]{2,1,0:T(8,128)(2,1)} %bitcast.62), calls=%async_computation.1 | async-start | bytes 4718592 | tf_op jit(solution)/shard_map/all_to_all | solution.py:328
  41.3 11.5 %copy.20 = bf16[1152,3456]{0,1:T(8,128)(2,1)} copy(bf16[1152,3456]{1,0:T(8,128)(2,1)} %param.16) | data formatting | bytes 15925248 | tf_op args[7]
  52.8 7.2 %copy.21 = bf16[3,2,8,72,1152]{4,3,2,1,0:T(8,128)(2,1)} copy(bf16[3,2,8,72,1152]{4,3,1,2,0:T(8,128)(2,1)} %bitcast.61) | data formatting | bytes 15925248 | tf_op jit(solution)/shard_map/transpose | solution.py:344
  60.0 0.2 convert_reduce_fusion
  60.2 0.5 fusion.9
  60.7 13.5 %all-to-all-done.1 = bf16[128,8,1152]{2,1,0:T(8,128)(2,1)} async-done(((bf16[128,8,1152]{2,1,0:T(8,128)(2,1)}), bf16[128,8,1152]{2,1,0:T(8,128)(2,1)}, u32[]{:S(2)}, u32[]{:S(2)}) %all-to-all-start.1) | async-done | bytes 2359328 | tf_op jit(solution)/shard_map/all_to_all | solution.py:328
  74.2 5.7 %gather_fusion.2 = bf16[512,1152]{1,0:T(8,128)(2,1)} fusion(bf16[1024,1152]{1,0:T(8,128)(2,1)} %bitcast.10, s32[1024]{0:T(1024)S(1)} %pad_clamp_fusion), kind=kCustom, calls=%fused_computation.2 | custom fusion | bytes 2361344 | tf_op jit(solution)/shard_map/gather | solution.py:329
  79.9 8.0 %fusion = f32[512,3456]{1,0:T(8,128)S(1)} fusion(bf16[1152,3456]{1,0:T(8,128)(2,1)} %param.14, f32[3456]{0:T(1024)S(1)} %copy-done.6, bf16[512,1152]{1,0:T(8,128)(2,1)} %gather_fusion.2, pred[512]{0:T(512)(128)(4,1)S(1)} %iota_compare_fusion.1), kind=kOutput, calls=%fused_computation.5 | convolution fusion | flops 4086300672 | bytes 16234496 | tf_op jit(solution)/shard_map/dot_general | solution.py:333
  87.9 0.6 fusion.12.mod_ref
  88.5 2.3 %copy-done.5 = f32[512,3456]{1,0:T(8,128)} copy-done((f32[512,3456]{1,0:T(8,128)}, f32[512,3456]{1,0:T(8,128)S(1)}, u32[]{:S(2)}) %copy-start.5) | copy-done | bytes 7077912
  90.8 33.8 %shard_map.91 = (bf16[8,72,512]{2,1,0:T(8,128)(2,1)S(1)}, bf16[8,512,72]{2,1,0:T(8,128)(2,1)S(1)}, bf16[8,72,512]{2,1,0:T(8,128)(2,1)S(1)}, bf16[8,72,512]{2,1,0...) custom-call(bf16[512,1152]{1,0:T(8,128)(2,1)S(1)} %fusion.12.mod_ref, ...), custom_call_target="tpu_custom_call" | custom-call | tf_op jit(solution)/shard_map/pallas_call | solution.py:263
  124.6 1.0 copy-done.1
  125.6 32.2 %shard_map.92 = (bf16[8,72,512]{2,1,0:T(8,128)(2,1)S(1)}, bf16[8,72,512]{2,1,0:T(8,128)(2,1)S(1)}, bf16[8,512,72]{2,1,0:T(8,128)(2,1)S(1)}, bf16[8,72,512]{2,1,0:T(8,128)(2,1)S(1)}) custom-call(bf16[8,72,512]{2,1,0:T(8,128)(2,1)S(1)} %get-tuple-element.17.refs_0_, bf16[8,512,72]{2,1,0:T(8,128)(2,1)S(1)} %get-tuple-element.18.refs_1_, ...), custom_call_target="tpu_custom_call" | custom-call | tf_op jit(solution)/shard_map/pallas_call | solution.py:209
  157.8 34.9 %shard_map.93 = (bf16[8,72,512]{2,1,0:T(8,128)(2,1)}, bf16[8,72,512]{2,1,0:T(8,128)(2,1)S(1)}, bf16[8,72,512]{2,1,0:T(8,128)(2,1)S(1)}) custom-call(bf16[8,72,512]{2,1,0:T(8,128)(2,1)S(1)} %get-tuple-element.23.refs_0_, bf16[8,512,72]{2,1,0:T(8,128)(2,1)S(1)} %get-tuple-element.24.refs_1_, bf16[8,72,512]{2,1,0:T(8,128)(2,1)S(1)} %get-tuple-element.25.refs_2_, ...), custom_call_target="tpu_custom_call" | custom-call | tf_op jit(solution)/shard_map/pallas_call | solution.py:209
  192.7 4.6 %fusion.7 = bf16[1,512,1152]{2,1,0:T(8,128)(2,1)} fusion(bf16[1,512,1152]{2,1,0:T(8,128)(2,1)S(1)} %copy-done.4, bf16[8,2,72,1152]{3,2,1,0:T(8,128)(2,1)S(1)} %bitcast.57, f32[512,3456]{1,0:T(8,128)} %copy-done.5, bf16[8,1,72,512]{3,2,0,1:T(8,128)(2,1)S(1)} %bitcast.59, bf16[8,1,72,512]{3,2,0,1:T(8,128)(2,1)S(1)} %bitcast.58), kind=kOutput, calls=%fused_computation.17 | convolution fusion | flops 1361903616 | bytes 8552448 | tf_op jit(solution)/shard_map/phet,pheD->tD/dot_general | solution.py:349
  (23 shorter events, 0.2 us)
Async XLA Ops:
  0.0 192.7 %copy-start = (bf16[1152,1152]{1,0:T(8,128)(2,1)S(1)}, bf16[1152,1152]{1,0:T(8,128)(2,1)}, u32[]{:S(2)}) copy-start(bf16[1152,1152]{1,0:T(8,128)(2,1)} %param.17) | copy-start | bytes 7962628
  0.0 29.9 %copy-start.2 = (bf16[128,1152]{1,0:T(8,128)(2,1)S(1)}, bf16[128,1152]{1,0:T(8,128)(2,1)}, u32[]{:S(2)}) copy-start(bf16[128,1152]{1,0:T(8,128)(2,1)} %param.13) | copy-start | bytes 884740
  35.4 38.8 %all-to-all-start.1 = ((bf16[128,8,1152]{2,1,0:T(8,128)(2,1)}), bf16[128,8,1152]{2,1,0:T(8,128)(2,1)}, u32[]{:S(2)}, u32[]{:S(2)}) async-start(bf16[128,8,1152]{2,1,0:T(8,128)(2,1)} %bitcast.62), calls=%async_computation.1 | async-start | bytes 4718592 | tf_op jit(solution)/shard_map/all_to_all | solution.py:328
  52.8 7.2 %copy-start.3 = (bf16[1,512,1152]{2,1,0:T(8,128)(2,1)S(1)}, bf16[1,512,1152]{2,1,0:T(8,128)(2,1)}, u32[]{:S(2)}) copy-start(bf16[1,512,1152]{2,1,0:T(8,128)(2,1)} %param.9) | copy-start | bytes 3538948
  74.2 5.7 %copy-start.6 = (f32[3456]{0:T(1024)S(1)}, f32[3456]{0:T(1024)}, u32[]{:S(2)}) copy-start(f32[3456]{0:T(1024)} %param.15) | copy-start | bytes 41476
  79.9 8.0 %copy-start.4 = (bf16[1,512,1152]{2,1,0:T(8,128)(2,1)S(1)}, bf16[1,512,1152]{2,1,0:T(8,128)(2,1)}, u32[]{:S(2)}) copy-start(bf16[1,512,1152]{2,1,0:T(8,128)(2,1)} %param.9) | copy-start | bytes 3538948
  87.9 2.9 %copy-start.5 = (f32[512,3456]{1,0:T(8,128)}, f32[512,3456]{1,0:T(8,128)S(1)}, u32[]{:S(2)}) copy-start(f32[512,3456]{1,0:T(8,128)S(1)} %fusion) | copy-start | bytes 21233668
  124.6 1.0 copy-start.1

commit v8 on v7

--- a/solution.py
+++ b/solution.py
@@ -324,9 +324,21 @@
         tiled=True,
     ).reshape(-1)
     pick_at = jnp.minimum(target, owners * capacity - 1)
-    served = cond_table[asked].reshape(owners, capacity, width)
+    served_hot = (asked[:, None] == jnp.arange(elem_rows, dtype=jnp.int32)[None, :]).astype(
+        jnp.bfloat16
+    )
+    served = (
+        jnp.dot(served_hot, cond_table, preferred_element_type=jnp.float32)
+        .astype(jnp.bfloat16)
+        .reshape(owners, capacity, width)
+    )
     replies = lax.all_to_all(served, ("region", "ctx"), split_axis=0, concat_axis=0, tiled=True)
-    picked = replies.reshape(owners * capacity, width)[pick_at]
+    pick_hot = (
+        pick_at[:, None] == jnp.arange(owners * capacity, dtype=jnp.int32)[None, :]
+    ).astype(jnp.bfloat16)
+    picked = jnp.dot(
+        pick_hot, replies.reshape(owners * capacity, width), preferred_element_type=jnp.float32
+    )
     activated = jnp.where(solid[:, None], jax.nn.silu(picked.astype(jnp.float32)), 0.0).astype(
         jnp.bfloat16
     )

time: 200 us -> 196 us (0.980)
  local copies, waits for them, and re-layouts: 39.8 us -> 26.4 us
  matrix products: 12.6 us -> 18.4 us
  other arithmetic: 3.23 us -> 6.01 us
    gather x2 -> x0, local copies, waits for them, and re-layouts: 11.2 us -> none  [the longest x1 5.68 us: per_device(): picked = replies.reshape(owners * capacity, width)[pick_at]]
    dot_general x1, matrix products: 8.01 us -> 13.2 us  [per_device(): jnp.dot(activated, w_ada, preferred_element_type=jnp.float32) + b_ada]
    convert_element_type x1, other arithmetic: 0.63 us -> 3.44 us  [layer_modulate(): return (normed * (1.0 + scale) + shift).astype(jnp.bfloat16)]
    unnamed x15 -> x17, local copies, waits for them, and re-layouts: 14.8 us -> 12.5 us
    dot_general x0 -> x1, matrix products: none -> 2.24 us  [per_device(): jnp.dot(served_hot, cond_table, preferred_element_type=jnp.float32)]
where the time goes in v8:
time: 196 us; the launch traced here: 193 us
  Pallas kernels  101 us (52%)
  local copies, waits for them, and re-layouts  26.4 us (13%)
  blocking collectives  20.5 us (10%)
  matrix products  18.4 us (9%)
  waiting for transfers between devices  13.5 us (7%)
  other arithmetic  6.01 us (3%)
  starting transfers between devices  5.9 us (3%)
    pallas_call x2, Pallas kernels, attend_send(): pl.pallas_call(kernel, out_shape=out_shape, in_specs=[vmem_spec] * 3 + [a...  67.3 us
    pallas_call x1, Pallas kernels, project_send(): pl.pallas_call(kernel, out_shape=shapes * pair, in_specs=[vmem_spec, vmem...  34 us
    all_to_all x1, blocking collectives, per_device(): lax.all_to_all(requests.reshape(owners, capacity), ('region', 'ctx'), spl...  20.5 us
    all_to_all x1, waiting for transfers between devices, per_device(): lax.all_to_all(served, ('region', 'ctx'), split_axis=0, concat_axis=0, ti...  13.5 us
    dot_general x1, matrix products, per_device(): jnp.dot(activated, w_ada, preferred_element_type=jnp.float32) + b_ada  13.2 us
    unnamed x17, local copies, waits for them, and re-layouts  12.5 us
    transpose x1, local copies, waits for them, and re-layouts, per_device(): w_t = w_qkv.reshape(width, 3, shards, pair, head_dim).transpose(1, 3, 2,...  7.2 us
    all_to_all x1, starting transfers between devices, per_device(): lax.all_to_all(served, ('region', 'ctx'), split_axis=0, concat_axis=0, ti...  5.9 us
  transfers between devices with their start and end apart: 1, of which 1 were waited for; matrix products, arithmetic and copies ran while one was open for 10% of the time, Pallas kernels for 0%

profile of v8, /device:TPU:0, one launch (start us, length us, event | category | flops | bytes accessed | tf_op | source)
XLA Modules:
  0.0 192.9 jit_solution(5488042073826834017)
XLA Ops:
  0.8 0.8 compare_select_fusion.1
  1.6 3.5 %gather_fusion = s32[512]{0:T(512)S(1)} fusion(s32[16384]{0:T(1024)} %param.11, s32[1024]{0:T(1024)S(1)} %pad_clamp_fusion), kind=kCustom, calls=%fused_computation | custom fusion | bytes 6144 | tf_op jit(solution)/shard_map/gather | solution.py:306
  5.1 0.3 convert_reduce_fusion.1
  5.4 2.4 %scatter_custom_fusion = s32[1024]{0:T(1024)S(1)} fusion(s32[512]{0:T(512)S(1)} %bitcast.75, s32[512]{0:T(512)S(1)} %get-tuple-element.29, s32[]{:T(128)} %constant.38.clone.1), kind=kCustom, calls=%fused_computation.53 | custom fusion | bytes 4100 | tf_op jit(solution)/shard_map/scatter | solution.py:318
  7.9 0.1 all_to_all.9
  8.0 20.5 %all_to_all.14 = s32[128,1,8]{2,1,0:T(1,128)S(1)} all-to-all(s32[128,1,8]{2,1,0:T(1,128)S(1)} %bitcast.71), channel_id=1, replica_groups=mesh['region'=16,'ctx'=8] {'region','ctx'}, dimensions={0} | all-to-all | bytes 8192 | tf_op jit(solution)/shard_map/all_to_all | solution.py:319
  28.4 0.6 broadcast.238
  29.0 0.8 reduce.4
  29.8 0.1 eq.49
  29.9 2.2 %fusion.1 = bf16[128,8,1152]{2,1,0:T(8,128)(2,1)} fusion(bf16[128,1152]{1,0:T(8,128)(2,1)S(1)} %copy-done.4, s32[1024]{0:T(1024)S(1)} %eq.49), kind=kOutput, calls=%fused_computation.5 | convolution fusion | flops 303300608 | bytes 2658304 | tf_op jit(solution)/shard_map/dot_general | solution.py:331
  32.2 5.9 %all-to-all-start.1 = ((bf16[128,8,1152]{2,1,0:T(8,128)(2,1)}), bf16[128,8,1152]{2,1,0:T(8,128)(2,1)}, u32[]{:S(2)}, u32[]{:S(2)}) async-start(bf16[128,8,1152]{2,1,0:T(8,128)(2,1)} %fusion.1), calls=%async_computation.1 | async-start | bytes 4718592 | tf_op jit(solution)/shard_map/all_to_all | solution.py:335
  38.1 11.5 %copy.20 = bf16[1152,3456]{0,1:T(8,128)(2,1)} copy(bf16[1152,3456]{1,0:T(8,128)(2,1)} %param.16) | data formatting | bytes 15925248 | tf_op args[7]
  49.5 7.2 %copy.21 = bf16[3,2,8,72,1152]{4,3,2,1,0:T(8,128)(2,1)} copy(bf16[3,2,8,72,1152]{4,3,1,2,0:T(8,128)(2,1)} %bitcast.68) | data formatting | bytes 15925248 | tf_op jit(solution)/shard_map/transpose | solution.py:356
  56.7 0.2 convert_reduce_fusion
  57.0 0.5 fusion.10
  57.4 13.5 %all-to-all-done.1 = bf16[128,8,1152]{2,1,0:T(8,128)(2,1)} async-done(((bf16[128,8,1152]{2,1,0:T(8,128)(2,1)}), bf16[128,8,1152]{2,1,0:T(8,128)(2,1)}, u32[]{:S(2)}, u32[]{:S(2)}) %all-to-all-start.1) | async-done | bytes 2359328 | tf_op jit(solution)/shard_map/all_to_all | solution.py:335
  70.9 13.2 %fusion = f32[512,3456]{1,0:T(8,128)} fusion(bf16[1152,3456]{1,0:T(8,128)(2,1)} %param.14, f32[3456]{0:T(1024)S(1)} %copy-done.5, bf16[128,8,1152]{2,1,0:T(8,128)(2,1)} %all-to-all-done.1, pred[512]{0:T(512)(128)(4,1)S(1)} %iota_compare_fusion.7, s32[512]{0:T(512)S(1)} %select_minimum_fusion), kind=kOutput, calls=%fused_computation.3 | convolution fusion | flops 5294194688 | bytes 17416192 | tf_op jit(solution)/shard_map/dot_general | solution.py:345
  84.2 3.4 %fusion.13.mod_ref = bf16[512,1152]{1,0:T(8,128)(2,1)S(1)} fusion(bf16[1,512,1152]{2,1,0:T(8,128)(2,1)} %param.9, f32[512,3456]{1,0:T(8,128)} %fusion, f32[512]{0:T(512)S(1)} %add_rsqrt_fusion, f32[512]{0:T(512)S(1)} %broadcast_multiply_fusion), kind=kLoop, calls=%fused_computation.20 | loop fusion | flops 4128768 | bytes 7081984 | tf_op jit(solution)/shard_map/convert_element_type | solution.py:21
  87.6 34.0 %shard_map.91 = (bf16[8,72,512]{2,1,0:T(8,128)(2,1)S(1)}, bf16[8,512,72]{2,1,0:T(8,128)(2,1)S(1)}, bf16[8,72,512]{2,1,0:T(8,128)(2,1)S(1)}, bf16[8,72,512]{2,1,0...) custom-call(bf16[512,1152]{1,0:T(8,128)(2,1)S(1)} %fusion.13.mod_ref, ...), custom_call_target="tpu_custom_call" | custom-call | tf_op jit(solution)/shard_map/pallas_call | solution.py:263
  121.7 1.0 copy-done.1
  122.6 32.2 %shard_map.92 = (bf16[8,72,512]{2,1,0:T(8,128)(2,1)S(1)}, bf16[8,72,512]{2,1,0:T(8,128)(2,1)S(1)}, bf16[8,512,72]{2,1,0:T(8,128)(2,1)S(1)}, bf16[8,72,512]{2,1,0:T(8,128)(2,1)S(1)}) custom-call(bf16[8,72,512]{2,1,0:T(8,128)(2,1)S(1)} %get-tuple-element.17.refs_0_, bf16[8,512,72]{2,1,0:T(8,128)(2,1)S(1)} %get-tuple-element.18.refs_1_, ...), custom_call_target="tpu_custom_call" | custom-call | tf_op jit(solution)/shard_map/pallas_call | solution.py:209
  154.8 0.0 copy-start.3
  154.8 35.1 %shard_map.93 = (bf16[8,72,512]{2,1,0:T(8,128)(2,1)}, bf16[8,72,512]{2,1,0:T(8,128)(2,1)S(1)}, bf16[8,72,512]{2,1,0:T(8,128)(2,1)S(1)}) custom-call(bf16[8,72,512]{2,1,0:T(8,128)(2,1)S(1)} %get-tuple-element.23.refs_0_, bf16[8,512,72]{2,1,0:T(8,128)(2,1)S(1)} %get-tuple-element.24.refs_1_, bf16[8,72,512]{2,1,0:T(8,128)(2,1)S(1)} %get-tuple-element.25.refs_2_, ...), custom_call_target="tpu_custom_call" | custom-call | tf_op jit(solution)/shard_map/pallas_call | solution.py:209
  190.0 2.9 %fusion.8 = bf16[1,512,1152]{2,1,0:T(8,128)(2,1)} fusion(bf16[1,512,1152]{2,1,0:T(8,128)(2,1)S(1)} %copy-done.3, bf16[8,2,72,1152]{3,2,1,0:T(8,128)(2,1)S(1)} %bitcast.64, f32[512,3456]{1,0:T(8,128)S(1)} %bitcast.70, bf16[8,1,72,512]{3,2,0,1:T(8,128)(2,1)S(1)} %bitcast.66, bf16[8,1,72,512]{3,2,0,1:T(8,128)(2,1)S(1)} %bitcast.65), kind=kOutput, calls=%fused_computation.15 | convolution fusion | flops 1361903616 | bytes 8552448 | tf_op jit(solution)/shard_map/phet,pheD->tD/dot_general | solution.py:361
  (22 shorter events, 0.1 us)
Async XLA Ops:
  0.0 189.9 %copy-start = (bf16[1152,1152]{1,0:T(8,128)(2,1)S(1)}, bf16[1152,1152]{1,0:T(8,128)(2,1)}, u32[]{:S(2)}) copy-start(bf16[1152,1152]{1,0:T(8,128)(2,1)} %param.17) | copy-start | bytes 7962628
  0.0 29.9 %copy-start.4 = (bf16[128,1152]{1,0:T(8,128)(2,1)S(1)}, bf16[128,1152]{1,0:T(8,128)(2,1)}, u32[]{:S(2)}) copy-start(bf16[128,1152]{1,0:T(8,128)(2,1)} %param.13) | copy-start | bytes 884740
  32.2 38.8 %all-to-all-start.1 = ((bf16[128,8,1152]{2,1,0:T(8,128)(2,1)}), bf16[128,8,1152]{2,1,0:T(8,128)(2,1)}, u32[]{:S(2)}, u32[]{:S(2)}) async-start(bf16[128,8,1152]{2,1,0:T(8,128)(2,1)} %fusion.1), calls=%async_computation.1 | async-start | bytes 4718592 | tf_op jit(solution)/shard_map/all_to_all | solution.py:335
  49.5 7.2 %copy-start.2 = (bf16[1,512,1152]{2,1,0:T(8,128)(2,1)S(1)}, bf16[1,512,1152]{2,1,0:T(8,128)(2,1)}, u32[]{:S(2)}) copy-start(bf16[1,512,1152]{2,1,0:T(8,128)(2,1)} %param.9) | copy-start | bytes 3538948
  56.7 14.2 %copy-start.5 = (f32[3456]{0:T(1024)S(1)}, f32[3456]{0:T(1024)}, u32[]{:S(2)}) copy-start(f32[3456]{0:T(1024)} %param.15) | copy-start | bytes 41476
  84.2 105.7 %slice-start = ((s8[7077888]{0:T(1024)(128)(4,1)}), s8[4194304]{0:T(1024)(128)(4,1)S(1)}, s32[]{:S(2)}) async-start(s8[7077888]{0:T(1024)(128)(4,1)} %bitcast.69), calls=%async_computation.2 | async-start | bytes 8388608
  87.6 102.3 %slice-start.1 = ((s8[7077888]{0:T(1024)(128)(4,1)}), s8[2883584]{0:T(1024)(128)(4,1)S(1)}, s32[]{:S(2)}) async-start(s8[7077888]{0:T(1024)(128)(4,1)} %bitcast.69), calls=%async_computation.3 | async-start | bytes 5767168
  121.6 1.0 copy-start.1
  154.8 35.1 %copy-start.3 = (bf16[1,512,1152]{2,1,0:T(8,128)(2,1)S(1)}, bf16[1,512,1152]{2,1,0:T(8,128)(2,1)}, u32[]{:S(2)}) copy-start(bf16[1,512,1152]{2,1,0:T(8,128)(2,1)} %param.9) | copy-start | bytes 3538948

commit v9 on v8

--- a/solution.py
+++ b/solution.py
@@ -221,11 +221,12 @@
     return outs[0], outs[1:]
 
 
-def project_kernel(mod_ref, w_ref, *refs, shards, pair, head_dim):
+def project_kernel(mod_ref, w_ref, act_ref, wg_ref, bg_ref, *refs, shards, pair, head_dim):
     got0 = refs[:3]
     later = refs[3 : 3 * pair]
-    send0 = refs[3 * pair : 3 * pair + 3]
-    sems = refs[3 * pair + 3 :]
+    gate_ref = refs[3 * pair]
+    send0 = refs[3 * pair + 1 : 3 * pair + 4]
+    sems = refs[3 * pair + 4 :]
     modulated = mod_ref[...]
 
     def fill(h, dests):
@@ -246,11 +247,13 @@
     copies = start_sends(send0, got0, *sems, shards)
     for h in range(1, pair):
         fill(h, later[3 * (h - 1) : 3 * h])
+    gate = jnp.dot(act_ref[...], wg_ref[...], preferred_element_type=jnp.float32)
+    gate_ref[...] = (gate + bg_ref[...]).astype(gate_ref.dtype)
     for copy in copies:
         copy.wait()
 
 
-def project_send(modulated, w_t, shards, pair, head_dim):
+def project_send(modulated, w_t, activated, w_gate, b_gate, shards, pair, head_dim):
     rows, width = modulated.shape
     q_shape = jax.ShapeDtypeStruct((shards, head_dim, rows), jnp.bfloat16)
     k_shape = jax.ShapeDtypeStruct((shards, rows, head_dim), jnp.bfloat16)
@@ -262,9 +265,10 @@
     vmem_spec = pl.BlockSpec(memory_space=pltpu.VMEM)
     outs = pl.pallas_call(
         kernel,
-        out_shape=shapes * pair,
-        in_specs=[vmem_spec, vmem_spec],
-        out_specs=[any_spec] * 3 + [vmem_spec] * (3 * (pair - 1)),
+        out_shape=shapes * pair
+        + [jax.ShapeDtypeStruct((rows, w_gate.shape[1]), jnp.bfloat16)],
+        in_specs=[vmem_spec] * 5,
+        out_specs=[any_spec] * 3 + [vmem_spec] * (3 * (pair - 1) + 1),
         scratch_shapes=[pltpu.VMEM(x.shape, x.dtype) for x in shapes]
         + send_scratch(3, shards),
         compiler_params=pltpu.CompilerParams(
@@ -272,12 +276,12 @@
             has_side_effects=True,
             vmem_limit_bytes=48 * 1024 * 1024,
         ),
-    )(modulated, w_t)
-    return outs[:3], [outs[3 * h : 3 * h + 3] for h in range(1, pair)]
-
-
-def head_pipeline(modulated, w_t, shards, pair, head_dim, inverse_root):
-    got, later = project_send(modulated, w_t, shards, pair, head_dim)
+    )(modulated, w_t, activated, w_gate, b_gate)
+    return outs[:3], [outs[3 * h : 3 * h + 3] for h in range(1, pair)], outs[3 * pair]
+
+
+def head_pipeline(modulated, w_t, gate_parts, shards, pair, head_dim, inverse_root):
+    got, later, gate = project_send(modulated, w_t, *gate_parts, shards, pair, head_dim)
     backs = []
     for h in range(pair):
         last = h + 1 == pair
@@ -291,7 +295,7 @@
             got = sent[:3]
             sent = sent[3:]
         backs.extend(sent)
-    return jnp.stack(backs, axis=1)
+    return jnp.stack(backs, axis=1), gate
 
 
 def per_device(
@@ -342,10 +346,12 @@
     activated = jnp.where(solid[:, None], jax.nn.silu(picked.astype(jnp.float32)), 0.0).astype(
         jnp.bfloat16
     )
-    mods = (jnp.dot(activated, w_ada, preferred_element_type=jnp.float32) + b_ada).astype(
-        jnp.bfloat16
-    )
+    mods = (
+        jnp.dot(activated, w_ada[:, : 2 * width], preferred_element_type=jnp.float32)
+        + b_ada[: 2 * width]
+    ).astype(jnp.bfloat16)
     mods = mods.astype(jnp.float32)
+    gate_parts = (activated, w_ada[:, 2 * width :], b_ada[None, 2 * width :])
     modulated = layer_modulate(device_tokens, mods, width)
 
     head_dim = width // HEADS
@@ -356,7 +362,9 @@
         .transpose(1, 3, 2, 4, 0)
         .reshape(3, pair, shards * head_dim, width)
     )
-    backs = head_pipeline(modulated, w_t, shards, pair, head_dim, inverse_root)
+    backs, gate = head_pipeline(
+        modulated, w_t, gate_parts, shards, pair, head_dim, inverse_root
+    )
     w_out_parts = w_out.reshape(shards, pair, head_dim, width)
     projected = jnp.einsum(
         "phet,pheD->tD",
@@ -364,7 +372,7 @@
         w_out_parts,
         preferred_element_type=jnp.float32,
     )
-    gate = mods[:, 2 * width :]
+    gate = gate.astype(jnp.float32)
     output = (device_tokens.astype(jnp.float32) + gate * projected).astype(jnp.bfloat16)
     return output[None]
 

time: 196 us -> 192 us (0.980)
  waiting for transfers between devices: 13.5 us -> 9.86 us
  local copies, waits for them, and re-layouts: 26.4 us -> 30 us
  matrix products: 18.4 us -> 14.9 us
  Pallas kernels: 101 us -> 103 us
    all_to_all x1, waiting for transfers between devices: 13.5 us -> 9.86 us  [per_device(): lax.all_to_all(served, ('region', 'ctx'), split_axis=0, concat_axis=0, ti...]
    slice x0 -> x4, local copies, waits for them, and re-layouts: none -> 3.62 us  [the longest x2 3.61 us: per_device(): gate_parts = (activated, w_ada[:, 2 * width:], b_ada[None, 2 * width:])]
    dot_general x1 -> x2, matrix products: 13.2 us -> 9.66 us  [the longest x1 6.17 us: per_device(): jnp.dot(activated, w_ada[:, :2 * width], preferred_element_type=jnp.float32)]
    unnamed x17 -> x15, local copies, waits for them, and re-layouts: 12.5 us -> 12.5 us
  transfers between devices with their start and end apart: 1 -> 1, of which waited for: 1 -> 1; matrix products, arithmetic and copies ran while one was open for 10% -> 12% of each run, Pallas kernels for 0% -> 0%
where the time goes in v9:
time: 192 us; the launch traced here: 189 us
  Pallas kernels  103 us (54%)
  local copies, waits for them, and re-layouts  30 us (16%)
  blocking collectives  20.5 us (11%)
  matrix products  14.9 us (8%)
  waiting for transfers between devices  9.86 us (5%)
  starting transfers between devices  6.04 us (3%)
  other arithmetic  4.23 us (2%)
    pallas_call x2, Pallas kernels, attend_send(): pl.pallas_call(kernel, out_shape=out_shape, in_specs=[vmem_spec] * 3 + [a...  67.3 us
    pallas_call x1, Pallas kernels, project_send(): pl.pallas_call(kernel, out_shape=shapes * pair + [jax.ShapeDtypeStruct((r...  35.4 us
    all_to_all x1, blocking collectives, per_device(): lax.all_to_all(requests.reshape(owners, capacity), ('region', 'ctx'), spl...  20.5 us
    unnamed x15, local copies, waits for them, and re-layouts  12.5 us
    all_to_all x1, waiting for transfers between devices, per_device(): lax.all_to_all(served, ('region', 'ctx'), split_axis=0, concat_axis=0, ti...  9.86 us
    transpose x1, local copies, waits for them, and re-layouts, per_device(): w_t = w_qkv.reshape(width, 3, shards, pair, head_dim).transpose(1, 3, 2,...  7.1 us
    dot_general x1, matrix products, per_device(): jnp.dot(activated, w_ada[:, :2 * width], preferred_element_type=jnp.float32)  6.17 us
    all_to_all x1, starting transfers between devices, per_device(): lax.all_to_all(served, ('region', 'ctx'), split_axis=0, concat_axis=0, ti...  6.04 us
  transfers between devices with their start and end apart: 1, of which 1 were waited for; matrix products, arithmetic and copies ran while one was open for 12% of the time, Pallas kernels for 0%

profile of v9, /device:TPU:0, one launch (start us, length us, event | category | flops | bytes accessed | tf_op | source)
XLA Modules:
  0.0 189.0 jit_solution(11812293871903157435)
XLA Ops:
  0.0 0.8 compare_select_fusion.1
  0.9 3.6 %gather_fusion = s32[512]{0:T(512)S(1)} fusion(s32[16384]{0:T(1024)} %param.11, s32[1024]{0:T(1024)S(1)} %pad_clamp_fusion), kind=kCustom, calls=%fused_computation | custom fusion | bytes 6144 | tf_op jit(solution)/shard_map/gather | solution.py:310
  5.1 0.3 convert_reduce_fusion.1
  5.4 2.4 %scatter_custom_fusion = s32[1024]{0:T(1024)S(1)} fusion(s32[512]{0:T(512)S(1)} %bitcast.70, s32[512]{0:T(512)S(1)} %get-tuple-element.31, s32[]{:T(128)} %constant.41.clone.1), kind=kCustom, calls=%fused_computation.52 | custom fusion | bytes 4100 | tf_op jit(solution)/shard_map/scatter | solution.py:322
  7.9 20.5 %all_to_all.14 = s32[128,1,8]{2,1,0:T(1,128)S(1)} all-to-all(s32[128,1,8]{2,1,0:T(1,128)S(1)} %bitcast.66), channel_id=1, replica_groups=mesh['region'=16,'ctx'=8] {'region','ctx'}, dimensions={0} | all-to-all | bytes 8192 | tf_op jit(solution)/shard_map/all_to_all | solution.py:323
  28.4 0.5 broadcast.238
  28.9 0.8 reduce.4
  29.7 0.1 eq.49
  29.8 2.2 %fusion.11 = bf16[128,8,1152]{2,1,0:T(8,128)(2,1)} fusion(bf16[128,1152]{1,0:T(8,128)(2,1)S(1)} %copy-done.5, s32[1024]{0:T(1024)S(1)} %eq.49), kind=kOutput, calls=%fused_computation.8 | convolution fusion | flops 303300608 | bytes 2658304 | tf_op jit(solution)/shard_map/dot_general | solution.py:335
  32.1 6.0 %all-to-all-start.1 = ((bf16[128,8,1152]{2,1,0:T(8,128)(2,1)}), bf16[128,8,1152]{2,1,0:T(8,128)(2,1)}, u32[]{:S(2)}, u32[]{:S(2)}) async-start(bf16[128,8,1152]{2,1,0:T(8,128)(2,1)} %fusion.11), calls=%async_computation.1 | async-start | bytes 4718592 | tf_op jit(solution)/shard_map/all_to_all | solution.py:339
  38.2 11.5 %copy.20 = bf16[1152,3456]{0,1:T(8,128)(2,1)} copy(bf16[1152,3456]{1,0:T(8,128)(2,1)} %param.16) | data formatting | bytes 15925248 | tf_op args[7]
  49.7 7.1 %copy.21 = bf16[3,2,8,72,1152]{4,3,2,1,0:T(8,128)(2,1)} copy(bf16[3,2,8,72,1152]{4,3,1,2,0:T(8,128)(2,1)} %bitcast.65) | data formatting | bytes 15925248 | tf_op jit(solution)/shard_map/transpose | solution.py:362
  56.8 3.6 %slice.22.wg_ref = bf16[1152,1152]{1,0:T(8,128)(2,1)} slice(bf16[1152,3456]{1,0:T(8,128)(2,1)} %param.14), slice={[0:1152], [2304:3456]} | slice | bytes 5308416 | tf_op jit(solution)/shard_map/slice | solution.py:354
  60.4 0.2 convert_reduce_fusion
  60.7 0.5 fusion.20
  61.2 9.9 %all-to-all-done.1 = bf16[128,8,1152]{2,1,0:T(8,128)(2,1)} async-done(((bf16[128,8,1152]{2,1,0:T(8,128)(2,1)}), bf16[128,8,1152]{2,1,0:T(8,128)(2,1)}, u32[]{:S(2)}, u32[]{:S(2)}) %all-to-all-start.1) | async-done | bytes 2359328 | tf_op jit(solution)/shard_map/all_to_all | solution.py:339
  71.0 3.5 %select_convert_fusion.act_ref = bf16[512,1152]{1,0:T(8,128)(2,1)S(1)} fusion(bf16[128,8,1152]{2,1,0:T(8,128)(2,1)} %all-to-all-done.1, pred[512]{0:T(512)(128)(4,1)S(1)} %iota_compare_fusion.5, s32[512]{0:T(512)S(1)} %select_minimum_fusion), kind=kOutput, calls=%fused_computation.27 | convolution fusion | flops 1212022784 | bytes 3541504 | tf_op jit(solution)/shard_map/dot_general | solution.py:343
  74.5 6.2 %fusion.8 = f32[512,2304]{1,0:T(8,128)S(1)} fusion(bf16[512,1152]{1,0:T(8,128)(2,1)S(1)} %select_convert_fusion.act_ref, bf16[1152,3456]{1,0:T(8,128)(2,1)} %param.14, f32[2304]{0:T(1024)S(1)} %slice-done), kind=kOutput, calls=%fused_computation.6 | convolution fusion | flops 2721447936 | bytes 11215872 | tf_op jit(solution)/shard_map/dot_general | solution.py:350
  80.7 1.6 fusion.23.mod_ref
  82.3 35.4 %shard_map.91 = (bf16[8,72,512]{2,1,0:T(8,128)(2,1)S(1)}, bf16[8,512,72]{2,1,0:T(8,128)(2,1)S(1)}, bf16[8,72,512]{2,1,0:T(8,128)(2,1)S(1)}, bf16[8,72,512]{2,1,0...) custom-call(bf16[512,1152]{1,0:T(8,128)(2,1)} %fusion.23.mod_ref, ...), custom_call_target="tpu_custom_call" | custom-call | tf_op jit(solution)/shard_map/pallas_call | solution.py:266
  117.8 1.0 copy-done.1
  118.7 32.4 %shard_map.92 = (bf16[8,72,512]{2,1,0:T(8,128)(2,1)S(1)}, bf16[8,72,512]{2,1,0:T(8,128)(2,1)S(1)}, bf16[8,512,72]{2,1,0:T(8,128)(2,1)S(1)}, bf16[8,72,512]{2,1,0:T(8,128)(2,1)S(1)}) custom-call(bf16[8,72,512]{2,1,0:T(8,128)(2,1)S(1)} %get-tuple-element.19.refs_0_, bf16[8,512,72]{2,1,0:T(8,128)(2,1)S(1)} %get-tuple-element.20.refs_1_, ...), custom_call_target="tpu_custom_call" | custom-call | tf_op jit(solution)/shard_map/pallas_call | solution.py:209
  151.1 34.9 %shard_map.93 = (bf16[8,72,512]{2,1,0:T(8,128)(2,1)}, bf16[8,72,512]{2,1,0:T(8,128)(2,1)S(1)}, bf16[8,72,512]{2,1,0:T(8,128)(2,1)S(1)}) custom-call(bf16[8,72,512]{2,1,0:T(8,128)(2,1)S(1)} %get-tuple-element.25.refs_0_, bf16[8,512,72]{2,1,0:T(8,128)(2,1)S(1)} %get-tuple-element.26.refs_1_, bf16[8,72,512]{2,1,0:T(8,128)(2,1)S(1)} %get-tuple-element.27.refs_2_, ...), custom_call_target="tpu_custom_call" | custom-call | tf_op jit(solution)/shard_map/pallas_call | solution.py:209
  186.0 3.0 %fusion.18 = bf16[1,512,1152]{2,1,0:T(8,128)(2,1)} fusion(bf16[1,512,1152]{2,1,0:T(8,128)(2,1)S(1)} %copy-done.3, bf16[8,2,72,1152]{3,2,1,0:T(8,128)(2,1)S(1)} %bitcast.61, bf16[512,1152]{1,0:T(8,128)(2,1)S(1)} %get-tuple-element.18, bf16[8,1,72,512]{3,2,0,1:T(8,128)(2,1)S(1)} %bitcast.63, bf16[8,1,72,512]{3,2,0,1:T(8,128)(2,1)S(1)} %bitcast.62), kind=kOutput, calls=%fused_computation.18 | convolution fusion | flops 1362493440 | bytes 7372800 | tf_op jit(solution)/shard_map/phet,pheD->tD/dot_general | solution.py:369
  (25 shorter events, 0.2 us)
Async XLA Ops:
  0.0 186.0 %copy-start = (bf16[1152,1152]{1,0:T(8,128)(2,1)S(1)}, bf16[1152,1152]{1,0:T(8,128)(2,1)}, u32[]{:S(2)}) copy-start(bf16[1152,1152]{1,0:T(8,128)(2,1)} %param.17) | copy-start | bytes 7962628
  0.0 29.8 %copy-start.5 = (bf16[128,1152]{1,0:T(8,128)(2,1)S(1)}, bf16[128,1152]{1,0:T(8,128)(2,1)}, u32[]{:S(2)}) copy-start(bf16[128,1152]{1,0:T(8,128)(2,1)} %param.13) | copy-start | bytes 884740
  32.1 6.0 %copy-start.6 = (f32[3456]{0:T(1024)S(1)}, f32[3456]{0:T(1024)}, u32[]{:S(2)}) copy-start(f32[3456]{0:T(1024)} %param.15) | copy-start | bytes 41476
  32.1 38.9 %all-to-all-start.1 = ((bf16[128,8,1152]{2,1,0:T(8,128)(2,1)}), bf16[128,8,1152]{2,1,0:T(8,128)(2,1)}, u32[]{:S(2)}, u32[]{:S(2)}) async-start(bf16[128,8,1152]{2,1,0:T(8,128)(2,1)} %fusion.11), calls=%async_computation.1 | async-start | bytes 4718592 | tf_op jit(solution)/shard_map/all_to_all | solution.py:339
  56.8 3.6 %copy-start.2 = (bf16[1,512,1152]{2,1,0:T(8,128)(2,1)S(1)}, bf16[1,512,1152]{2,1,0:T(8,128)(2,1)}, u32[]{:S(2)}) copy-start(bf16[1,512,1152]{2,1,0:T(8,128)(2,1)} %param.9) | copy-start | bytes 3538948
  61.1 13.4 %slice-start = ((f32[3456]{0:T(1024)}), f32[2304]{0:T(1024)S(1)}, s32[]{:S(2)}) async-start(f32[3456]{0:T(1024)} %param.15), calls=%async_computation.2 | async-start | bytes 24576 | tf_op jit(solution)/shard_map/slice | solution.py:351
  74.5 6.2 %copy-start.4 = (bf16[512,1152]{1,0:T(8,128)(2,1)}, bf16[512,1152]{1,0:T(8,128)(2,1)S(1)}, u32[]{:S(2)}) copy-start(bf16[512,1152]{1,0:T(8,128)(2,1)S(1)} %select_convert_fusion.act_ref) | copy-start | bytes 3538948
  74.5 6.2 %copy-start.3 = (bf16[1,512,1152]{2,1,0:T(8,128)(2,1)S(1)}, bf16[1,512,1152]{2,1,0:T(8,128)(2,1)}, u32[]{:S(2)}) copy-start(bf16[1,512,1152]{2,1,0:T(8,128)(2,1)} %param.9) | copy-start | bytes 3538948
  117.8 1.0 copy-start.1

commit v10 on v9

--- a/solution.py
+++ b/solution.py
@@ -83,8 +83,10 @@
     )(*arrays)
 
 
-def attend_body(qt_ref, k_ref, vt_ref, o_ref, s_scr, inv_root, after_block=None):
+def attend_body(qt_ref, kt_ref, vt_ref, o_ref, s_scr, k_ref, inv_root, after_block=None):
     blocks, head_dim, q_rows = qt_ref.shape
+    for c in range(blocks):
+        k_ref[c] = kt_ref[c].astype(jnp.float32).T.astype(k_ref.dtype)
 
     def one_block(b, carry):
         qt = qt_ref[b]
@@ -134,7 +136,8 @@
     if stream:
         back_ref = rest[0]
         rest = rest[1:]
-    s_scr = rest[0]
+    s_scr, k_scr = rest[0], rest[1]
+    rest = rest[1:]
     copies = start_sends(sends, gots, *rest[1:4], shards)
     after_block = None
     if stream:
@@ -164,7 +167,7 @@
             def _():
                 remote_block(b).start()
 
-    attend_body(qt_ref, k_ref, vt_ref, o_ref, s_scr, inv_root, after_block)
+    attend_body(qt_ref, k_ref, vt_ref, o_ref, s_scr, k_scr, inv_root, after_block)
     for copy in copies:
         copy.wait()
     if stream:
@@ -197,7 +200,10 @@
     out_shape = [jax.ShapeDtypeStruct(q_t.shape, jnp.bfloat16)]
     out_shape += [jax.ShapeDtypeStruct(x.shape, x.dtype) for x in sends]
     out_specs = [vmem_spec] + [any_spec] * count
-    scratch = [pltpu.VMEM((blocks, rows, rows), jnp.float32)] + send_scratch(count, shards)
+    scratch = [
+        pltpu.VMEM((blocks, rows, rows), jnp.float32),
+        pltpu.VMEM((blocks, rows, head_dim), jnp.bfloat16),
+    ] + send_scratch(count, shards)
     if stream:
         out_shape.append(jax.ShapeDtypeStruct(q_t.shape, jnp.bfloat16))
         out_specs.append(any_spec)
@@ -239,8 +245,6 @@
             )
             for p in range(shards):
                 piece = out_t[p * head_dim : (p + 1) * head_dim]
-                if i == 1:
-                    piece = piece.T
                 dests[i][p] = piece.astype(jnp.bfloat16)
 
     fill(0, send0)
@@ -256,8 +260,7 @@
 def project_send(modulated, w_t, activated, w_gate, b_gate, shards, pair, head_dim):
     rows, width = modulated.shape
     q_shape = jax.ShapeDtypeStruct((shards, head_dim, rows), jnp.bfloat16)
-    k_shape = jax.ShapeDtypeStruct((shards, rows, head_dim), jnp.bfloat16)
-    shapes = [q_shape, k_shape, q_shape]
+    shapes = [q_shape, q_shape, q_shape]
     kernel = functools.partial(
         project_kernel, shards=shards, pair=pair, head_dim=head_dim
     )

time: 192 us -> 186 us (0.969)
  Pallas kernels: 103 us -> 98.4 us
    pallas_call x1, Pallas kernels: 35.4 us -> 30.2 us  [project_send(): pl.pallas_call(kernel, out_shape=shapes * pair + [jax.ShapeDtypeStruct((r...]
    unnamed x15 -> x13, local copies, waits for them, and re-layouts: 12.5 us -> 11.5 us
  transfers between devices with their start and end apart: 1 -> 1, of which waited for: 1 -> 1; matrix products, arithmetic and copies ran while one was open for 12% -> 13% of each run, Pallas kernels for 0% -> 0%
where the time goes in v10:
time: 186 us; the launch traced here: 183 us
  Pallas kernels  98.4 us (53%)
  local copies, waits for them, and re-layouts  28.9 us (16%)
  blocking collectives  20.5 us (11%)
  matrix products  14.9 us (8%)
  waiting for transfers between devices  9.92 us (5%)
  starting transfers between devices  6.03 us (3%)
  other arithmetic  3.15 us (2%)
    pallas_call x2, Pallas kernels, attend_send(): pl.pallas_call(kernel, out_shape=out_shape, in_specs=[vmem_spec] * 3 + [a...  68.2 us
    pallas_call x1, Pallas kernels, project_send(): pl.pallas_call(kernel, out_shape=shapes * pair + [jax.ShapeDtypeStruct((r...  30.2 us
    all_to_all x1, blocking collectives, per_device(): lax.all_to_all(requests.reshape(owners, capacity), ('region', 'ctx'), spl...  20.5 us
    unnamed x13, local copies, waits for them, and re-layouts  11.5 us
    all_to_all x1, waiting for transfers between devices, per_device(): lax.all_to_all(served, ('region', 'ctx'), split_axis=0, concat_axis=0, ti...  9.92 us
    transpose x1, local copies, waits for them, and re-layouts, per_device(): w_t = w_qkv.reshape(width, 3, shards, pair, head_dim).transpose(1, 3, 2,...  7.11 us
    dot_general x1, matrix products, per_device(): jnp.dot(activated, w_ada[:, :2 * width], preferred_element_type=jnp.float32)  6.17 us
    all_to_all x1, starting transfers between devices, per_device(): lax.all_to_all(served, ('region', 'ctx'), split_axis=0, concat_axis=0, ti...  6.03 us
  transfers between devices with their start and end apart: 1, of which 1 were waited for; matrix products, arithmetic and copies ran while one was open for 13% of the time, Pallas kernels for 0%

profile of v10, /device:TPU:0, one launch (start us, length us, event | category | flops | bytes accessed | tf_op | source)
XLA Modules:
  0.0 182.6 jit_solution(11863627292500398940)
XLA Ops:
  0.0 0.8 compare_select_fusion.1
  0.9 3.6 %gather_fusion = s32[512]{0:T(512)S(1)} fusion(s32[16384]{0:T(1024)} %param.11, s32[1024]{0:T(1024)S(1)} %pad_clamp_fusion), kind=kCustom, calls=%fused_computation | custom fusion | bytes 6144 | tf_op jit(solution)/shard_map/gather | solution.py:313
  5.1 0.3 convert_reduce_fusion.1
  5.4 2.4 %scatter_custom_fusion = s32[1024]{0:T(1024)S(1)} fusion(s32[512]{0:T(512)S(1)} %bitcast.70, s32[512]{0:T(512)S(1)} %get-tuple-element.31, s32[]{:T(128)} %constant.41.clone.1), kind=kCustom, calls=%fused_computation.52 | custom fusion | bytes 4100 | tf_op jit(solution)/shard_map/scatter | solution.py:325
  7.9 0.1 all_to_all.9
  7.9 20.5 %all_to_all.14 = s32[128,1,8]{2,1,0:T(1,128)S(1)} all-to-all(s32[128,1,8]{2,1,0:T(1,128)S(1)} %bitcast.66), channel_id=1, replica_groups=mesh['region'=16,'ctx'=8] {'region','ctx'}, dimensions={0} | all-to-all | bytes 8192 | tf_op jit(solution)/shard_map/all_to_all | solution.py:326
  28.4 0.5 broadcast.238
  28.9 0.7 reduce.4
  29.6 0.1 eq.49
  29.7 2.2 %fusion.11 = bf16[128,8,1152]{2,1,0:T(8,128)(2,1)} fusion(bf16[128,1152]{1,0:T(8,128)(2,1)S(1)} %copy-done.4, s32[1024]{0:T(1024)S(1)} %eq.49), kind=kOutput, calls=%fused_computation.8 | convolution fusion | flops 303300608 | bytes 2658304 | tf_op jit(solution)/shard_map/dot_general | solution.py:338
  32.0 6.0 %all-to-all-start.1 = ((bf16[128,8,1152]{2,1,0:T(8,128)(2,1)}), bf16[128,8,1152]{2,1,0:T(8,128)(2,1)}, u32[]{:S(2)}, u32[]{:S(2)}) async-start(bf16[128,8,1152]{2,1,0:T(8,128)(2,1)} %fusion.11), calls=%async_computation.1 | async-start | bytes 4718592 | tf_op jit(solution)/shard_map/all_to_all | solution.py:342
  38.0 11.5 %copy.20 = bf16[1152,3456]{0,1:T(8,128)(2,1)} copy(bf16[1152,3456]{1,0:T(8,128)(2,1)} %param.16) | data formatting | bytes 15925248 | tf_op args[7]
  49.5 7.1 %copy.21 = bf16[3,2,8,72,1152]{4,3,2,1,0:T(8,128)(2,1)} copy(bf16[3,2,8,72,1152]{4,3,1,2,0:T(8,128)(2,1)} %bitcast.65) | data formatting | bytes 15925248 | tf_op jit(solution)/shard_map/transpose | solution.py:365
  56.6 3.6 %slice.22.wg_ref = bf16[1152,1152]{1,0:T(8,128)(2,1)} slice(bf16[1152,3456]{1,0:T(8,128)(2,1)} %param.14), slice={[0:1152], [2304:3456]} | slice | bytes 5308416 | tf_op jit(solution)/shard_map/slice | solution.py:357
  60.2 0.2 convert_reduce_fusion
  60.5 0.5 fusion.20
  61.0 9.9 %all-to-all-done.1 = bf16[128,8,1152]{2,1,0:T(8,128)(2,1)} async-done(((bf16[128,8,1152]{2,1,0:T(8,128)(2,1)}), bf16[128,8,1152]{2,1,0:T(8,128)(2,1)}, u32[]{:S(2)}, u32[]{:S(2)}) %all-to-all-start.1) | async-done | bytes 2359328 | tf_op jit(solution)/shard_map/all_to_all | solution.py:342
  70.9 3.5 %select_convert_fusion.act_ref = bf16[512,1152]{1,0:T(8,128)(2,1)S(1)} fusion(bf16[128,8,1152]{2,1,0:T(8,128)(2,1)} %all-to-all-done.1, pred[512]{0:T(512)(128)(4,1)S(1)} %iota_compare_fusion.5, s32[512]{0:T(512)S(1)} %select_minimum_fusion), kind=kOutput, calls=%fused_computation.27 | convolution fusion | flops 1212022784 | bytes 3541504 | tf_op jit(solution)/shard_map/dot_general | solution.py:346
  74.4 6.2 %fusion.8 = f32[512,2304]{1,0:T(8,128)S(1)} fusion(bf16[512,1152]{1,0:T(8,128)(2,1)S(1)} %select_convert_fusion.act_ref, bf16[1152,3456]{1,0:T(8,128)(2,1)} %param.14, f32[2304]{0:T(1024)S(1)} %slice-done), kind=kOutput, calls=%fused_computation.6 | convolution fusion | flops 2721447936 | bytes 11215872 | tf_op jit(solution)/shard_map/dot_general | solution.py:353
  80.6 0.6 fusion.23.mod_ref
  81.2 30.2 %shard_map.91 = (bf16[8,72,512]{2,1,0:T(8,128)(2,1)S(1)}, bf16[8,72,512]{2,1,0:T(8,128)(2,1)S(1)}, bf16[8,72,512]{2,1,0:T(8,128)(2,1)S(1)}, bf16[8,72,512]{2,1,0...) custom-call(bf16[512,1152]{1,0:T(8,128)(2,1)S(1)} %fusion.23.mod_ref, ...), custom_call_target="tpu_custom_call" | custom-call | tf_op jit(solution)/shard_map/pallas_call | solution.py:269
  111.4 32.9 %shard_map.92 = (bf16[8,72,512]{2,1,0:T(8,128)(2,1)S(1)}, bf16[8,72,512]{2,1,0:T(8,128)(2,1)S(1)}, bf16[8,72,512]{2,1,0:T(8,128)(2,1)S(1)}, bf16[8,72,512]{2,1,0:T(8,128)(2,1)S(1)}) custom-call(bf16[8,72,512]{2,1,0:T(8,128)(2,1)S(1)} %get-tuple-element.19.refs_0_, bf16[8,72,512]{2,1,0:T(8,128)(2,1)S(1)} %get-tuple-element.20.refs_1_, ...), custom_call_target="tpu_custom_call" | custom-call | tf_op jit(solution)/shard_map/pallas_call | solution.py:215
  144.3 35.3 %shard_map.93 = (bf16[8,72,512]{2,1,0:T(8,128)(2,1)}, bf16[8,72,512]{2,1,0:T(8,128)(2,1)S(1)}, bf16[8,72,512]{2,1,0:T(8,128)(2,1)S(1)}) custom-call(bf16[8,72,512]{2,1,0:T(8,128)(2,1)S(1)} %get-tuple-element.25.refs_0_, bf16[8,72,512]{2,1,0:T(8,128)(2,1)S(1)} %get-tuple-element.26.refs_1_, bf16[8,72,512]{2,1,0:T(8,128)(2,1)S(1)} %get-tuple-element.27.refs_2_, ...), custom_call_target="tpu_custom_call" | custom-call | tf_op jit(solution)/shard_map/pallas_call | solution.py:215
  179.6 3.0 %fusion.18 = bf16[1,512,1152]{2,1,0:T(8,128)(2,1)} fusion(bf16[1,512,1152]{2,1,0:T(8,128)(2,1)S(1)} %copy-done.2, bf16[8,2,72,1152]{3,2,1,0:T(8,128)(2,1)S(1)} %bitcast.61, bf16[512,1152]{1,0:T(8,128)(2,1)S(1)} %get-tuple-element.18, bf16[8,1,72,512]{3,2,0,1:T(8,128)(2,1)S(1)} %bitcast.63, bf16[8,1,72,512]{3,2,0,1:T(8,128)(2,1)S(1)} %bitcast.62), kind=kOutput, calls=%fused_computation.18 | convolution fusion | flops 1362493440 | bytes 7372800 | tf_op jit(solution)/shard_map/phet,pheD->tD/dot_general | solution.py:372
  (23 shorter events, 0.1 us)
Async XLA Ops:
  0.0 179.6 %copy-start = (bf16[1152,1152]{1,0:T(8,128)(2,1)S(1)}, bf16[1152,1152]{1,0:T(8,128)(2,1)}, u32[]{:S(2)}) copy-start(bf16[1152,1152]{1,0:T(8,128)(2,1)} %param.17) | copy-start | bytes 7962628
  0.0 29.7 %copy-start.4 = (bf16[128,1152]{1,0:T(8,128)(2,1)S(1)}, bf16[128,1152]{1,0:T(8,128)(2,1)}, u32[]{:S(2)}) copy-start(bf16[128,1152]{1,0:T(8,128)(2,1)} %param.13) | copy-start | bytes 884740
  32.0 6.0 %copy-start.5 = (f32[3456]{0:T(1024)S(1)}, f32[3456]{0:T(1024)}, u32[]{:S(2)}) copy-start(f32[3456]{0:T(1024)} %param.15) | copy-start | bytes 41476
  32.0 38.9 %all-to-all-start.1 = ((bf16[128,8,1152]{2,1,0:T(8,128)(2,1)}), bf16[128,8,1152]{2,1,0:T(8,128)(2,1)}, u32[]{:S(2)}, u32[]{:S(2)}) async-start(bf16[128,8,1152]{2,1,0:T(8,128)(2,1)} %fusion.11), calls=%async_computation.1 | async-start | bytes 4718592 | tf_op jit(solution)/shard_map/all_to_all | solution.py:342
  56.6 3.6 %copy-start.1 = (bf16[1,512,1152]{2,1,0:T(8,128)(2,1)S(1)}, bf16[1,512,1152]{2,1,0:T(8,128)(2,1)}, u32[]{:S(2)}) copy-start(bf16[1,512,1152]{2,1,0:T(8,128)(2,1)} %param.9) | copy-start | bytes 3538948
  61.0 13.4 %slice-start = ((f32[3456]{0:T(1024)}), f32[2304]{0:T(1024)S(1)}, s32[]{:S(2)}) async-start(f32[3456]{0:T(1024)} %param.15), calls=%async_computation.2 | async-start | bytes 24576 | tf_op jit(solution)/shard_map/slice | solution.py:354
  74.4 6.2 %copy-start.3 = (bf16[512,1152]{1,0:T(8,128)(2,1)}, bf16[512,1152]{1,0:T(8,128)(2,1)S(1)}, u32[]{:S(2)}) copy-start(bf16[512,1152]{1,0:T(8,128)(2,1)S(1)} %select_convert_fusion.act_ref) | copy-start | bytes 3538948
  74.4 6.2 %copy-start.2 = (bf16[1,512,1152]{2,1,0:T(8,128)(2,1)S(1)}, bf16[1,512,1152]{2,1,0:T(8,128)(2,1)}, u32[]{:S(2)}) copy-start(bf16[1,512,1152]{2,1,0:T(8,128)(2,1)} %param.9) | copy-start | bytes 3538948

commit v11 on v10

--- a/solution.py
+++ b/solution.py
@@ -21,33 +21,44 @@
     return (normed * (1.0 + scale) + shift).astype(jnp.bfloat16)
 
 
-def start_sends(sends, gots, send_sem, recv_sem, local_sem, shards):
+def enter(shards):
     me = lax.axis_index("ctx")
     region = lax.axis_index("region")
-    mesh_id = pl.DeviceIdType.MESH
     barrier = pltpu.get_barrier_semaphore()
     for d in range(1, shards):
         peer = lax.rem(me + d, shards)
-        pl.semaphore_signal(barrier, 1, device_id=(region, peer), device_id_type=mesh_id)
+        pl.semaphore_signal(
+            barrier, 1, device_id=(region, peer), device_id_type=pl.DeviceIdType.MESH
+        )
     pl.semaphore_wait(barrier, shards - 1)
+
+
+def start_array(a, send, got, send_sem, recv_sem, local_sem, shards):
+    me = lax.axis_index("ctx")
+    region = lax.axis_index("region")
+    local = pltpu.make_async_copy(send.at[me], got.at[me], local_sem.at[a])
+    local.start()
+    copies = [local]
+    for d in range(1, shards):
+        peer = lax.rem(me + d, shards)
+        remote = pltpu.make_async_remote_copy(
+            src_ref=send.at[peer],
+            dst_ref=got.at[me],
+            send_sem=send_sem.at[a, d - 1],
+            recv_sem=recv_sem.at[a, d - 1],
+            device_id=(region, peer),
+            device_id_type=pl.DeviceIdType.MESH,
+        )
+        remote.start()
+        copies.append(remote)
+    return copies
+
+
+def start_sends(sends, gots, send_sem, recv_sem, local_sem, shards):
+    enter(shards)
     copies = []
     for a in range(len(sends)):
-        local = pltpu.make_async_copy(sends[a].at[me], gots[a].at[me], local_sem.at[a])
-        local.start()
-        copies.append(local)
-    for d in range(1, shards):
-        peer = lax.rem(me + d, shards)
-        for a in range(len(sends)):
-            remote = pltpu.make_async_remote_copy(
-                src_ref=sends[a].at[peer],
-                dst_ref=gots[a].at[me],
-                send_sem=send_sem.at[a, d - 1],
-                recv_sem=recv_sem.at[a, d - 1],
-                device_id=(region, peer),
-                device_id_type=mesh_id,
-            )
-            remote.start()
-            copies.append(remote)
+        copies += start_array(a, sends[a], gots[a], send_sem, recv_sem, local_sem, shards)
     return copies
 
 
@@ -235,22 +246,25 @@
     sems = refs[3 * pair + 4 :]
     modulated = mod_ref[...]
 
-    def fill(h, dests):
+    def fill(h, dests, i):
+        out_t = lax.dot_general(
+            w_ref[i, h],
+            modulated,
+            (((1,), (1,)), ((), ())),
+            preferred_element_type=jnp.float32,
+        )
+        for p in range(shards):
+            piece = out_t[p * head_dim : (p + 1) * head_dim]
+            dests[i][p] = piece.astype(jnp.bfloat16)
+
+    enter(shards)
+    copies = []
+    for i in range(3):
+        fill(0, send0, i)
+        copies += start_array(i, send0[i], got0[i], *sems, shards)
+    for h in range(1, pair):
         for i in range(3):
-            out_t = lax.dot_general(
-                w_ref[i, h],
-                modulated,
-                (((1,), (1,)), ((), ())),
-                preferred_element_type=jnp.float32,
-            )
-            for p in range(shards):
-                piece = out_t[p * head_dim : (p + 1) * head_dim]
-                dests[i][p] = piece.astype(jnp.bfloat16)
-
-    fill(0, send0)
-    copies = start_sends(send0, got0, *sems, shards)
-    for h in range(1, pair):
-        fill(h, later[3 * (h - 1) : 3 * h])
+            fill(h, later[3 * (h - 1) : 3 * h], i)
     gate = jnp.dot(act_ref[...], wg_ref[...], preferred_element_type=jnp.float32)
     gate_ref[...] = (gate + bg_ref[...]).astype(gate_ref.dtype)
     for copy in copies:

time: 186 us -> 184 us (0.989)
  no operation moved by 1% of the time
where the time goes in v11:
time: 184 us; the launch traced here: 181 us
  Pallas kernels  96.8 us (53%)
  local copies, waits for them, and re-layouts  28.9 us (16%)
  blocking collectives  20.5 us (11%)
  matrix products  14.9 us (8%)
  waiting for transfers between devices  9.92 us (5%)
  starting transfers between devices  6.03 us (3%)
  other arithmetic  3.15 us (2%)
    pallas_call x2, Pallas kernels, attend_send(): pl.pallas_call(kernel, out_shape=out_shape, in_specs=[vmem_spec] * 3 + [a...  68.2 us
    pallas_call x1, Pallas kernels, project_send(): pl.pallas_call(kernel, out_shape=shapes * pair + [jax.ShapeDtypeStruct((r...  28.6 us
    all_to_all x1, blocking collectives, per_device(): lax.all_to_all(requests.reshape(owners, capacity), ('region', 'ctx'), spl...  20.5 us
    unnamed x13, local copies, waits for them, and re-layouts  11.5 us
    all_to_all x1, waiting for transfers between devices, per_device(): lax.all_to_all(served, ('region', 'ctx'), split_axis=0, concat_axis=0, ti...  9.92 us
    transpose x1, local copies, waits for them, and re-layouts, per_device(): w_t = w_qkv.reshape(width, 3, shards, pair, head_dim).transpose(1, 3, 2,...  7.11 us
    dot_general x1, matrix products, per_device(): jnp.dot(activated, w_ada[:, :2 * width], preferred_element_type=jnp.float32)  6.17 us
    all_to_all x1, starting transfers between devices, per_device(): lax.all_to_all(served, ('region', 'ctx'), split_axis=0, concat_axis=0, ti...  6.03 us
  transfers between devices with their start and end apart: 1, of which 1 were waited for; matrix products, arithmetic and copies ran while one was open for 13% of the time, Pallas kernels for 0%

profile of v11, /device:TPU:0, one launch (start us, length us, event | category | flops | bytes accessed | tf_op | source)
XLA Modules:
  0.0 181.0 jit_solution(11774159276842373647)
XLA Ops:
  0.0 0.8 compare_select_fusion.1
  0.9 3.6 %gather_fusion = s32[512]{0:T(512)S(1)} fusion(s32[16384]{0:T(1024)} %param.11, s32[1024]{0:T(1024)S(1)} %pad_clamp_fusion), kind=kCustom, calls=%fused_computation | custom fusion | bytes 6144 | tf_op jit(solution)/shard_map/gather | solution.py:327
  5.1 0.3 convert_reduce_fusion.1
  5.4 2.4 %scatter_custom_fusion = s32[1024]{0:T(1024)S(1)} fusion(s32[512]{0:T(512)S(1)} %bitcast.70, s32[512]{0:T(512)S(1)} %get-tuple-element.31, s32[]{:T(128)} %constant.41.clone.1), kind=kCustom, calls=%fused_computation.52 | custom fusion | bytes 4100 | tf_op jit(solution)/shard_map/scatter | solution.py:339
  7.9 0.1 all_to_all.9
  7.9 20.5 %all_to_all.14 = s32[128,1,8]{2,1,0:T(1,128)S(1)} all-to-all(s32[128,1,8]{2,1,0:T(1,128)S(1)} %bitcast.66), channel_id=1, replica_groups=mesh['region'=16,'ctx'=8] {'region','ctx'}, dimensions={0} | all-to-all | bytes 8192 | tf_op jit(solution)/shard_map/all_to_all | solution.py:340
  28.4 0.5 broadcast.238
  28.9 0.7 reduce.4
  29.6 0.1 eq.49
  29.7 2.2 %fusion.11 = bf16[128,8,1152]{2,1,0:T(8,128)(2,1)} fusion(bf16[128,1152]{1,0:T(8,128)(2,1)S(1)} %copy-done.4, s32[1024]{0:T(1024)S(1)} %eq.49), kind=kOutput, calls=%fused_computation.8 | convolution fusion | flops 303300608 | bytes 2658304 | tf_op jit(solution)/shard_map/dot_general | solution.py:352
  32.0 6.0 %all-to-all-start.1 = ((bf16[128,8,1152]{2,1,0:T(8,128)(2,1)}), bf16[128,8,1152]{2,1,0:T(8,128)(2,1)}, u32[]{:S(2)}, u32[]{:S(2)}) async-start(bf16[128,8,1152]{2,1,0:T(8,128)(2,1)} %fusion.11), calls=%async_computation.1 | async-start | bytes 4718592 | tf_op jit(solution)/shard_map/all_to_all | solution.py:356
  38.0 11.5 %copy.20 = bf16[1152,3456]{0,1:T(8,128)(2,1)} copy(bf16[1152,3456]{1,0:T(8,128)(2,1)} %param.16) | data formatting | bytes 15925248 | tf_op args[7]
  49.5 7.1 %copy.21 = bf16[3,2,8,72,1152]{4,3,2,1,0:T(8,128)(2,1)} copy(bf16[3,2,8,72,1152]{4,3,1,2,0:T(8,128)(2,1)} %bitcast.65) | data formatting | bytes 15925248 | tf_op jit(solution)/shard_map/transpose | solution.py:379
  56.6 3.6 %slice.22.wg_ref = bf16[1152,1152]{1,0:T(8,128)(2,1)} slice(bf16[1152,3456]{1,0:T(8,128)(2,1)} %param.14), slice={[0:1152], [2304:3456]} | slice | bytes 5308416 | tf_op jit(solution)/shard_map/slice | solution.py:371
  60.2 0.2 convert_reduce_fusion
  60.5 0.5 fusion.20
  61.0 9.9 %all-to-all-done.1 = bf16[128,8,1152]{2,1,0:T(8,128)(2,1)} async-done(((bf16[128,8,1152]{2,1,0:T(8,128)(2,1)}), bf16[128,8,1152]{2,1,0:T(8,128)(2,1)}, u32[]{:S(2)}, u32[]{:S(2)}) %all-to-all-start.1) | async-done | bytes 2359328 | tf_op jit(solution)/shard_map/all_to_all | solution.py:356
  70.9 3.5 %select_convert_fusion.act_ref = bf16[512,1152]{1,0:T(8,128)(2,1)S(1)} fusion(bf16[128,8,1152]{2,1,0:T(8,128)(2,1)} %all-to-all-done.1, pred[512]{0:T(512)(128)(4,1)S(1)} %iota_compare_fusion.5, s32[512]{0:T(512)S(1)} %select_minimum_fusion), kind=kOutput, calls=%fused_computation.27 | convolution fusion | flops 1212022784 | bytes 3541504 | tf_op jit(solution)/shard_map/dot_general | solution.py:360
  74.4 6.2 %fusion.8 = f32[512,2304]{1,0:T(8,128)S(1)} fusion(bf16[512,1152]{1,0:T(8,128)(2,1)S(1)} %select_convert_fusion.act_ref, bf16[1152,3456]{1,0:T(8,128)(2,1)} %param.14, f32[2304]{0:T(1024)S(1)} %slice-done), kind=kOutput, calls=%fused_computation.6 | convolution fusion | flops 2721447936 | bytes 11215872 | tf_op jit(solution)/shard_map/dot_general | solution.py:367
  80.6 0.6 fusion.23.mod_ref
  81.2 28.6 %shard_map.91 = (bf16[8,72,512]{2,1,0:T(8,128)(2,1)S(1)}, bf16[8,72,512]{2,1,0:T(8,128)(2,1)S(1)}, bf16[8,72,512]{2,1,0:T(8,128)(2,1)S(1)}, bf16[8,72,512]{2,1,0...) custom-call(bf16[512,1152]{1,0:T(8,128)(2,1)S(1)} %fusion.23.mod_ref, ...), custom_call_target="tpu_custom_call" | custom-call | tf_op jit(solution)/shard_map/pallas_call | solution.py:283
  109.8 32.9 %shard_map.92 = (bf16[8,72,512]{2,1,0:T(8,128)(2,1)S(1)}, bf16[8,72,512]{2,1,0:T(8,128)(2,1)S(1)}, bf16[8,72,512]{2,1,0:T(8,128)(2,1)S(1)}, bf16[8,72,512]{2,1,0:T(8,128)(2,1)S(1)}) custom-call(bf16[8,72,512]{2,1,0:T(8,128)(2,1)S(1)} %get-tuple-element.19.refs_0_, bf16[8,72,512]{2,1,0:T(8,128)(2,1)S(1)} %get-tuple-element.20.refs_1_, ...), custom_call_target="tpu_custom_call" | custom-call | tf_op jit(solution)/shard_map/pallas_call | solution.py:226
  142.7 35.3 %shard_map.93 = (bf16[8,72,512]{2,1,0:T(8,128)(2,1)}, bf16[8,72,512]{2,1,0:T(8,128)(2,1)S(1)}, bf16[8,72,512]{2,1,0:T(8,128)(2,1)S(1)}) custom-call(bf16[8,72,512]{2,1,0:T(8,128)(2,1)S(1)} %get-tuple-element.25.refs_0_, bf16[8,72,512]{2,1,0:T(8,128)(2,1)S(1)} %get-tuple-element.26.refs_1_, bf16[8,72,512]{2,1,0:T(8,128)(2,1)S(1)} %get-tuple-element.27.refs_2_, ...), custom_call_target="tpu_custom_call" | custom-call | tf_op jit(solution)/shard_map/pallas_call | solution.py:226
  178.0 3.0 %fusion.18 = bf16[1,512,1152]{2,1,0:T(8,128)(2,1)} fusion(bf16[1,512,1152]{2,1,0:T(8,128)(2,1)S(1)} %copy-done.2, bf16[8,2,72,1152]{3,2,1,0:T(8,128)(2,1)S(1)} %bitcast.61, bf16[512,1152]{1,0:T(8,128)(2,1)S(1)} %get-tuple-element.18, bf16[8,1,72,512]{3,2,0,1:T(8,128)(2,1)S(1)} %bitcast.63, bf16[8,1,72,512]{3,2,0,1:T(8,128)(2,1)S(1)} %bitcast.62), kind=kOutput, calls=%fused_computation.18 | convolution fusion | flops 1362493440 | bytes 7372800 | tf_op jit(solution)/shard_map/phet,pheD->tD/dot_general | solution.py:386
  (23 shorter events, 0.1 us)
Async XLA Ops:
  0.0 178.0 %copy-start = (bf16[1152,1152]{1,0:T(8,128)(2,1)S(1)}, bf16[1152,1152]{1,0:T(8,128)(2,1)}, u32[]{:S(2)}) copy-start(bf16[1152,1152]{1,0:T(8,128)(2,1)} %param.17) | copy-start | bytes 7962628
  0.0 29.7 %copy-start.4 = (bf16[128,1152]{1,0:T(8,128)(2,1)S(1)}, bf16[128,1152]{1,0:T(8,128)(2,1)}, u32[]{:S(2)}) copy-start(bf16[128,1152]{1,0:T(8,128)(2,1)} %param.13) | copy-start | bytes 884740
  32.0 6.0 %copy-start.5 = (f32[3456]{0:T(1024)S(1)}, f32[3456]{0:T(1024)}, u32[]{:S(2)}) copy-start(f32[3456]{0:T(1024)} %param.15) | copy-start | bytes 41476
  32.0 38.9 %all-to-all-start.1 = ((bf16[128,8,1152]{2,1,0:T(8,128)(2,1)}), bf16[128,8,1152]{2,1,0:T(8,128)(2,1)}, u32[]{:S(2)}, u32[]{:S(2)}) async-start(bf16[128,8,1152]{2,1,0:T(8,128)(2,1)} %fusion.11), calls=%async_computation.1 | async-start | bytes 4718592 | tf_op jit(solution)/shard_map/all_to_all | solution.py:356
  56.6 3.6 %copy-start.1 = (bf16[1,512,1152]{2,1,0:T(8,128)(2,1)S(1)}, bf16[1,512,1152]{2,1,0:T(8,128)(2,1)}, u32[]{:S(2)}) copy-start(bf16[1,512,1152]{2,1,0:T(8,128)(2,1)} %param.9) | copy-start | bytes 3538948
  61.0 13.4 %slice-start = ((f32[3456]{0:T(1024)}), f32[2304]{0:T(1024)S(1)}, s32[]{:S(2)}) async-start(f32[3456]{0:T(1024)} %param.15), calls=%async_computation.2 | async-start | bytes 24576 | tf_op jit(solution)/shard_map/slice | solution.py:368
  74.4 6.2 %copy-start.3 = (bf16[512,1152]{1,0:T(8,128)(2,1)}, bf16[512,1152]{1,0:T(8,128)(2,1)S(1)}, u32[]{:S(2)}) copy-start(bf16[512,1152]{1,0:T(8,128)(2,1)S(1)} %select_convert_fusion.act_ref) | copy-start | bytes 3538948
  74.4 6.2 %copy-start.2 = (bf16[1,512,1152]{2,1,0:T(8,128)(2,1)S(1)}, bf16[1,512,1152]{2,1,0:T(8,128)(2,1)}, u32[]{:S(2)}) copy-start(bf16[1,512,1152]{2,1,0:T(8,128)(2,1)} %param.9) | copy-start | bytes 3538948

commit v12 on v11

--- a/solution.py
+++ b/solution.py
@@ -99,7 +99,10 @@
     for c in range(blocks):
         k_ref[c] = kt_ref[c].astype(jnp.float32).T.astype(k_ref.dtype)
 
-    def one_block(b, carry):
+    me = lax.axis_index("ctx")
+
+    def one_block(j, carry):
+        b = lax.rem(j + me + 1, blocks)
         qt = qt_ref[b]
 
         def score(c, m):

time: 184 us -> 180 us (0.978); the launches traced: 181 us -> 179 us
  no operation moved by 1% of the time
where the time goes in v12:
time: 180 us; the launch traced here: 179 us
  Pallas kernels  95 us (53%)
  local copies, waits for them, and re-layouts  28.9 us (16%)
  blocking collectives  20.5 us (11%)
  matrix products  14.9 us (8%)
  waiting for transfers between devices  9.92 us (6%)
  starting transfers between devices  6.03 us (3%)
  other arithmetic  3.15 us (2%)
    pallas_call x2, Pallas kernels, attend_send(): pl.pallas_call(kernel, out_shape=out_shape, in_specs=[vmem_spec] * 3 + [a...  66.4 us
    pallas_call x1, Pallas kernels, project_send(): pl.pallas_call(kernel, out_shape=shapes * pair + [jax.ShapeDtypeStruct((r...  28.6 us
    all_to_all x1, blocking collectives, per_device(): lax.all_to_all(requests.reshape(owners, capacity), ('region', 'ctx'), spl...  20.5 us
    unnamed x13, local copies, waits for them, and re-layouts  11.5 us
    all_to_all x1, waiting for transfers between devices, per_device(): lax.all_to_all(served, ('region', 'ctx'), split_axis=0, concat_axis=0, ti...  9.92 us
    transpose x1, local copies, waits for them, and re-layouts, per_device(): w_t = w_qkv.reshape(width, 3, shards, pair, head_dim).transpose(1, 3, 2,...  7.11 us
    dot_general x1, matrix products, per_device(): jnp.dot(activated, w_ada[:, :2 * width], preferred_element_type=jnp.float32)  6.17 us
    all_to_all x1, starting transfers between devices, per_device(): lax.all_to_all(served, ('region', 'ctx'), split_axis=0, concat_axis=0, ti...  6.03 us
  transfers between devices with their start and end apart: 1, of which 1 were waited for; matrix products, arithmetic and copies ran while one was open for 13% of the time, Pallas kernels for 0%

profile of v12, /device:TPU:0, one launch (start us, length us, event | category | flops | bytes accessed | tf_op | source)
XLA Modules:
  0.0 179.2 jit_solution(15246020898980347952)
XLA Ops:
  0.0 0.8 compare_select_fusion.1
  0.9 3.6 %gather_fusion = s32[512]{0:T(512)S(1)} fusion(s32[16384]{0:T(1024)} %param.11, s32[1024]{0:T(1024)S(1)} %pad_clamp_fusion), kind=kCustom, calls=%fused_computation | custom fusion | bytes 6144 | tf_op jit(solution)/shard_map/gather | solution.py:330
  5.1 0.3 convert_reduce_fusion.1
  5.4 2.4 %scatter_custom_fusion = s32[1024]{0:T(1024)S(1)} fusion(s32[512]{0:T(512)S(1)} %bitcast.70, s32[512]{0:T(512)S(1)} %get-tuple-element.31, s32[]{:T(128)} %constant.41.clone.1), kind=kCustom, calls=%fused_computation.52 | custom fusion | bytes 4100 | tf_op jit(solution)/shard_map/scatter | solution.py:342
  7.9 0.1 all_to_all.9
  7.9 20.5 %all_to_all.14 = s32[128,1,8]{2,1,0:T(1,128)S(1)} all-to-all(s32[128,1,8]{2,1,0:T(1,128)S(1)} %bitcast.66), channel_id=1, replica_groups=mesh['region'=16,'ctx'=8] {'region','ctx'}, dimensions={0} | all-to-all | bytes 8192 | tf_op jit(solution)/shard_map/all_to_all | solution.py:343
  28.4 0.5 broadcast.238
  28.9 0.7 reduce.4
  29.6 0.1 eq.49
  29.7 2.2 %fusion.11 = bf16[128,8,1152]{2,1,0:T(8,128)(2,1)} fusion(bf16[128,1152]{1,0:T(8,128)(2,1)S(1)} %copy-done.4, s32[1024]{0:T(1024)S(1)} %eq.49), kind=kOutput, calls=%fused_computation.8 | convolution fusion | flops 303300608 | bytes 2658304 | tf_op jit(solution)/shard_map/dot_general | solution.py:355
  32.0 6.0 %all-to-all-start.1 = ((bf16[128,8,1152]{2,1,0:T(8,128)(2,1)}), bf16[128,8,1152]{2,1,0:T(8,128)(2,1)}, u32[]{:S(2)}, u32[]{:S(2)}) async-start(bf16[128,8,1152]{2,1,0:T(8,128)(2,1)} %fusion.11), calls=%async_computation.1 | async-start | bytes 4718592 | tf_op jit(solution)/shard_map/all_to_all | solution.py:359
  38.0 11.5 %copy.20 = bf16[1152,3456]{0,1:T(8,128)(2,1)} copy(bf16[1152,3456]{1,0:T(8,128)(2,1)} %param.16) | data formatting | bytes 15925248 | tf_op args[7]
  49.5 7.1 %copy.21 = bf16[3,2,8,72,1152]{4,3,2,1,0:T(8,128)(2,1)} copy(bf16[3,2,8,72,1152]{4,3,1,2,0:T(8,128)(2,1)} %bitcast.65) | data formatting | bytes 15925248 | tf_op jit(solution)/shard_map/transpose | solution.py:382
  56.6 3.6 %slice.22.wg_ref = bf16[1152,1152]{1,0:T(8,128)(2,1)} slice(bf16[1152,3456]{1,0:T(8,128)(2,1)} %param.14), slice={[0:1152], [2304:3456]} | slice | bytes 5308416 | tf_op jit(solution)/shard_map/slice | solution.py:374
  60.2 0.2 convert_reduce_fusion
  60.5 0.5 fusion.20
  61.0 9.9 %all-to-all-done.1 = bf16[128,8,1152]{2,1,0:T(8,128)(2,1)} async-done(((bf16[128,8,1152]{2,1,0:T(8,128)(2,1)}), bf16[128,8,1152]{2,1,0:T(8,128)(2,1)}, u32[]{:S(2)}, u32[]{:S(2)}) %all-to-all-start.1) | async-done | bytes 2359328 | tf_op jit(solution)/shard_map/all_to_all | solution.py:359
  70.9 3.5 %select_convert_fusion.act_ref = bf16[512,1152]{1,0:T(8,128)(2,1)S(1)} fusion(bf16[128,8,1152]{2,1,0:T(8,128)(2,1)} %all-to-all-done.1, pred[512]{0:T(512)(128)(4,1)S(1)} %iota_compare_fusion.5, s32[512]{0:T(512)S(1)} %select_minimum_fusion), kind=kOutput, calls=%fused_computation.27 | convolution fusion | flops 1212022784 | bytes 3541504 | tf_op jit(solution)/shard_map/dot_general | solution.py:363
  74.4 6.2 %fusion.8 = f32[512,2304]{1,0:T(8,128)S(1)} fusion(bf16[512,1152]{1,0:T(8,128)(2,1)S(1)} %select_convert_fusion.act_ref, bf16[1152,3456]{1,0:T(8,128)(2,1)} %param.14, f32[2304]{0:T(1024)S(1)} %slice-done), kind=kOutput, calls=%fused_computation.6 | convolution fusion | flops 2721447936 | bytes 11215872 | tf_op jit(solution)/shard_map/dot_general | solution.py:370
  80.6 0.6 fusion.23.mod_ref
  81.2 28.6 %shard_map.91 = (bf16[8,72,512]{2,1,0:T(8,128)(2,1)S(1)}, bf16[8,72,512]{2,1,0:T(8,128)(2,1)S(1)}, bf16[8,72,512]{2,1,0:T(8,128)(2,1)S(1)}, bf16[8,72,512]{2,1,0...) custom-call(bf16[512,1152]{1,0:T(8,128)(2,1)S(1)} %fusion.23.mod_ref, ...), custom_call_target="tpu_custom_call" | custom-call | tf_op jit(solution)/shard_map/pallas_call | solution.py:286
  109.8 32.9 %shard_map.92 = (bf16[8,72,512]{2,1,0:T(8,128)(2,1)S(1)}, bf16[8,72,512]{2,1,0:T(8,128)(2,1)S(1)}, bf16[8,72,512]{2,1,0:T(8,128)(2,1)S(1)}, bf16[8,72,512]{2,1,0:T(8,128)(2,1)S(1)}) custom-call(bf16[8,72,512]{2,1,0:T(8,128)(2,1)S(1)} %get-tuple-element.19.refs_0_, bf16[8,72,512]{2,1,0:T(8,128)(2,1)S(1)} %get-tuple-element.20.refs_1_, ...), custom_call_target="tpu_custom_call" | custom-call | tf_op jit(solution)/shard_map/pallas_call | solution.py:229
  142.7 33.5 %shard_map.93 = (bf16[8,72,512]{2,1,0:T(8,128)(2,1)}, bf16[8,72,512]{2,1,0:T(8,128)(2,1)S(1)}, bf16[8,72,512]{2,1,0:T(8,128)(2,1)S(1)}) custom-call(bf16[8,72,512]{2,1,0:T(8,128)(2,1)S(1)} %get-tuple-element.25.refs_0_, bf16[8,72,512]{2,1,0:T(8,128)(2,1)S(1)} %get-tuple-element.26.refs_1_, bf16[8,72,512]{2,1,0:T(8,128)(2,1)S(1)} %get-tuple-element.27.refs_2_, ...), custom_call_target="tpu_custom_call" | custom-call | tf_op jit(solution)/shard_map/pallas_call | solution.py:229
  176.2 3.0 %fusion.18 = bf16[1,512,1152]{2,1,0:T(8,128)(2,1)} fusion(bf16[1,512,1152]{2,1,0:T(8,128)(2,1)S(1)} %copy-done.2, bf16[8,2,72,1152]{3,2,1,0:T(8,128)(2,1)S(1)} %bitcast.61, bf16[512,1152]{1,0:T(8,128)(2,1)S(1)} %get-tuple-element.18, bf16[8,1,72,512]{3,2,0,1:T(8,128)(2,1)S(1)} %bitcast.63, bf16[8,1,72,512]{3,2,0,1:T(8,128)(2,1)S(1)} %bitcast.62), kind=kOutput, calls=%fused_computation.18 | convolution fusion | flops 1362493440 | bytes 7372800 | tf_op jit(solution)/shard_map/phet,pheD->tD/dot_general | solution.py:389
  (23 shorter events, 0.1 us)
Async XLA Ops:
  0.0 176.2 %copy-start = (bf16[1152,1152]{1,0:T(8,128)(2,1)S(1)}, bf16[1152,1152]{1,0:T(8,128)(2,1)}, u32[]{:S(2)}) copy-start(bf16[1152,1152]{1,0:T(8,128)(2,1)} %param.17) | copy-start | bytes 7962628
  0.0 29.7 %copy-start.4 = (bf16[128,1152]{1,0:T(8,128)(2,1)S(1)}, bf16[128,1152]{1,0:T(8,128)(2,1)}, u32[]{:S(2)}) copy-start(bf16[128,1152]{1,0:T(8,128)(2,1)} %param.13) | copy-start | bytes 884740
  32.0 6.0 %copy-start.5 = (f32[3456]{0:T(1024)S(1)}, f32[3456]{0:T(1024)}, u32[]{:S(2)}) copy-start(f32[3456]{0:T(1024)} %param.15) | copy-start | bytes 41476
  32.0 38.9 %all-to-all-start.1 = ((bf16[128,8,1152]{2,1,0:T(8,128)(2,1)}), bf16[128,8,1152]{2,1,0:T(8,128)(2,1)}, u32[]{:S(2)}, u32[]{:S(2)}) async-start(bf16[128,8,1152]{2,1,0:T(8,128)(2,1)} %fusion.11), calls=%async_computation.1 | async-start | bytes 4718592 | tf_op jit(solution)/shard_map/all_to_all | solution.py:359
  56.6 3.6 %copy-start.1 = (bf16[1,512,1152]{2,1,0:T(8,128)(2,1)S(1)}, bf16[1,512,1152]{2,1,0:T(8,128)(2,1)}, u32[]{:S(2)}) copy-start(bf16[1,512,1152]{2,1,0:T(8,128)(2,1)} %param.9) | copy-start | bytes 3538948
  61.0 13.4 %slice-start = ((f32[3456]{0:T(1024)}), f32[2304]{0:T(1024)S(1)}, s32[]{:S(2)}) async-start(f32[3456]{0:T(1024)} %param.15), calls=%async_computation.2 | async-start | bytes 24576 | tf_op jit(solution)/shard_map/slice | solution.py:371
  74.4 6.2 %copy-start.3 = (bf16[512,1152]{1,0:T(8,128)(2,1)}, bf16[512,1152]{1,0:T(8,128)(2,1)S(1)}, u32[]{:S(2)}) copy-start(bf16[512,1152]{1,0:T(8,128)(2,1)S(1)} %select_convert_fusion.act_ref) | copy-start | bytes 3538948
  74.4 6.2 %copy-start.2 = (bf16[1,512,1152]{2,1,0:T(8,128)(2,1)S(1)}, bf16[1,512,1152]{2,1,0:T(8,128)(2,1)}, u32[]{:S(2)}) copy-start(bf16[1,512,1152]{2,1,0:T(8,128)(2,1)} %param.9) | copy-start | bytes 3538948

commit v13 on v12

--- a/solution.py
+++ b/solution.py
@@ -340,13 +340,9 @@
     place_rank = jnp.sum(earlier.astype(jnp.int32), axis=1)
     target = jnp.where(solid, owner_index * capacity + place_rank, owners * capacity)
     requests = jnp.zeros((owners * capacity,), jnp.int32).at[target].set(local_row, mode="drop")
-    asked = lax.all_to_all(
-        requests.reshape(owners, capacity),
-        ("region", "ctx"),
-        split_axis=0,
-        concat_axis=0,
-        tiled=True,
-    ).reshape(-1)
+    by_owner = requests.reshape(owners // shards, shards, capacity)
+    by_owner = lax.all_to_all(by_owner, "ctx", split_axis=1, concat_axis=1, tiled=True)
+    asked = lax.all_to_all(by_owner, "region", split_axis=0, concat_axis=0, tiled=True).reshape(-1)
     pick_at = jnp.minimum(target, owners * capacity - 1)
     served_hot = (asked[:, None] == jnp.arange(elem_rows, dtype=jnp.int32)[None, :]).astype(
         jnp.bfloat16

time: 180 us -> 186 us (1.033)
  blocking collectives: 20.5 us -> 26.5 us
    all_to_all x1 -> x2, blocking collectives: 20.5 us -> 26.5 us  [the longest x1 14.2 us: per_device(): lax.all_to_all(by_owner, 'region', split_axis=0, concat_axis=0, tiled=True)]
    unnamed x13 -> x15, local copies, waits for them, and re-layouts: 11.5 us -> 11.7 us
  transfers between devices with their start and end apart: 1 -> 1, of which waited for: 1 -> 1; matrix products, arithmetic and copies ran while one was open for 13% -> 12% of each run, Pallas kernels for 0% -> 0%
where the time goes in v13:
time: 186 us; the launch traced here: 185 us
  Pallas kernels  95 us (51%)
  local copies, waits for them, and re-layouts  29.3 us (16%)
  blocking collectives  26.5 us (14%)
  matrix products  14.9 us (8%)
  waiting for transfers between devices  9.92 us (5%)
  starting transfers between devices  6.03 us (3%)
  other arithmetic  3 us (2%)
    pallas_call x2, Pallas kernels, attend_send(): pl.pallas_call(kernel, out_shape=out_shape, in_specs=[vmem_spec] * 3 + [a...  66.4 us
    pallas_call x1, Pallas kernels, project_send(): pl.pallas_call(kernel, out_shape=shapes * pair + [jax.ShapeDtypeStruct((r...  28.6 us
    all_to_all x1, blocking collectives, per_device(): lax.all_to_all(by_owner, 'region', split_axis=0, concat_axis=0, tiled=True)  14.2 us
    all_to_all x1, blocking collectives, per_device(): lax.all_to_all(by_owner, 'ctx', split_axis=1, concat_axis=1, tiled=True)  12.3 us
    unnamed x15, local copies, waits for them, and re-layouts  11.7 us
    all_to_all x1, waiting for transfers between devices, per_device(): lax.all_to_all(served, ('region', 'ctx'), split_axis=0, concat_axis=0, ti...  9.92 us
    transpose x1, local copies, waits for them, and re-layouts, per_device(): w_t = w_qkv.reshape(width, 3, shards, pair, head_dim).transpose(1, 3, 2,...  7.11 us
    dot_general x1, matrix products, per_device(): jnp.dot(activated, w_ada[:, :2 * width], preferred_element_type=jnp.float32)  6.17 us
  transfers between devices with their start and end apart: 1, of which 1 were waited for; matrix products, arithmetic and copies ran while one was open for 12% of the time, Pallas kernels for 0%

profile of v13, /device:TPU:0, one launch (start us, length us, event | category | flops | bytes accessed | tf_op | source)
XLA Modules:
  0.0 185.4 jit_solution(15256272577891289861)
XLA Ops:
  0.0 0.8 compare_select_fusion.1
  0.9 3.6 %gather_fusion = s32[512]{0:T(512)S(1)} fusion(s32[16384]{0:T(1024)} %param.11, s32[1024]{0:T(1024)S(1)} %pad_clamp_fusion), kind=kCustom, calls=%fused_computation | custom fusion | bytes 6144 | tf_op jit(solution)/shard_map/gather | solution.py:330
  5.1 0.3 convert_reduce_fusion.1
  5.4 2.4 %scatter_custom_fusion = s32[1024]{0:T(1024)S(1)} fusion(s32[512]{0:T(512)S(1)} %bitcast.72, s32[512]{0:T(512)S(1)} %get-tuple-element.31, s32[]{:T(128)} %constant.41.clone.1), kind=kCustom, calls=%fused_computation.52 | custom fusion | bytes 4100 | tf_op jit(solution)/shard_map/scatter | solution.py:342
  8.1 12.3 %all_to_all.15 = s32[8,1,128]{2,1,0:T(1,128)S(1)} all-to-all(s32[8,1,128]{2,1,0:T(1,128)S(1)} %reshape.196), channel_id=1, replica_groups=mesh['region'=16,'ctx'=8] {'ctx'}, dimensions={0} | all-to-all | bytes 8192 | tf_op jit(solution)/shard_map/all_to_all | solution.py:344
  20.4 0.5 broadcast.235
  20.9 0.6 reduce.1
  21.5 0.1 copy.26
  21.6 14.2 %all_to_all.16 = s32[16,8,8]{2,1,0:T(8,128)S(1)} all-to-all(s32[16,8,8]{2,1,0:T(8,128)S(1)} %copy.26), channel_id=1, replica_groups=mesh['region'=16,'ctx'=8] {'region'}, dimensions={0} | all-to-all | bytes 8192 | tf_op jit(solution)/shard_map/all_to_all | solution.py:345
  36.0 2.2 %fusion.11 = bf16[128,8,1152]{2,1,0:T(8,128)(2,1)} fusion(bf16[128,1152]{1,0:T(8,128)(2,1)S(1)} %copy-done.4, s32[1024]{0:T(1024)S(1)} %eq.49), kind=kOutput, calls=%fused_computation.8 | convolution fusion | flops 303300608 | bytes 2658304 | tf_op jit(solution)/shard_map/dot_general | solution.py:351
  38.2 6.0 %all-to-all-start.2 = ((bf16[128,8,1152]{2,1,0:T(8,128)(2,1)}), bf16[128,8,1152]{2,1,0:T(8,128)(2,1)}, u32[]{:S(2)}, u32[]{:S(2)}) async-start(bf16[128,8,1152]{2,1,0:T(8,128)(2,1)} %fusion.11), calls=%async_computation.2 | async-start | bytes 4718592 | tf_op jit(solution)/shard_map/all_to_all | solution.py:355
  44.2 11.5 %copy.27 = bf16[1152,3456]{0,1:T(8,128)(2,1)} copy(bf16[1152,3456]{1,0:T(8,128)(2,1)} %param.16) | data formatting | bytes 15925248 | tf_op args[7]
  55.7 7.1 %copy.28 = bf16[3,2,8,72,1152]{4,3,2,1,0:T(8,128)(2,1)} copy(bf16[3,2,8,72,1152]{4,3,1,2,0:T(8,128)(2,1)} %bitcast.66) | data formatting | bytes 15925248 | tf_op jit(solution)/shard_map/transpose | solution.py:378
  62.8 3.6 %slice.22.wg_ref = bf16[1152,1152]{1,0:T(8,128)(2,1)} slice(bf16[1152,3456]{1,0:T(8,128)(2,1)} %param.14), slice={[0:1152], [2304:3456]} | slice | bytes 5308416 | tf_op jit(solution)/shard_map/slice | solution.py:370
  66.5 0.2 convert_reduce_fusion
  66.7 0.5 fusion.20
  67.2 9.9 %all-to-all-done.2 = bf16[128,8,1152]{2,1,0:T(8,128)(2,1)} async-done(((bf16[128,8,1152]{2,1,0:T(8,128)(2,1)}), bf16[128,8,1152]{2,1,0:T(8,128)(2,1)}, u32[]{:S(2)}, u32[]{:S(2)}) %all-to-all-start.2) | async-done | bytes 2359328 | tf_op jit(solution)/shard_map/all_to_all | solution.py:355
  77.1 3.5 %select_convert_fusion.act_ref = bf16[512,1152]{1,0:T(8,128)(2,1)S(1)} fusion(bf16[128,8,1152]{2,1,0:T(8,128)(2,1)} %all-to-all-done.2, pred[512]{0:T(512)(128)(4,1)S(1)} %iota_compare_fusion.5, s32[512]{0:T(512)S(1)} %select_minimum_fusion), kind=kOutput, calls=%fused_computation.27 | convolution fusion | flops 1212022784 | bytes 3541504 | tf_op jit(solution)/shard_map/dot_general | solution.py:359
  80.6 6.2 %fusion.8 = f32[512,2304]{1,0:T(8,128)S(1)} fusion(bf16[512,1152]{1,0:T(8,128)(2,1)S(1)} %select_convert_fusion.act_ref, bf16[1152,3456]{1,0:T(8,128)(2,1)} %param.14, f32[2304]{0:T(1024)S(1)} %slice-done), kind=kOutput, calls=%fused_computation.6 | convolution fusion | flops 2721447936 | bytes 11215872 | tf_op jit(solution)/shard_map/dot_general | solution.py:366
  86.8 0.6 fusion.23.mod_ref
  87.4 28.6 %shard_map.91 = (bf16[8,72,512]{2,1,0:T(8,128)(2,1)S(1)}, bf16[8,72,512]{2,1,0:T(8,128)(2,1)S(1)}, bf16[8,72,512]{2,1,0:T(8,128)(2,1)S(1)}, bf16[8,72,512]{2,1,0...) custom-call(bf16[512,1152]{1,0:T(8,128)(2,1)S(1)} %fusion.23.mod_ref, ...), custom_call_target="tpu_custom_call" | custom-call | tf_op jit(solution)/shard_map/pallas_call | solution.py:286
  116.0 32.9 %shard_map.92 = (bf16[8,72,512]{2,1,0:T(8,128)(2,1)S(1)}, bf16[8,72,512]{2,1,0:T(8,128)(2,1)S(1)}, bf16[8,72,512]{2,1,0:T(8,128)(2,1)S(1)}, bf16[8,72,512]{2,1,0:T(8,128)(2,1)S(1)}) custom-call(bf16[8,72,512]{2,1,0:T(8,128)(2,1)S(1)} %get-tuple-element.19.refs_0_, bf16[8,72,512]{2,1,0:T(8,128)(2,1)S(1)} %get-tuple-element.20.refs_1_, ...), custom_call_target="tpu_custom_call" | custom-call | tf_op jit(solution)/shard_map/pallas_call | solution.py:229
  148.9 33.5 %shard_map.93 = (bf16[8,72,512]{2,1,0:T(8,128)(2,1)}, bf16[8,72,512]{2,1,0:T(8,128)(2,1)S(1)}, bf16[8,72,512]{2,1,0:T(8,128)(2,1)S(1)}) custom-call(bf16[8,72,512]{2,1,0:T(8,128)(2,1)S(1)} %get-tuple-element.25.refs_0_, bf16[8,72,512]{2,1,0:T(8,128)(2,1)S(1)} %get-tuple-element.26.refs_1_, bf16[8,72,512]{2,1,0:T(8,128)(2,1)S(1)} %get-tuple-element.27.refs_2_, ...), custom_call_target="tpu_custom_call" | custom-call | tf_op jit(solution)/shard_map/pallas_call | solution.py:229
  182.4 3.0 %fusion.18 = bf16[1,512,1152]{2,1,0:T(8,128)(2,1)} fusion(bf16[1,512,1152]{2,1,0:T(8,128)(2,1)S(1)} %copy-done.2, bf16[8,2,72,1152]{3,2,1,0:T(8,128)(2,1)S(1)} %bitcast.62, bf16[512,1152]{1,0:T(8,128)(2,1)S(1)} %get-tuple-element.18, bf16[8,1,72,512]{3,2,0,1:T(8,128)(2,1)S(1)} %bitcast.64, bf16[8,1,72,512]{3,2,0,1:T(8,128)(2,1)S(1)} %bitcast.63), kind=kOutput, calls=%fused_computation.18 | convolution fusion | flops 1362493440 | bytes 7372800 | tf_op jit(solution)/shard_map/phet,pheD->tD/dot_general | solution.py:385
  (28 shorter events, 0.5 us)
Async XLA Ops:
  0.0 182.4 %copy-start = (bf16[1152,1152]{1,0:T(8,128)(2,1)S(1)}, bf16[1152,1152]{1,0:T(8,128)(2,1)}, u32[]{:S(2)}) copy-start(bf16[1152,1152]{1,0:T(8,128)(2,1)} %param.17) | copy-start | bytes 7962628
  0.0 35.9 %copy-start.4 = (bf16[128,1152]{1,0:T(8,128)(2,1)S(1)}, bf16[128,1152]{1,0:T(8,128)(2,1)}, u32[]{:S(2)}) copy-start(bf16[128,1152]{1,0:T(8,128)(2,1)} %param.13) | copy-start | bytes 884740
  38.2 6.0 %copy-start.5 = (f32[3456]{0:T(1024)S(1)}, f32[3456]{0:T(1024)}, u32[]{:S(2)}) copy-start(f32[3456]{0:T(1024)} %param.15) | copy-start | bytes 41476
  38.2 38.9 %all-to-all-start.2 = ((bf16[128,8,1152]{2,1,0:T(8,128)(2,1)}), bf16[128,8,1152]{2,1,0:T(8,128)(2,1)}, u32[]{:S(2)}, u32[]{:S(2)}) async-start(bf16[128,8,1152]{2,1,0:T(8,128)(2,1)} %fusion.11), calls=%async_computation.2 | async-start | bytes 4718592 | tf_op jit(solution)/shard_map/all_to_all | solution.py:355
  62.8 3.6 %copy-start.1 = (bf16[1,512,1152]{2,1,0:T(8,128)(2,1)S(1)}, bf16[1,512,1152]{2,1,0:T(8,128)(2,1)}, u32[]{:S(2)}) copy-start(bf16[1,512,1152]{2,1,0:T(8,128)(2,1)} %param.9) | copy-start | bytes 3538948
  67.2 13.4 %slice-start = ((f32[3456]{0:T(1024)}), f32[2304]{0:T(1024)S(1)}, s32[]{:S(2)}) async-start(f32[3456]{0:T(1024)} %param.15), calls=%async_computation.3 | async-start | bytes 24576 | tf_op jit(solution)/shard_map/slice | solution.py:367
  80.6 6.2 %copy-start.3 = (bf16[512,1152]{1,0:T(8,128)(2,1)}, bf16[512,1152]{1,0:T(8,128)(2,1)S(1)}, u32[]{:S(2)}) copy-start(bf16[512,1152]{1,0:T(8,128)(2,1)S(1)} %select_convert_fusion.act_ref) | copy-start | bytes 3538948
  80.6 6.2 %copy-start.2 = (bf16[1,512,1152]{2,1,0:T(8,128)(2,1)S(1)}, bf16[1,512,1152]{2,1,0:T(8,128)(2,1)}, u32[]{:S(2)}) copy-start(bf16[1,512,1152]{2,1,0:T(8,128)(2,1)} %param.9) | copy-start | bytes 3538948

commit v14 on v13

--- a/solution.py
+++ b/solution.py
@@ -318,6 +318,65 @@
     return jnp.stack(backs, axis=1), gate
 
 
+def request_kernel(req_ref, asked_ref, send_sem, recv_sem, local_sem, *, groups, shards):
+    total = groups * shards
+    me = lax.axis_index("region") * shards + lax.axis_index("ctx")
+    mesh_id = pl.DeviceIdType.MESH
+    barrier = pltpu.get_barrier_semaphore()
+
+    def greet(d, carry):
+        peer = lax.rem(me + d, total)
+        pl.semaphore_signal(
+            barrier, 1, device_id=(peer // shards, peer % shards), device_id_type=mesh_id
+        )
+        return carry
+
+    lax.fori_loop(1, total, greet, 0)
+    pl.semaphore_wait(barrier, total - 1)
+    local = pltpu.make_async_copy(req_ref.at[me], asked_ref.at[me], local_sem.at[0])
+    local.start()
+
+    def remote(d):
+        peer = lax.rem(me + d, total)
+        return pltpu.make_async_remote_copy(
+            src_ref=req_ref.at[peer],
+            dst_ref=asked_ref.at[me],
+            send_sem=send_sem.at[d - 1],
+            recv_sem=recv_sem.at[d - 1],
+            device_id=(peer // shards, peer % shards),
+            device_id_type=mesh_id,
+        )
+
+    def launch(d, carry):
+        remote(d).start()
+        return carry
+
+    def finish(d, carry):
+        remote(d).wait()
+        return carry
+
+    lax.fori_loop(1, total, launch, 0)
+    local.wait()
+    lax.fori_loop(1, total, finish, 0)
+
+
+def exchange_requests(requests, groups, shards):
+    total = groups * shards
+    any_spec = pl.BlockSpec(memory_space=pl.ANY)
+    return pl.pallas_call(
+        functools.partial(request_kernel, groups=groups, shards=shards),
+        out_shape=jax.ShapeDtypeStruct(requests.shape, requests.dtype),
+        in_specs=[any_spec],
+        out_specs=any_spec,
+        scratch_shapes=[
+            pltpu.SemaphoreType.DMA((total - 1,)),
+            pltpu.SemaphoreType.DMA((total - 1,)),
+            pltpu.SemaphoreType.DMA((1,)),
+        ],
+        compiler_params=pltpu.CompilerParams(collective_id=7, has_side_effects=True),
+    )(requests)
+
+
 def per_device(
     tokens, element_ids, element_slot, live_count, cond_table, w_ada, b_ada, w_qkv, w_out
 ):
@@ -340,9 +399,9 @@
     place_rank = jnp.sum(earlier.astype(jnp.int32), axis=1)
     target = jnp.where(solid, owner_index * capacity + place_rank, owners * capacity)
     requests = jnp.zeros((owners * capacity,), jnp.int32).at[target].set(local_row, mode="drop")
-    by_owner = requests.reshape(owners // shards, shards, capacity)
-    by_owner = lax.all_to_all(by_owner, "ctx", split_axis=1, concat_axis=1, tiled=True)
-    asked = lax.all_to_all(by_owner, "region", split_axis=0, concat_axis=0, tiled=True).reshape(-1)
+    asked = exchange_requests(
+        requests.reshape(owners, capacity), owners // shards, shards
+    ).reshape(-1)
     pick_at = jnp.minimum(target, owners * capacity - 1)
     served_hot = (asked[:, None] == jnp.arange(elem_rows, dtype=jnp.int32)[None, :]).astype(
         jnp.bfloat16

time: 186 us -> 180 us (0.968)
  blocking collectives: 26.5 us -> 0 us
  Pallas kernels: 95 us -> 114 us
    all_to_all x2 -> x0, blocking collectives: 26.5 us -> none  [the longest x1 14.2 us: per_device(): lax.all_to_all(by_owner, 'region', split_axis=0, concat_axis=0, tiled=True)]
    pallas_call x0 -> x1, Pallas kernels: none -> 19.1 us  [exchange_requests(): pl.pallas_call(functools.partial(request_kernel, groups=groups, shards=sh...]
    unnamed x15 -> x13, local copies, waits for them, and re-layouts: 11.7 us -> 11.4 us
  transfers between devices with their start and end apart: 1 -> 1, of which waited for: 1 -> 1; matrix products, arithmetic and copies ran while one was open for 12% -> 13% of each run, Pallas kernels for 0% -> 0%
where the time goes in v14:
time: 180 us
  Pallas kernels  114 us (63%)
  local copies, waits for them, and re-layouts  29.8 us (17%)
  matrix products  14.9 us (8%)
  waiting for transfers between devices  9.99 us (6%)
  starting transfers between devices  7.47 us (4%)
  other arithmetic  2.43 us (1%)
    pallas_call x2, Pallas kernels, attend_send(): pl.pallas_call(kernel, out_shape=out_shape, in_specs=[vmem_spec] * 3 + [a...  66.4 us
    pallas_call x1, Pallas kernels, project_send(): pl.pallas_call(kernel, out_shape=shapes * pair + [jax.ShapeDtypeStruct((r...  28.6 us
    pallas_call x1, Pallas kernels, exchange_requests(): pl.pallas_call(functools.partial(request_kernel, groups=groups, shards=sh...  19.1 us
    unnamed x13, local copies, waits for them, and re-layouts  11.4 us
    all_to_all x1, waiting for transfers between devices, per_device(): lax.all_to_all(served, ('region', 'ctx'), split_axis=0, concat_axis=0, ti...  9.99 us
    all_to_all x1, starting transfers between devices, per_device(): lax.all_to_all(served, ('region', 'ctx'), split_axis=0, concat_axis=0, ti...  7.47 us
    transpose x1, local copies, waits for them, and re-layouts, per_device(): w_t = w_qkv.reshape(width, 3, shards, pair, head_dim).transpose(1, 3, 2,...  7.1 us
    dot_general x1, matrix products, per_device(): jnp.dot(activated, w_ada[:, :2 * width], preferred_element_type=jnp.float32)  6.17 us
  transfers between devices with their start and end apart: 1, of which 1 were waited for; matrix products, arithmetic and copies ran while one was open for 13% of the time, Pallas kernels for 0%

profile of v14, /device:TPU:0, one launch (start us, length us, event | category | flops | bytes accessed | tf_op | source)
XLA Modules:
  0.0 179.6 jit_solution(11514732415543727793)
XLA Ops:
  0.0 0.8 compare_select_fusion.1
  0.9 3.6 %gather_fusion = s32[512]{0:T(512)S(1)} fusion(s32[16384]{0:T(1024)} %param.11, s32[1024]{0:T(1024)S(1)} %pad_clamp_fusion), kind=kCustom, calls=%fused_computation | custom fusion | bytes 6144 | tf_op jit(solution)/shard_map/gather | solution.py:389
  5.1 0.3 convert_reduce_fusion.1
  5.4 2.4 %scatter_custom_fusion = s32[1024]{0:T(1024)S(1)} fusion(s32[512]{0:T(512)S(1)} %bitcast.68, s32[512]{0:T(512)S(1)} %get-tuple-element.31, s32[]{:T(128)} %constant.41.clone.1), kind=kCustom, calls=%fused_computation.52 | custom fusion | bytes 4100 | tf_op jit(solution)/shard_map/scatter | solution.py:401
  7.9 0.7 reshape.171.req_ref
  8.6 19.1 %shard_map.91 = s32[128,8]{1,0:T(8,128)} custom-call(s32[128,8]{1,0:T(8,128)} %reshape.171.req_ref), custom_call_target="tpu_custom_call" | custom-call | tf_op jit(solution)/shard_map/pallas_call | solution.py:366
  27.7 0.9 eq.49
  28.7 2.2 %fusion.11 = bf16[128,8,1152]{2,1,0:T(8,128)(2,1)} fusion(bf16[128,1152]{1,0:T(8,128)(2,1)S(1)} %copy-done.4, s32[1024]{0:T(1024)S(1)} %eq.49), kind=kOutput, calls=%fused_computation.8 | convolution fusion | flops 303300608 | bytes 2658304 | tf_op jit(solution)/shard_map/dot_general | solution.py:410
  30.9 7.5 %all-to-all-start = ((bf16[128,8,1152]{2,1,0:T(8,128)(2,1)}), bf16[128,8,1152]{2,1,0:T(8,128)(2,1)}, u32[]{:S(2)}, u32[]{:S(2)}) async-start(bf16[128,8,1152]{2,1,0:T(8,128)(2,1)} %fusion.11), calls=%async_computation | async-start | bytes 4718592 | tf_op jit(solution)/shard_map/all_to_all | solution.py:414
  38.4 11.4 %copy.15 = bf16[1152,3456]{0,1:T(8,128)(2,1)} copy(bf16[1152,3456]{1,0:T(8,128)(2,1)} %param.16) | data formatting | bytes 15925248 | tf_op args[7]
  49.8 7.1 %copy.16 = bf16[3,2,8,72,1152]{4,3,2,1,0:T(8,128)(2,1)} copy(bf16[3,2,8,72,1152]{4,3,1,2,0:T(8,128)(2,1)} %bitcast.64) | data formatting | bytes 15925248 | tf_op jit(solution)/shard_map/transpose | solution.py:437
  56.9 3.6 %slice.22.wg_ref = bf16[1152,1152]{1,0:T(8,128)(2,1)} slice(bf16[1152,3456]{1,0:T(8,128)(2,1)} %param.14), slice={[0:1152], [2304:3456]} | slice | bytes 5308416 | tf_op jit(solution)/shard_map/slice | solution.py:429
  60.5 0.2 convert_reduce_fusion
  60.8 0.5 fusion.20
  61.3 0.0 slice-start
  61.3 10.0 %all-to-all-done = bf16[128,8,1152]{2,1,0:T(8,128)(2,1)} async-done(((bf16[128,8,1152]{2,1,0:T(8,128)(2,1)}), bf16[128,8,1152]{2,1,0:T(8,128)(2,1)}, u32[]{:S(2)}, u32[]{:S(2)}) %all-to-all-start) | async-done | bytes 2359328 | tf_op jit(solution)/shard_map/all_to_all | solution.py:414
  71.3 3.5 %select_convert_fusion.act_ref = bf16[512,1152]{1,0:T(8,128)(2,1)S(1)} fusion(bf16[128,8,1152]{2,1,0:T(8,128)(2,1)} %all-to-all-done, pred[512]{0:T(512)(128)(4,1)S(1)} %iota_compare_fusion.5, s32[512]{0:T(512)S(1)} %select_minimum_fusion), kind=kOutput, calls=%fused_computation.27 | convolution fusion | flops 1212022784 | bytes 3541504 | tf_op jit(solution)/shard_map/dot_general | solution.py:418
  74.8 0.0 copy-start.3
  74.8 6.2 %fusion.8 = f32[512,2304]{1,0:T(8,128)S(1)} fusion(bf16[512,1152]{1,0:T(8,128)(2,1)S(1)} %select_convert_fusion.act_ref, bf16[1152,3456]{1,0:T(8,128)(2,1)} %param.14, f32[2304]{0:T(1024)S(1)} %slice-done), kind=kOutput, calls=%fused_computation.6 | convolution fusion | flops 2721447936 | bytes 11215872 | tf_op jit(solution)/shard_map/dot_general | solution.py:425
  81.0 0.6 fusion.23.mod_ref
  81.6 28.6 %shard_map.92 = (bf16[8,72,512]{2,1,0:T(8,128)(2,1)S(1)}, bf16[8,72,512]{2,1,0:T(8,128)(2,1)S(1)}, bf16[8,72,512]{2,1,0:T(8,128)(2,1)S(1)}, bf16[8,72,512]{2,1,0...) custom-call(bf16[512,1152]{1,0:T(8,128)(2,1)S(1)} %fusion.23.mod_ref, ...), custom_call_target="tpu_custom_call" | custom-call | tf_op jit(solution)/shard_map/pallas_call | solution.py:286
  110.1 32.9 %shard_map.93 = (bf16[8,72,512]{2,1,0:T(8,128)(2,1)S(1)}, bf16[8,72,512]{2,1,0:T(8,128)(2,1)S(1)}, bf16[8,72,512]{2,1,0:T(8,128)(2,1)S(1)}, bf16[8,72,512]{2,1,0:T(8,128)(2,1)S(1)}) custom-call(bf16[8,72,512]{2,1,0:T(8,128)(2,1)S(1)} %get-tuple-element.19.refs_0_, bf16[8,72,512]{2,1,0:T(8,128)(2,1)S(1)} %get-tuple-element.20.refs_1_, ...), custom_call_target="tpu_custom_call" | custom-call | tf_op jit(solution)/shard_map/pallas_call | solution.py:229
  143.0 33.5 %shard_map.94 = (bf16[8,72,512]{2,1,0:T(8,128)(2,1)}, bf16[8,72,512]{2,1,0:T(8,128)(2,1)S(1)}, bf16[8,72,512]{2,1,0:T(8,128)(2,1)S(1)}) custom-call(bf16[8,72,512]{2,1,0:T(8,128)(2,1)S(1)} %get-tuple-element.25.refs_0_, bf16[8,72,512]{2,1,0:T(8,128)(2,1)S(1)} %get-tuple-element.26.refs_1_, bf16[8,72,512]{2,1,0:T(8,128)(2,1)S(1)} %get-tuple-element.27.refs_2_, ...), custom_call_target="tpu_custom_call" | custom-call | tf_op jit(solution)/shard_map/pallas_call | solution.py:229
  176.6 3.0 %fusion.18 = bf16[1,512,1152]{2,1,0:T(8,128)(2,1)} fusion(bf16[1,512,1152]{2,1,0:T(8,128)(2,1)S(1)} %copy-done.2, bf16[8,2,72,1152]{3,2,1,0:T(8,128)(2,1)S(1)} %bitcast.60, bf16[512,1152]{1,0:T(8,128)(2,1)S(1)} %get-tuple-element.18, bf16[8,1,72,512]{3,2,0,1:T(8,128)(2,1)S(1)} %bitcast.62, bf16[8,1,72,512]{3,2,0,1:T(8,128)(2,1)S(1)} %bitcast.61), kind=kOutput, calls=%fused_computation.18 | convolution fusion | flops 1362493440 | bytes 7372800 | tf_op jit(solution)/shard_map/phet,pheD->tD/dot_general | solution.py:444
  (21 shorter events, 0.1 us)
Async XLA Ops:
  0.0 176.5 %copy-start = (bf16[1152,1152]{1,0:T(8,128)(2,1)S(1)}, bf16[1152,1152]{1,0:T(8,128)(2,1)}, u32[]{:S(2)}) copy-start(bf16[1152,1152]{1,0:T(8,128)(2,1)} %param.17) | copy-start | bytes 7962628
  0.0 28.6 %copy-start.4 = (bf16[128,1152]{1,0:T(8,128)(2,1)S(1)}, bf16[128,1152]{1,0:T(8,128)(2,1)}, u32[]{:S(2)}) copy-start(bf16[128,1152]{1,0:T(8,128)(2,1)} %param.13) | copy-start | bytes 884740
  30.9 7.5 %copy-start.5 = (f32[3456]{0:T(1024)S(1)}, f32[3456]{0:T(1024)}, u32[]{:S(2)}) copy-start(f32[3456]{0:T(1024)} %param.15) | copy-start | bytes 41476
  30.9 40.4 %all-to-all-start = ((bf16[128,8,1152]{2,1,0:T(8,128)(2,1)}), bf16[128,8,1152]{2,1,0:T(8,128)(2,1)}, u32[]{:S(2)}, u32[]{:S(2)}) async-start(bf16[128,8,1152]{2,1,0:T(8,128)(2,1)} %fusion.11), calls=%async_computation | async-start | bytes 4718592 | tf_op jit(solution)/shard_map/all_to_all | solution.py:414
  56.9 3.6 %copy-start.1 = (bf16[1,512,1152]{2,1,0:T(8,128)(2,1)S(1)}, bf16[1,512,1152]{2,1,0:T(8,128)(2,1)}, u32[]{:S(2)}) copy-start(bf16[1,512,1152]{2,1,0:T(8,128)(2,1)} %param.9) | copy-start | bytes 3538948
  61.3 13.5 %slice-start = ((f32[3456]{0:T(1024)}), f32[2304]{0:T(1024)S(1)}, s32[]{:S(2)}) async-start(f32[3456]{0:T(1024)} %param.15), calls=%async_computation.1 | async-start | bytes 24576 | tf_op jit(solution)/shard_map/slice | solution.py:426
  74.8 6.2 %copy-start.3 = (bf16[512,1152]{1,0:T(8,128)(2,1)}, bf16[512,1152]{1,0:T(8,128)(2,1)S(1)}, u32[]{:S(2)}) copy-start(bf16[512,1152]{1,0:T(8,128)(2,1)S(1)} %select_convert_fusion.act_ref) | copy-start | bytes 3538948
  74.8 6.2 %copy-start.2 = (bf16[1,512,1152]{2,1,0:T(8,128)(2,1)S(1)}, bf16[1,512,1152]{2,1,0:T(8,128)(2,1)}, u32[]{:S(2)}) copy-start(bf16[1,512,1152]{2,1,0:T(8,128)(2,1)} %param.9) | copy-start | bytes 3538948

commit v15 on v14

--- a/solution.py
+++ b/solution.py
@@ -94,7 +94,10 @@
     )(*arrays)
 
 
-def attend_body(qt_ref, kt_ref, vt_ref, o_ref, s_scr, k_ref, inv_root, after_block=None):
+def attend_body(
+    qt_ref, kt_ref, vt_ref, o_ref, s_scr, k_ref, inv_root, after_block=None, before_block=None,
+    first=1,
+):
     blocks, head_dim, q_rows = qt_ref.shape
     for c in range(blocks):
         k_ref[c] = kt_ref[c].astype(jnp.float32).T.astype(k_ref.dtype)
@@ -102,7 +105,9 @@
     me = lax.axis_index("ctx")
 
     def one_block(j, carry):
-        b = lax.rem(j + me + 1, blocks)
+        b = lax.rem(j + me + first, blocks)
+        if before_block is not None:
+            before_block(j, b)
         qt = qt_ref[b]
 
         def score(c, m):
@@ -141,7 +146,7 @@
     lax.fori_loop(0, blocks, one_block, 0)
 
 
-def attend_send_kernel(*refs, count, shards, inv_root, stream):
+def attend_send_kernel(*refs, count, shards, inv_root, stream, pull):
     qt_ref, k_ref, vt_ref = refs[:3]
     sends = refs[3 : 3 + count]
     o_ref = refs[3 + count]
@@ -153,6 +158,47 @@
     s_scr, k_scr = rest[0], rest[1]
     rest = rest[1:]
     copies = start_sends(sends, gots, *rest[1:4], shards)
+    before_block = None
+    first = 1
+    if pull:
+        q_vmem, q_send, q_recv, q_local = rest[7:11] if stream else rest[4:8]
+        me_q = lax.axis_index("ctx")
+        region_q = lax.axis_index("region")
+        q_local_copy = pltpu.make_async_copy(qt_ref.at[me_q], q_vmem.at[me_q], q_local.at[0])
+        q_local_copy.start()
+
+        def q_remote(d):
+            peer = lax.rem(me_q + d, shards)
+            return pltpu.make_async_remote_copy(
+                src_ref=qt_ref.at[peer],
+                dst_ref=q_vmem.at[me_q],
+                send_sem=q_send.at[d - 1],
+                recv_sem=q_recv.at[d - 1],
+                device_id=(region_q, peer),
+                device_id_type=pl.DeviceIdType.MESH,
+            )
+
+        for d in range(1, shards):
+            q_remote(d).start()
+
+        def before_block(j, b):
+            @pl.when(j == 0)
+            def _():
+                q_local_copy.wait()
+
+            @pl.when(j > 0)
+            def _():
+                pltpu.make_async_remote_copy(
+                    src_ref=qt_ref.at[b],
+                    dst_ref=q_vmem.at[b],
+                    send_sem=q_send.at[shards - 1 - j],
+                    recv_sem=q_recv.at[shards - 1 - j],
+                    device_id=(region_q, b),
+                    device_id_type=pl.DeviceIdType.MESH,
+                ).wait_recv()
+
+        first = 0
+        qt_ref = q_vmem
     after_block = None
     if stream:
         block_send, block_recv, block_local = rest[4:7]
@@ -181,9 +227,14 @@
             def _():
                 remote_block(b).start()
 
-    attend_body(qt_ref, k_ref, vt_ref, o_ref, s_scr, k_scr, inv_root, after_block)
+    attend_body(
+        qt_ref, k_ref, vt_ref, o_ref, s_scr, k_scr, inv_root, after_block, before_block, first
+    )
     for copy in copies:
         copy.wait()
+    if pull:
+        for d in range(1, shards):
+            q_remote(d).wait_send()
     if stream:
         for b in range(shards):
             @pl.when(b == me)
@@ -203,11 +254,18 @@
                 ).wait_recv()
 
 
-def attend_send(q_t, k_tok, v_t, sends, shards, inv_root, collective_id, stream=False):
+def attend_send(
+    q_t, k_tok, v_t, sends, shards, inv_root, collective_id, stream=False, pull=False
+):
     blocks, head_dim, rows = q_t.shape
     count = len(sends)
     kernel = functools.partial(
-        attend_send_kernel, count=count, shards=shards, inv_root=inv_root, stream=stream
+        attend_send_kernel,
+        count=count,
+        shards=shards,
+        inv_root=inv_root,
+        stream=stream,
+        pull=pull,
     )
     any_spec = pl.BlockSpec(memory_space=pl.ANY)
     vmem_spec = pl.BlockSpec(memory_space=pltpu.VMEM)
@@ -226,10 +284,17 @@
             pltpu.SemaphoreType.DMA((shards,)),
             pltpu.SemaphoreType.DMA((1,)),
         ]
+    if pull:
+        scratch += [
+            pltpu.VMEM(q_t.shape, q_t.dtype),
+            pltpu.SemaphoreType.DMA((shards - 1,)),
+            pltpu.SemaphoreType.DMA((shards - 1,)),
+            pltpu.SemaphoreType.DMA((1,)),
+        ]
     outs = pl.pallas_call(
         kernel,
         out_shape=out_shape,
-        in_specs=[vmem_spec] * 3 + [any_spec] * count,
+        in_specs=[any_spec if pull else vmem_spec] + [vmem_spec] * 2 + [any_spec] * count,
         out_specs=out_specs,
         scratch_shapes=scratch,
         compiler_params=pltpu.CompilerParams(
@@ -242,11 +307,12 @@
 
 
 def project_kernel(mod_ref, w_ref, act_ref, wg_ref, bg_ref, *refs, shards, pair, head_dim):
-    got0 = refs[:3]
+    got0 = refs[:2]
+    q0_ref = refs[2]
     later = refs[3 : 3 * pair]
     gate_ref = refs[3 * pair]
-    send0 = refs[3 * pair + 1 : 3 * pair + 4]
-    sems = refs[3 * pair + 4 :]
+    send0 = (q0_ref,) + tuple(refs[3 * pair + 1 : 3 * pair + 3])
+    sems = refs[3 * pair + 3 :]
     modulated = mod_ref[...]
 
     def fill(h, dests, i):
@@ -262,9 +328,10 @@
 
     enter(shards)
     copies = []
-    for i in range(3):
+    fill(0, send0, 0)
+    for i in range(1, 3):
         fill(0, send0, i)
-        copies += start_array(i, send0[i], got0[i], *sems, shards)
+        copies += start_array(i - 1, send0[i], got0[i - 1], *sems, shards)
     for h in range(1, pair):
         for i in range(3):
             fill(h, later[3 * (h - 1) : 3 * h], i)
@@ -288,16 +355,17 @@
         out_shape=shapes * pair
         + [jax.ShapeDtypeStruct((rows, w_gate.shape[1]), jnp.bfloat16)],
         in_specs=[vmem_spec] * 5,
-        out_specs=[any_spec] * 3 + [vmem_spec] * (3 * (pair - 1) + 1),
-        scratch_shapes=[pltpu.VMEM(x.shape, x.dtype) for x in shapes]
-        + send_scratch(3, shards),
+        out_specs=[any_spec] * 2 + [vmem_spec] * (3 * (pair - 1) + 2),
+        scratch_shapes=[pltpu.VMEM(x.shape, x.dtype) for x in shapes[1:]]
+        + send_scratch(2, shards),
         compiler_params=pltpu.CompilerParams(
             collective_id=pair + 1,
             has_side_effects=True,
             vmem_limit_bytes=48 * 1024 * 1024,
         ),
     )(modulated, w_t, activated, w_gate, b_gate)
-    return outs[:3], [outs[3 * h : 3 * h + 3] for h in range(1, pair)], outs[3 * pair]
+    got = (outs[2], outs[0], outs[1])
+    return got, [outs[3 * h : 3 * h + 3] for h in range(1, pair)], outs[3 * pair]
 
 
 def head_pipeline(modulated, w_t, gate_parts, shards, pair, head_dim, inverse_root):
@@ -309,7 +377,7 @@
         if h > 0:
             sends = sends + [out_prev]
         out_prev, sent = attend_send(
-            *got, sends, shards, inverse_root, 1 + h, stream=last
+            *got, sends, shards, inverse_root, 1 + h, stream=last, pull=h == 0
         )
         if not last:
             got = sent[:3]

time: 180 us -> 197 us (1.094)
  Pallas kernels: 114 us -> 131 us
    pallas_call x2, Pallas kernels: 66.4 us -> 89.2 us  [attend_send(): pl.pallas_call(kernel, out_shape=out_shape, in_specs=[any_spec if pull el...]
    pallas_call x1, Pallas kernels: 28.6 us -> 22.9 us  [project_send(): pl.pallas_call(kernel, out_shape=shapes * pair + [jax.ShapeDtypeStruct((r...]
  transfers between devices with their start and end apart: 1 -> 1, of which waited for: 1 -> 1; matrix products, arithmetic and copies ran while one was open for 13% -> 12% of each run, Pallas kernels for 0% -> 0%
where the time goes in v15:
time: 197 us
  Pallas kernels  131 us (66%)
  local copies, waits for them, and re-layouts  29.8 us (15%)
  matrix products  14.9 us (8%)
  waiting for transfers between devices  9.99 us (5%)
  starting transfers between devices  7.47 us (4%)
  other arithmetic  2.43 us (1%)
    pallas_call x2, Pallas kernels, attend_send(): pl.pallas_call(kernel, out_shape=out_shape, in_specs=[any_spec if pull el...  89.2 us
    pallas_call x1, Pallas kernels, project_send(): pl.pallas_call(kernel, out_shape=shapes * pair + [jax.ShapeDtypeStruct((r...  22.9 us
    pallas_call x1, Pallas kernels, exchange_requests(): pl.pallas_call(functools.partial(request_kernel, groups=groups, shards=sh...  19.1 us
    unnamed x13, local copies, waits for them, and re-layouts  11.4 us
    all_to_all x1, waiting for transfers between devices, per_device(): lax.all_to_all(served, ('region', 'ctx'), split_axis=0, concat_axis=0, ti...  9.99 us
    all_to_all x1, starting transfers between devices, per_device(): lax.all_to_all(served, ('region', 'ctx'), split_axis=0, concat_axis=0, ti...  7.47 us
    transpose x1, local copies, waits for them, and re-layouts, per_device(): w_t = w_qkv.reshape(width, 3, shards, pair, head_dim).transpose(1, 3, 2,...  7.1 us
    dot_general x1, matrix products, per_device(): jnp.dot(activated, w_ada[:, :2 * width], preferred_element_type=jnp.float32)  6.17 us
  transfers between devices with their start and end apart: 1, of which 1 were waited for; matrix products, arithmetic and copies ran while one was open for 12% of the time, Pallas kernels for 0%

profile of v15, /device:TPU:0, one launch (start us, length us, event | category | flops | bytes accessed | tf_op | source)
XLA Modules:
  0.0 196.6 jit_solution(1574747816470706139)
XLA Ops:
  0.0 0.8 compare_select_fusion.1
  0.9 3.6 %gather_fusion = s32[512]{0:T(512)S(1)} fusion(s32[16384]{0:T(1024)} %param.11, s32[1024]{0:T(1024)S(1)} %pad_clamp_fusion), kind=kCustom, calls=%fused_computation | custom fusion | bytes 6144 | tf_op jit(solution)/shard_map/gather | solution.py:457
  5.1 0.3 convert_reduce_fusion.1
  5.4 2.4 %scatter_custom_fusion = s32[1024]{0:T(1024)S(1)} fusion(s32[512]{0:T(512)S(1)} %bitcast.68, s32[512]{0:T(512)S(1)} %get-tuple-element.31, s32[]{:T(128)} %constant.41.clone.1), kind=kCustom, calls=%fused_computation.52 | custom fusion | bytes 4100 | tf_op jit(solution)/shard_map/scatter | solution.py:469
  7.9 0.7 reshape.171.req_ref
  8.6 19.1 %shard_map.91 = s32[128,8]{1,0:T(8,128)} custom-call(s32[128,8]{1,0:T(8,128)} %reshape.171.req_ref), custom_call_target="tpu_custom_call" | custom-call | tf_op jit(solution)/shard_map/pallas_call | solution.py:434
  27.7 0.9 eq.49
  28.7 2.2 %fusion.11 = bf16[128,8,1152]{2,1,0:T(8,128)(2,1)} fusion(bf16[128,1152]{1,0:T(8,128)(2,1)S(1)} %copy-done.4, s32[1024]{0:T(1024)S(1)} %eq.49), kind=kOutput, calls=%fused_computation.8 | convolution fusion | flops 303300608 | bytes 2658304 | tf_op jit(solution)/shard_map/dot_general | solution.py:478
  30.9 7.5 %all-to-all-start = ((bf16[128,8,1152]{2,1,0:T(8,128)(2,1)}), bf16[128,8,1152]{2,1,0:T(8,128)(2,1)}, u32[]{:S(2)}, u32[]{:S(2)}) async-start(bf16[128,8,1152]{2,1,0:T(8,128)(2,1)} %fusion.11), calls=%async_computation | async-start | bytes 4718592 | tf_op jit(solution)/shard_map/all_to_all | solution.py:482
  38.4 11.4 %copy.15 = bf16[1152,3456]{0,1:T(8,128)(2,1)} copy(bf16[1152,3456]{1,0:T(8,128)(2,1)} %param.16) | data formatting | bytes 15925248 | tf_op args[7]
  49.8 7.1 %copy.16 = bf16[3,2,8,72,1152]{4,3,2,1,0:T(8,128)(2,1)} copy(bf16[3,2,8,72,1152]{4,3,1,2,0:T(8,128)(2,1)} %bitcast.64) | data formatting | bytes 15925248 | tf_op jit(solution)/shard_map/transpose | solution.py:505
  56.9 3.6 %slice.22.wg_ref = bf16[1152,1152]{1,0:T(8,128)(2,1)} slice(bf16[1152,3456]{1,0:T(8,128)(2,1)} %param.14), slice={[0:1152], [2304:3456]} | slice | bytes 5308416 | tf_op jit(solution)/shard_map/slice | solution.py:497
  60.5 0.2 convert_reduce_fusion
  60.8 0.5 fusion.20
  61.3 0.0 slice-start
  61.3 10.0 %all-to-all-done = bf16[128,8,1152]{2,1,0:T(8,128)(2,1)} async-done(((bf16[128,8,1152]{2,1,0:T(8,128)(2,1)}), bf16[128,8,1152]{2,1,0:T(8,128)(2,1)}, u32[]{:S(2)}, u32[]{:S(2)}) %all-to-all-start) | async-done | bytes 2359328 | tf_op jit(solution)/shard_map/all_to_all | solution.py:482
  71.3 3.5 %select_convert_fusion.act_ref = bf16[512,1152]{1,0:T(8,128)(2,1)S(1)} fusion(bf16[128,8,1152]{2,1,0:T(8,128)(2,1)} %all-to-all-done, pred[512]{0:T(512)(128)(4,1)S(1)} %iota_compare_fusion.5, s32[512]{0:T(512)S(1)} %select_minimum_fusion), kind=kOutput, calls=%fused_computation.27 | convolution fusion | flops 1212022784 | bytes 3541504 | tf_op jit(solution)/shard_map/dot_general | solution.py:486
  74.8 0.0 copy-start.3
  74.8 6.2 %fusion.8 = f32[512,2304]{1,0:T(8,128)S(1)} fusion(bf16[512,1152]{1,0:T(8,128)(2,1)S(1)} %select_convert_fusion.act_ref, bf16[1152,3456]{1,0:T(8,128)(2,1)} %param.14, f32[2304]{0:T(1024)S(1)} %slice-done), kind=kOutput, calls=%fused_computation.6 | convolution fusion | flops 2721447936 | bytes 11215872 | tf_op jit(solution)/shard_map/dot_general | solution.py:493
  81.0 0.6 fusion.23.mod_ref
  81.6 22.9 %shard_map.92 = (bf16[8,72,512]{2,1,0:T(8,128)(2,1)S(1)}, bf16[8,72,512]{2,1,0:T(8,128)(2,1)S(1)}, bf16[8,72,512]{2,1,0:T(8,128)(2,1)S(1)}, bf16[8,72,512]{2,1,0...) custom-call(bf16[512,1152]{1,0:T(8,128)(2,1)S(1)} %fusion.23.mod_ref, ...), custom_call_target="tpu_custom_call" | custom-call | tf_op jit(solution)/shard_map/pallas_call | solution.py:353
  104.5 53.7 %shard_map.93 = (bf16[8,72,512]{2,1,0:T(8,128)(2,1)S(1)}, bf16[8,72,512]{2,1,0:T(8,128)(2,1)S(1)}, bf16[8,72,512]{2,1,0:T(8,128)(2,1)S(1)}, bf16[8,72,512]{2,1,0:T(8,128)(2,1)S(1)}) custom-call(bf16[8,72,512]{2,1,0:T(8,128)(2,1)S(1)} %get-tuple-element.19.refs_0_, bf16[8,72,512]{2,1,0:T(8,128)(2,1)S(1)} %get-tuple-element.20.refs_1_, ...), custom_call_target="tpu_custom_call" | custom-call | tf_op jit(solution)/shard_map/pallas_call | solution.py:294
  158.2 35.5 %shard_map.94 = (bf16[8,72,512]{2,1,0:T(8,128)(2,1)}, bf16[8,72,512]{2,1,0:T(8,128)(2,1)S(1)}, bf16[8,72,512]{2,1,0:T(8,128)(2,1)S(1)}) custom-call(bf16[8,72,512]{2,1,0:T(8,128)(2,1)S(1)} %get-tuple-element.25.refs_0_, bf16[8,72,512]{2,1,0:T(8,128)(2,1)S(1)} %get-tuple-element.26.refs_1_, bf16[8,72,512]{2,1,0:T(8,128)(2,1)S(1)} %get-tuple-element.27.refs_2_, ...), custom_call_target="tpu_custom_call" | custom-call | tf_op jit(solution)/shard_map/pallas_call | solution.py:294
  193.6 3.0 %fusion.18 = bf16[1,512,1152]{2,1,0:T(8,128)(2,1)} fusion(bf16[1,512,1152]{2,1,0:T(8,128)(2,1)S(1)} %copy-done.2, bf16[8,2,72,1152]{3,2,1,0:T(8,128)(2,1)S(1)} %bitcast.60, bf16[512,1152]{1,0:T(8,128)(2,1)S(1)} %get-tuple-element.18, bf16[8,1,72,512]{3,2,0,1:T(8,128)(2,1)S(1)} %bitcast.62, bf16[8,1,72,512]{3,2,0,1:T(8,128)(2,1)S(1)} %bitcast.61), kind=kOutput, calls=%fused_computation.18 | convolution fusion | flops 1362493440 | bytes 7372800 | tf_op jit(solution)/shard_map/phet,pheD->tD/dot_general | solution.py:512
  (21 shorter events, 0.1 us)
Async XLA Ops:
  0.0 193.6 %copy-start = (bf16[1152,1152]{1,0:T(8,128)(2,1)S(1)}, bf16[1152,1152]{1,0:T(8,128)(2,1)}, u32[]{:S(2)}) copy-start(bf16[1152,1152]{1,0:T(8,128)(2,1)} %param.17) | copy-start | bytes 7962628
  0.0 28.6 %copy-start.4 = (bf16[128,1152]{1,0:T(8,128)(2,1)S(1)}, bf16[128,1152]{1,0:T(8,128)(2,1)}, u32[]{:S(2)}) copy-start(bf16[128,1152]{1,0:T(8,128)(2,1)} %param.13) | copy-start | bytes 884740
  30.9 7.5 %copy-start.5 = (f32[3456]{0:T(1024)S(1)}, f32[3456]{0:T(1024)}, u32[]{:S(2)}) copy-start(f32[3456]{0:T(1024)} %param.15) | copy-start | bytes 41476
  30.9 40.4 %all-to-all-start = ((bf16[128,8,1152]{2,1,0:T(8,128)(2,1)}), bf16[128,8,1152]{2,1,0:T(8,128)(2,1)}, u32[]{:S(2)}, u32[]{:S(2)}) async-start(bf16[128,8,1152]{2,1,0:T(8,128)(2,1)} %fusion.11), calls=%async_computation | async-start | bytes 4718592 | tf_op jit(solution)/shard_map/all_to_all | solution.py:482
  56.9 3.6 %copy-start.1 = (bf16[1,512,1152]{2,1,0:T(8,128)(2,1)S(1)}, bf16[1,512,1152]{2,1,0:T(8,128)(2,1)}, u32[]{:S(2)}) copy-start(bf16[1,512,1152]{2,1,0:T(8,128)(2,1)} %param.9) | copy-start | bytes 3538948
  61.3 13.5 %slice-start = ((f32[3456]{0:T(1024)}), f32[2304]{0:T(1024)S(1)}, s32[]{:S(2)}) async-start(f32[3456]{0:T(1024)} %param.15), calls=%async_computation.1 | async-start | bytes 24576 | tf_op jit(solution)/shard_map/slice | solution.py:494
  74.8 6.2 %copy-start.3 = (bf16[512,1152]{1,0:T(8,128)(2,1)}, bf16[512,1152]{1,0:T(8,128)(2,1)S(1)}, u32[]{:S(2)}) copy-start(bf16[512,1152]{1,0:T(8,128)(2,1)S(1)} %select_convert_fusion.act_ref) | copy-start | bytes 3538948
  74.8 6.2 %copy-start.2 = (bf16[1,512,1152]{2,1,0:T(8,128)(2,1)S(1)}, bf16[1,512,1152]{2,1,0:T(8,128)(2,1)}, u32[]{:S(2)}) copy-start(bf16[1,512,1152]{2,1,0:T(8,128)(2,1)} %param.9) | copy-start | bytes 3538948

commit v16 on v15

--- a/solution.py
+++ b/solution.py
@@ -157,7 +157,7 @@
         rest = rest[1:]
     s_scr, k_scr = rest[0], rest[1]
     rest = rest[1:]
-    copies = start_sends(sends, gots, *rest[1:4], shards)
+    enter(shards)
     before_block = None
     first = 1
     if pull:
@@ -199,6 +199,9 @@
 
         first = 0
         qt_ref = q_vmem
+    copies = []
+    for a in range(count):
+        copies += start_array(a, sends[a], gots[a], *rest[1:4], shards)
     after_block = None
     if stream:
         block_send, block_recv, block_local = rest[4:7]

time: 197 us -> 180 us (0.914)
  Pallas kernels: 131 us -> 114 us
    pallas_call x2, Pallas kernels: 89.2 us -> 72.4 us  [attend_send(): pl.pallas_call(kernel, out_shape=out_shape, in_specs=[any_spec if pull el...]
  transfers between devices with their start and end apart: 1 -> 1, of which waited for: 1 -> 1; matrix products, arithmetic and copies ran while one was open for 12% -> 13% of each run, Pallas kernels for 0% -> 0%
where the time goes in v16:
time: 180 us
  Pallas kernels  114 us (63%)
  local copies, waits for them, and re-layouts  29.8 us (17%)
  matrix products  14.9 us (8%)
  waiting for transfers between devices  9.99 us (6%)
  starting transfers between devices  7.46 us (4%)
  other arithmetic  2.43 us (1%)
    pallas_call x2, Pallas kernels, attend_send(): pl.pallas_call(kernel, out_shape=out_shape, in_specs=[any_spec if pull el...  72.4 us
    pallas_call x1, Pallas kernels, project_send(): pl.pallas_call(kernel, out_shape=shapes * pair + [jax.ShapeDtypeStruct((r...  22.9 us
    pallas_call x1, Pallas kernels, exchange_requests(): pl.pallas_call(functools.partial(request_kernel, groups=groups, shards=sh...  19.1 us
    unnamed x13, local copies, waits for them, and re-layouts  11.4 us
    all_to_all x1, waiting for transfers between devices, per_device(): lax.all_to_all(served, ('region', 'ctx'), split_axis=0, concat_axis=0, ti...  9.99 us
    all_to_all x1, starting transfers between devices, per_device(): lax.all_to_all(served, ('region', 'ctx'), split_axis=0, concat_axis=0, ti...  7.46 us
    transpose x1, local copies, waits for them, and re-layouts, per_device(): w_t = w_qkv.reshape(width, 3, shards, pair, head_dim).transpose(1, 3, 2,...  7.1 us
    dot_general x1, matrix products, per_device(): jnp.dot(activated, w_ada[:, :2 * width], preferred_element_type=jnp.float32)  6.17 us
  transfers between devices with their start and end apart: 1, of which 1 were waited for; matrix products, arithmetic and copies ran while one was open for 13% of the time, Pallas kernels for 0%

profile of v16, /device:TPU:0, one launch (start us, length us, event | category | flops | bytes accessed | tf_op | source)
XLA Modules:
  0.0 179.9 jit_solution(16976717202205872538)
XLA Ops:
  0.0 0.8 compare_select_fusion.1
  0.9 3.6 %gather_fusion = s32[512]{0:T(512)S(1)} fusion(s32[16384]{0:T(1024)} %param.11, s32[1024]{0:T(1024)S(1)} %pad_clamp_fusion), kind=kCustom, calls=%fused_computation | custom fusion | bytes 6144 | tf_op jit(solution)/shard_map/gather | solution.py:460
  5.1 0.3 convert_reduce_fusion.1
  5.4 2.4 %scatter_custom_fusion = s32[1024]{0:T(1024)S(1)} fusion(s32[512]{0:T(512)S(1)} %bitcast.68, s32[512]{0:T(512)S(1)} %get-tuple-element.31, s32[]{:T(128)} %constant.41.clone.1), kind=kCustom, calls=%fused_computation.52 | custom fusion | bytes 4100 | tf_op jit(solution)/shard_map/scatter | solution.py:472
  7.9 0.7 reshape.171.req_ref
  8.6 19.1 %shard_map.91 = s32[128,8]{1,0:T(8,128)} custom-call(s32[128,8]{1,0:T(8,128)} %reshape.171.req_ref), custom_call_target="tpu_custom_call" | custom-call | tf_op jit(solution)/shard_map/pallas_call | solution.py:437
  27.7 0.9 eq.49
  28.7 2.2 %fusion.11 = bf16[128,8,1152]{2,1,0:T(8,128)(2,1)} fusion(bf16[128,1152]{1,0:T(8,128)(2,1)S(1)} %copy-done.4, s32[1024]{0:T(1024)S(1)} %eq.49), kind=kOutput, calls=%fused_computation.8 | convolution fusion | flops 303300608 | bytes 2658304 | tf_op jit(solution)/shard_map/dot_general | solution.py:481
  30.9 7.5 %all-to-all-start = ((bf16[128,8,1152]{2,1,0:T(8,128)(2,1)}), bf16[128,8,1152]{2,1,0:T(8,128)(2,1)}, u32[]{:S(2)}, u32[]{:S(2)}) async-start(bf16[128,8,1152]{2,1,0:T(8,128)(2,1)} %fusion.11), calls=%async_computation | async-start | bytes 4718592 | tf_op jit(solution)/shard_map/all_to_all | solution.py:485
  38.4 11.4 %copy.15 = bf16[1152,3456]{0,1:T(8,128)(2,1)} copy(bf16[1152,3456]{1,0:T(8,128)(2,1)} %param.16) | data formatting | bytes 15925248 | tf_op args[7]
  49.8 7.1 %copy.16 = bf16[3,2,8,72,1152]{4,3,2,1,0:T(8,128)(2,1)} copy(bf16[3,2,8,72,1152]{4,3,1,2,0:T(8,128)(2,1)} %bitcast.64) | data formatting | bytes 15925248 | tf_op jit(solution)/shard_map/transpose | solution.py:508
  56.9 3.6 %slice.22.wg_ref = bf16[1152,1152]{1,0:T(8,128)(2,1)} slice(bf16[1152,3456]{1,0:T(8,128)(2,1)} %param.14), slice={[0:1152], [2304:3456]} | slice | bytes 5308416 | tf_op jit(solution)/shard_map/slice | solution.py:500
  60.5 0.2 convert_reduce_fusion
  60.8 0.5 fusion.20
  61.3 0.0 slice-start
  61.3 10.0 %all-to-all-done = bf16[128,8,1152]{2,1,0:T(8,128)(2,1)} async-done(((bf16[128,8,1152]{2,1,0:T(8,128)(2,1)}), bf16[128,8,1152]{2,1,0:T(8,128)(2,1)}, u32[]{:S(2)}, u32[]{:S(2)}) %all-to-all-start) | async-done | bytes 2359328 | tf_op jit(solution)/shard_map/all_to_all | solution.py:485
  71.3 3.5 %select_convert_fusion.act_ref = bf16[512,1152]{1,0:T(8,128)(2,1)S(1)} fusion(bf16[128,8,1152]{2,1,0:T(8,128)(2,1)} %all-to-all-done, pred[512]{0:T(512)(128)(4,1)S(1)} %iota_compare_fusion.5, s32[512]{0:T(512)S(1)} %select_minimum_fusion), kind=kOutput, calls=%fused_computation.27 | convolution fusion | flops 1212022784 | bytes 3541504 | tf_op jit(solution)/shard_map/dot_general | solution.py:489
  74.8 0.0 copy-start.3
  74.8 6.2 %fusion.8 = f32[512,2304]{1,0:T(8,128)S(1)} fusion(bf16[512,1152]{1,0:T(8,128)(2,1)S(1)} %select_convert_fusion.act_ref, bf16[1152,3456]{1,0:T(8,128)(2,1)} %param.14, f32[2304]{0:T(1024)S(1)} %slice-done), kind=kOutput, calls=%fused_computation.6 | convolution fusion | flops 2721447936 | bytes 11215872 | tf_op jit(solution)/shard_map/dot_general | solution.py:496
  81.0 0.6 fusion.23.mod_ref
  81.6 22.9 %shard_map.92 = (bf16[8,72,512]{2,1,0:T(8,128)(2,1)S(1)}, bf16[8,72,512]{2,1,0:T(8,128)(2,1)S(1)}, bf16[8,72,512]{2,1,0:T(8,128)(2,1)S(1)}, bf16[8,72,512]{2,1,0...) custom-call(bf16[512,1152]{1,0:T(8,128)(2,1)S(1)} %fusion.23.mod_ref, ...), custom_call_target="tpu_custom_call" | custom-call | tf_op jit(solution)/shard_map/pallas_call | solution.py:356
  104.5 37.2 %shard_map.93 = (bf16[8,72,512]{2,1,0:T(8,128)(2,1)S(1)}, bf16[8,72,512]{2,1,0:T(8,128)(2,1)S(1)}, bf16[8,72,512]{2,1,0:T(8,128)(2,1)S(1)}, bf16[8,72,512]{2,1,0:T(8,128)(2,1)S(1)}) custom-call(bf16[8,72,512]{2,1,0:T(8,128)(2,1)S(1)} %get-tuple-element.19.refs_0_, bf16[8,72,512]{2,1,0:T(8,128)(2,1)S(1)} %get-tuple-element.20.refs_1_, ...), custom_call_target="tpu_custom_call" | custom-call | tf_op jit(solution)/shard_map/pallas_call | solution.py:297
  141.7 35.1 %shard_map.94 = (bf16[8,72,512]{2,1,0:T(8,128)(2,1)}, bf16[8,72,512]{2,1,0:T(8,128)(2,1)S(1)}, bf16[8,72,512]{2,1,0:T(8,128)(2,1)S(1)}) custom-call(bf16[8,72,512]{2,1,0:T(8,128)(2,1)S(1)} %get-tuple-element.25.refs_0_, bf16[8,72,512]{2,1,0:T(8,128)(2,1)S(1)} %get-tuple-element.26.refs_1_, bf16[8,72,512]{2,1,0:T(8,128)(2,1)S(1)} %get-tuple-element.27.refs_2_, ...), custom_call_target="tpu_custom_call" | custom-call | tf_op jit(solution)/shard_map/pallas_call | solution.py:297
  176.9 3.0 %fusion.18 = bf16[1,512,1152]{2,1,0:T(8,128)(2,1)} fusion(bf16[1,512,1152]{2,1,0:T(8,128)(2,1)S(1)} %copy-done.2, bf16[8,2,72,1152]{3,2,1,0:T(8,128)(2,1)S(1)} %bitcast.60, bf16[512,1152]{1,0:T(8,128)(2,1)S(1)} %get-tuple-element.18, bf16[8,1,72,512]{3,2,0,1:T(8,128)(2,1)S(1)} %bitcast.62, bf16[8,1,72,512]{3,2,0,1:T(8,128)(2,1)S(1)} %bitcast.61), kind=kOutput, calls=%fused_computation.18 | convolution fusion | flops 1362493440 | bytes 7372800 | tf_op jit(solution)/shard_map/phet,pheD->tD/dot_general | solution.py:515
  (21 shorter events, 0.1 us)
Async XLA Ops:
  0.0 176.8 %copy-start = (bf16[1152,1152]{1,0:T(8,128)(2,1)S(1)}, bf16[1152,1152]{1,0:T(8,128)(2,1)}, u32[]{:S(2)}) copy-start(bf16[1152,1152]{1,0:T(8,128)(2,1)} %param.17) | copy-start | bytes 7962628
  0.0 28.7 %copy-start.4 = (bf16[128,1152]{1,0:T(8,128)(2,1)S(1)}, bf16[128,1152]{1,0:T(8,128)(2,1)}, u32[]{:S(2)}) copy-start(bf16[128,1152]{1,0:T(8,128)(2,1)} %param.13) | copy-start | bytes 884740
  30.9 7.5 %copy-start.5 = (f32[3456]{0:T(1024)S(1)}, f32[3456]{0:T(1024)}, u32[]{:S(2)}) copy-start(f32[3456]{0:T(1024)} %param.15) | copy-start | bytes 41476
  30.9 40.3 %all-to-all-start = ((bf16[128,8,1152]{2,1,0:T(8,128)(2,1)}), bf16[128,8,1152]{2,1,0:T(8,128)(2,1)}, u32[]{:S(2)}, u32[]{:S(2)}) async-start(bf16[128,8,1152]{2,1,0:T(8,128)(2,1)} %fusion.11), calls=%async_computation | async-start | bytes 4718592 | tf_op jit(solution)/shard_map/all_to_all | solution.py:485
  56.9 3.6 %copy-start.1 = (bf16[1,512,1152]{2,1,0:T(8,128)(2,1)S(1)}, bf16[1,512,1152]{2,1,0:T(8,128)(2,1)}, u32[]{:S(2)}) copy-start(bf16[1,512,1152]{2,1,0:T(8,128)(2,1)} %param.9) | copy-start | bytes 3538948
  61.3 13.5 %slice-start = ((f32[3456]{0:T(1024)}), f32[2304]{0:T(1024)S(1)}, s32[]{:S(2)}) async-start(f32[3456]{0:T(1024)} %param.15), calls=%async_computation.1 | async-start | bytes 24576 | tf_op jit(solution)/shard_map/slice | solution.py:497
  74.8 6.2 %copy-start.3 = (bf16[512,1152]{1,0:T(8,128)(2,1)}, bf16[512,1152]{1,0:T(8,128)(2,1)S(1)}, u32[]{:S(2)}) copy-start(bf16[512,1152]{1,0:T(8,128)(2,1)S(1)} %select_convert_fusion.act_ref) | copy-start | bytes 3538948
  74.8 6.2 %copy-start.2 = (bf16[1,512,1152]{2,1,0:T(8,128)(2,1)S(1)}, bf16[1,512,1152]{2,1,0:T(8,128)(2,1)}, u32[]{:S(2)}) copy-start(bf16[1,512,1152]{2,1,0:T(8,128)(2,1)} %param.9) | copy-start | bytes 3538948

commit v17 on v16

--- a/solution.py
+++ b/solution.py
@@ -105,7 +105,10 @@
     me = lax.axis_index("ctx")
 
     def one_block(j, carry):
-        b = lax.rem(j + me + first, blocks)
+        if first == 0:
+            b = lax.rem(me - j + blocks, blocks)
+        else:
+            b = lax.rem(j + me + first, blocks)
         if before_block is not None:
             before_block(j, b)
         qt = qt_ref[b]
@@ -191,8 +194,8 @@
                 pltpu.make_async_remote_copy(
                     src_ref=qt_ref.at[b],
                     dst_ref=q_vmem.at[b],
-                    send_sem=q_send.at[shards - 1 - j],
-                    recv_sem=q_recv.at[shards - 1 - j],
+                    send_sem=q_send.at[j - 1],
+                    recv_sem=q_recv.at[j - 1],
                     device_id=(region_q, b),
                     device_id_type=pl.DeviceIdType.MESH,
                 ).wait_recv()

time: 180 us -> 176 us (0.978)
  Pallas kernels: 114 us -> 109 us
    pallas_call x2, Pallas kernels: 72.4 us -> 67.4 us  [attend_send(): pl.pallas_call(kernel, out_shape=out_shape, in_specs=[any_spec if pull el...]
where the time goes in v17:
time: 176 us; the launch traced here: 175 us
  Pallas kernels  109 us (62%)
  local copies, waits for them, and re-layouts  29.8 us (17%)
  matrix products  14.9 us (8%)
  waiting for transfers between devices  9.99 us (6%)
  starting transfers between devices  7.47 us (4%)
  other arithmetic  2.43 us (1%)
    pallas_call x2, Pallas kernels, attend_send(): pl.pallas_call(kernel, out_shape=out_shape, in_specs=[any_spec if pull el...  67.4 us
    pallas_call x1, Pallas kernels, project_send(): pl.pallas_call(kernel, out_shape=shapes * pair + [jax.ShapeDtypeStruct((r...  22.9 us
    pallas_call x1, Pallas kernels, exchange_requests(): pl.pallas_call(functools.partial(request_kernel, groups=groups, shards=sh...  19.1 us
    unnamed x13, local copies, waits for them, and re-layouts  11.4 us
    all_to_all x1, waiting for transfers between devices, per_device(): lax.all_to_all(served, ('region', 'ctx'), split_axis=0, concat_axis=0, ti...  9.99 us
    all_to_all x1, starting transfers between devices, per_device(): lax.all_to_all(served, ('region', 'ctx'), split_axis=0, concat_axis=0, ti...  7.47 us
    transpose x1, local copies, waits for them, and re-layouts, per_device(): w_t = w_qkv.reshape(width, 3, shards, pair, head_dim).transpose(1, 3, 2,...  7.1 us
    dot_general x1, matrix products, per_device(): jnp.dot(activated, w_ada[:, :2 * width], preferred_element_type=jnp.float32)  6.17 us
  transfers between devices with their start and end apart: 1, of which 1 were waited for; matrix products, arithmetic and copies ran while one was open for 13% of the time, Pallas kernels for 0%

profile of v17, /device:TPU:0, one launch (start us, length us, event | category | flops | bytes accessed | tf_op | source)
XLA Modules:
  0.0 174.9 jit_solution(10015715829120654824)
XLA Ops:
  0.0 0.8 compare_select_fusion.1
  0.9 3.6 %gather_fusion = s32[512]{0:T(512)S(1)} fusion(s32[16384]{0:T(1024)} %param.11, s32[1024]{0:T(1024)S(1)} %pad_clamp_fusion), kind=kCustom, calls=%fused_computation | custom fusion | bytes 6144 | tf_op jit(solution)/shard_map/gather | solution.py:463
  5.1 0.3 convert_reduce_fusion.1
  5.4 2.4 %scatter_custom_fusion = s32[1024]{0:T(1024)S(1)} fusion(s32[512]{0:T(512)S(1)} %bitcast.68, s32[512]{0:T(512)S(1)} %get-tuple-element.31, s32[]{:T(128)} %constant.41.clone.1), kind=kCustom, calls=%fused_computation.52 | custom fusion | bytes 4100 | tf_op jit(solution)/shard_map/scatter | solution.py:475
  7.9 0.7 reshape.171.req_ref
  8.6 19.1 %shard_map.91 = s32[128,8]{1,0:T(8,128)} custom-call(s32[128,8]{1,0:T(8,128)} %reshape.171.req_ref), custom_call_target="tpu_custom_call" | custom-call | tf_op jit(solution)/shard_map/pallas_call | solution.py:440
  27.7 0.9 eq.49
  28.7 2.2 %fusion.11 = bf16[128,8,1152]{2,1,0:T(8,128)(2,1)} fusion(bf16[128,1152]{1,0:T(8,128)(2,1)S(1)} %copy-done.4, s32[1024]{0:T(1024)S(1)} %eq.49), kind=kOutput, calls=%fused_computation.8 | convolution fusion | flops 303300608 | bytes 2658304 | tf_op jit(solution)/shard_map/dot_general | solution.py:484
  30.9 7.5 %all-to-all-start = ((bf16[128,8,1152]{2,1,0:T(8,128)(2,1)}), bf16[128,8,1152]{2,1,0:T(8,128)(2,1)}, u32[]{:S(2)}, u32[]{:S(2)}) async-start(bf16[128,8,1152]{2,1,0:T(8,128)(2,1)} %fusion.11), calls=%async_computation | async-start | bytes 4718592 | tf_op jit(solution)/shard_map/all_to_all | solution.py:488
  38.4 11.4 %copy.15 = bf16[1152,3456]{0,1:T(8,128)(2,1)} copy(bf16[1152,3456]{1,0:T(8,128)(2,1)} %param.16) | data formatting | bytes 15925248 | tf_op args[7]
  49.8 7.1 %copy.16 = bf16[3,2,8,72,1152]{4,3,2,1,0:T(8,128)(2,1)} copy(bf16[3,2,8,72,1152]{4,3,1,2,0:T(8,128)(2,1)} %bitcast.64) | data formatting | bytes 15925248 | tf_op jit(solution)/shard_map/transpose | solution.py:511
  56.9 3.6 %slice.22.wg_ref = bf16[1152,1152]{1,0:T(8,128)(2,1)} slice(bf16[1152,3456]{1,0:T(8,128)(2,1)} %param.14), slice={[0:1152], [2304:3456]} | slice | bytes 5308416 | tf_op jit(solution)/shard_map/slice | solution.py:503
  60.5 0.2 convert_reduce_fusion
  60.8 0.5 fusion.20
  61.3 0.0 slice-start
  61.3 10.0 %all-to-all-done = bf16[128,8,1152]{2,1,0:T(8,128)(2,1)} async-done(((bf16[128,8,1152]{2,1,0:T(8,128)(2,1)}), bf16[128,8,1152]{2,1,0:T(8,128)(2,1)}, u32[]{:S(2)}, u32[]{:S(2)}) %all-to-all-start) | async-done | bytes 2359328 | tf_op jit(solution)/shard_map/all_to_all | solution.py:488
  71.3 3.5 %select_convert_fusion.act_ref = bf16[512,1152]{1,0:T(8,128)(2,1)S(1)} fusion(bf16[128,8,1152]{2,1,0:T(8,128)(2,1)} %all-to-all-done, pred[512]{0:T(512)(128)(4,1)S(1)} %iota_compare_fusion.5, s32[512]{0:T(512)S(1)} %select_minimum_fusion), kind=kOutput, calls=%fused_computation.27 | convolution fusion | flops 1212022784 | bytes 3541504 | tf_op jit(solution)/shard_map/dot_general | solution.py:492
  74.8 0.0 copy-start.3
  74.8 6.2 %fusion.8 = f32[512,2304]{1,0:T(8,128)S(1)} fusion(bf16[512,1152]{1,0:T(8,128)(2,1)S(1)} %select_convert_fusion.act_ref, bf16[1152,3456]{1,0:T(8,128)(2,1)} %param.14, f32[2304]{0:T(1024)S(1)} %slice-done), kind=kOutput, calls=%fused_computation.6 | convolution fusion | flops 2721447936 | bytes 11215872 | tf_op jit(solution)/shard_map/dot_general | solution.py:499
  81.0 0.6 fusion.23.mod_ref
  81.6 22.9 %shard_map.92 = (bf16[8,72,512]{2,1,0:T(8,128)(2,1)S(1)}, bf16[8,72,512]{2,1,0:T(8,128)(2,1)S(1)}, bf16[8,72,512]{2,1,0:T(8,128)(2,1)S(1)}, bf16[8,72,512]{2,1,0...) custom-call(bf16[512,1152]{1,0:T(8,128)(2,1)S(1)} %fusion.23.mod_ref, ...), custom_call_target="tpu_custom_call" | custom-call | tf_op jit(solution)/shard_map/pallas_call | solution.py:359
  104.5 35.6 %shard_map.93 = (bf16[8,72,512]{2,1,0:T(8,128)(2,1)S(1)}, bf16[8,72,512]{2,1,0:T(8,128)(2,1)S(1)}, bf16[8,72,512]{2,1,0:T(8,128)(2,1)S(1)}, bf16[8,72,512]{2,1,0:T(8,128)(2,1)S(1)}) custom-call(bf16[8,72,512]{2,1,0:T(8,128)(2,1)S(1)} %get-tuple-element.19.refs_0_, bf16[8,72,512]{2,1,0:T(8,128)(2,1)S(1)} %get-tuple-element.20.refs_1_, ...), custom_call_target="tpu_custom_call" | custom-call | tf_op jit(solution)/shard_map/pallas_call | solution.py:300
  140.1 31.8 %shard_map.94 = (bf16[8,72,512]{2,1,0:T(8,128)(2,1)}, bf16[8,72,512]{2,1,0:T(8,128)(2,1)S(1)}, bf16[8,72,512]{2,1,0:T(8,128)(2,1)S(1)}) custom-call(bf16[8,72,512]{2,1,0:T(8,128)(2,1)S(1)} %get-tuple-element.25.refs_0_, bf16[8,72,512]{2,1,0:T(8,128)(2,1)S(1)} %get-tuple-element.26.refs_1_, bf16[8,72,512]{2,1,0:T(8,128)(2,1)S(1)} %get-tuple-element.27.refs_2_, ...), custom_call_target="tpu_custom_call" | custom-call | tf_op jit(solution)/shard_map/pallas_call | solution.py:300
  171.9 3.0 %fusion.18 = bf16[1,512,1152]{2,1,0:T(8,128)(2,1)} fusion(bf16[1,512,1152]{2,1,0:T(8,128)(2,1)S(1)} %copy-done.2, bf16[8,2,72,1152]{3,2,1,0:T(8,128)(2,1)S(1)} %bitcast.60, bf16[512,1152]{1,0:T(8,128)(2,1)S(1)} %get-tuple-element.18, bf16[8,1,72,512]{3,2,0,1:T(8,128)(2,1)S(1)} %bitcast.62, bf16[8,1,72,512]{3,2,0,1:T(8,128)(2,1)S(1)} %bitcast.61), kind=kOutput, calls=%fused_computation.18 | convolution fusion | flops 1362493440 | bytes 7372800 | tf_op jit(solution)/shard_map/phet,pheD->tD/dot_general | solution.py:518
  (21 shorter events, 0.1 us)
Async XLA Ops:
  0.0 171.9 %copy-start = (bf16[1152,1152]{1,0:T(8,128)(2,1)S(1)}, bf16[1152,1152]{1,0:T(8,128)(2,1)}, u32[]{:S(2)}) copy-start(bf16[1152,1152]{1,0:T(8,128)(2,1)} %param.17) | copy-start | bytes 7962628
  0.0 28.6 %copy-start.4 = (bf16[128,1152]{1,0:T(8,128)(2,1)S(1)}, bf16[128,1152]{1,0:T(8,128)(2,1)}, u32[]{:S(2)}) copy-start(bf16[128,1152]{1,0:T(8,128)(2,1)} %param.13) | copy-start | bytes 884740
  30.9 7.5 %copy-start.5 = (f32[3456]{0:T(1024)S(1)}, f32[3456]{0:T(1024)}, u32[]{:S(2)}) copy-start(f32[3456]{0:T(1024)} %param.15) | copy-start | bytes 41476
  30.9 40.4 %all-to-all-start = ((bf16[128,8,1152]{2,1,0:T(8,128)(2,1)}), bf16[128,8,1152]{2,1,0:T(8,128)(2,1)}, u32[]{:S(2)}, u32[]{:S(2)}) async-start(bf16[128,8,1152]{2,1,0:T(8,128)(2,1)} %fusion.11), calls=%async_computation | async-start | bytes 4718592 | tf_op jit(solution)/shard_map/all_to_all | solution.py:488
  56.9 3.6 %copy-start.1 = (bf16[1,512,1152]{2,1,0:T(8,128)(2,1)S(1)}, bf16[1,512,1152]{2,1,0:T(8,128)(2,1)}, u32[]{:S(2)}) copy-start(bf16[1,512,1152]{2,1,0:T(8,128)(2,1)} %param.9) | copy-start | bytes 3538948
  61.3 13.5 %slice-start = ((f32[3456]{0:T(1024)}), f32[2304]{0:T(1024)S(1)}, s32[]{:S(2)}) async-start(f32[3456]{0:T(1024)} %param.15), calls=%async_computation.1 | async-start | bytes 24576 | tf_op jit(solution)/shard_map/slice | solution.py:500
  74.8 6.2 %copy-start.3 = (bf16[512,1152]{1,0:T(8,128)(2,1)}, bf16[512,1152]{1,0:T(8,128)(2,1)S(1)}, u32[]{:S(2)}) copy-start(bf16[512,1152]{1,0:T(8,128)(2,1)S(1)} %select_convert_fusion.act_ref) | copy-start | bytes 3538948
  74.8 6.2 %copy-start.2 = (bf16[1,512,1152]{2,1,0:T(8,128)(2,1)S(1)}, bf16[1,512,1152]{2,1,0:T(8,128)(2,1)}, u32[]{:S(2)}) copy-start(bf16[1,512,1152]{2,1,0:T(8,128)(2,1)} %param.9) | copy-start | bytes 3538948

commit v18 on v17

--- a/solution.py
+++ b/solution.py
@@ -334,10 +334,10 @@
 
     enter(shards)
     copies = []
-    fill(0, send0, 0)
     for i in range(1, 3):
         fill(0, send0, i)
         copies += start_array(i - 1, send0[i], got0[i - 1], *sems, shards)
+    fill(0, send0, 0)
     for h in range(1, pair):
         for i in range(3):
             fill(h, later[3 * (h - 1) : 3 * h], i)

time: 176 us -> 175 us (level)
  no operation moved by 1% of the time
where the time goes in v18:
time: 175 us; the launch traced here: 174 us
  Pallas kernels  109 us (62%)
  local copies, waits for them, and re-layouts  29.8 us (17%)
  matrix products  14.9 us (9%)
  waiting for transfers between devices  9.99 us (6%)
  starting transfers between devices  7.46 us (4%)
  other arithmetic  2.43 us (1%)
    pallas_call x2, Pallas kernels, attend_send(): pl.pallas_call(kernel, out_shape=out_shape, in_specs=[any_spec if pull el...  67.4 us
    pallas_call x1, Pallas kernels, project_send(): pl.pallas_call(kernel, out_shape=shapes * pair + [jax.ShapeDtypeStruct((r...  22.1 us
    pallas_call x1, Pallas kernels, exchange_requests(): pl.pallas_call(functools.partial(request_kernel, groups=groups, shards=sh...  19.1 us
    unnamed x13, local copies, waits for them, and re-layouts  11.4 us
    all_to_all x1, waiting for transfers between devices, per_device(): lax.all_to_all(served, ('region', 'ctx'), split_axis=0, concat_axis=0, ti...  9.99 us
    all_to_all x1, starting transfers between devices, per_device(): lax.all_to_all(served, ('region', 'ctx'), split_axis=0, concat_axis=0, ti...  7.46 us
    transpose x1, local copies, waits for them, and re-layouts, per_device(): w_t = w_qkv.reshape(width, 3, shards, pair, head_dim).transpose(1, 3, 2,...  7.1 us
    dot_general x1, matrix products, per_device(): jnp.dot(activated, w_ada[:, :2 * width], preferred_element_type=jnp.float32)  6.17 us
  transfers between devices with their start and end apart: 1, of which 1 were waited for; matrix products, arithmetic and copies ran while one was open for 13% of the time, Pallas kernels for 0%

profile of v18, /device:TPU:0, one launch (start us, length us, event | category | flops | bytes accessed | tf_op | source)
XLA Modules:
  0.0 174.2 jit_solution(1770399362941049958)
XLA Ops:
  0.0 0.8 compare_select_fusion.1
  0.9 3.6 %gather_fusion = s32[512]{0:T(512)S(1)} fusion(s32[16384]{0:T(1024)} %param.11, s32[1024]{0:T(1024)S(1)} %pad_clamp_fusion), kind=kCustom, calls=%fused_computation | custom fusion | bytes 6144 | tf_op jit(solution)/shard_map/gather | solution.py:463
  5.1 0.3 convert_reduce_fusion.1
  5.4 2.4 %scatter_custom_fusion = s32[1024]{0:T(1024)S(1)} fusion(s32[512]{0:T(512)S(1)} %bitcast.68, s32[512]{0:T(512)S(1)} %get-tuple-element.31, s32[]{:T(128)} %constant.41.clone.1), kind=kCustom, calls=%fused_computation.52 | custom fusion | bytes 4100 | tf_op jit(solution)/shard_map/scatter | solution.py:475
  7.9 0.7 reshape.171.req_ref
  8.6 19.1 %shard_map.91 = s32[128,8]{1,0:T(8,128)} custom-call(s32[128,8]{1,0:T(8,128)} %reshape.171.req_ref), custom_call_target="tpu_custom_call" | custom-call | tf_op jit(solution)/shard_map/pallas_call | solution.py:440
  27.7 0.9 eq.49
  28.7 2.2 %fusion.11 = bf16[128,8,1152]{2,1,0:T(8,128)(2,1)} fusion(bf16[128,1152]{1,0:T(8,128)(2,1)S(1)} %copy-done.4, s32[1024]{0:T(1024)S(1)} %eq.49), kind=kOutput, calls=%fused_computation.8 | convolution fusion | flops 303300608 | bytes 2658304 | tf_op jit(solution)/shard_map/dot_general | solution.py:484
  30.9 7.5 %all-to-all-start = ((bf16[128,8,1152]{2,1,0:T(8,128)(2,1)}), bf16[128,8,1152]{2,1,0:T(8,128)(2,1)}, u32[]{:S(2)}, u32[]{:S(2)}) async-start(bf16[128,8,1152]{2,1,0:T(8,128)(2,1)} %fusion.11), calls=%async_computation | async-start | bytes 4718592 | tf_op jit(solution)/shard_map/all_to_all | solution.py:488
  38.4 11.4 %copy.15 = bf16[1152,3456]{0,1:T(8,128)(2,1)} copy(bf16[1152,3456]{1,0:T(8,128)(2,1)} %param.16) | data formatting | bytes 15925248 | tf_op args[7]
  49.8 7.1 %copy.16 = bf16[3,2,8,72,1152]{4,3,2,1,0:T(8,128)(2,1)} copy(bf16[3,2,8,72,1152]{4,3,1,2,0:T(8,128)(2,1)} %bitcast.64) | data formatting | bytes 15925248 | tf_op jit(solution)/shard_map/transpose | solution.py:511
  56.9 3.6 %slice.22.wg_ref = bf16[1152,1152]{1,0:T(8,128)(2,1)} slice(bf16[1152,3456]{1,0:T(8,128)(2,1)} %param.14), slice={[0:1152], [2304:3456]} | slice | bytes 5308416 | tf_op jit(solution)/shard_map/slice | solution.py:503
  60.5 0.2 convert_reduce_fusion
  60.8 0.5 fusion.20
  61.3 0.0 slice-start
  61.3 10.0 %all-to-all-done = bf16[128,8,1152]{2,1,0:T(8,128)(2,1)} async-done(((bf16[128,8,1152]{2,1,0:T(8,128)(2,1)}), bf16[128,8,1152]{2,1,0:T(8,128)(2,1)}, u32[]{:S(2)}, u32[]{:S(2)}) %all-to-all-start) | async-done | bytes 2359328 | tf_op jit(solution)/shard_map/all_to_all | solution.py:488
  71.3 3.5 %select_convert_fusion.act_ref = bf16[512,1152]{1,0:T(8,128)(2,1)S(1)} fusion(bf16[128,8,1152]{2,1,0:T(8,128)(2,1)} %all-to-all-done, pred[512]{0:T(512)(128)(4,1)S(1)} %iota_compare_fusion.5, s32[512]{0:T(512)S(1)} %select_minimum_fusion), kind=kOutput, calls=%fused_computation.27 | convolution fusion | flops 1212022784 | bytes 3541504 | tf_op jit(solution)/shard_map/dot_general | solution.py:492
  74.8 0.0 copy-start.3
  74.8 6.2 %fusion.8 = f32[512,2304]{1,0:T(8,128)S(1)} fusion(bf16[512,1152]{1,0:T(8,128)(2,1)S(1)} %select_convert_fusion.act_ref, bf16[1152,3456]{1,0:T(8,128)(2,1)} %param.14, f32[2304]{0:T(1024)S(1)} %slice-done), kind=kOutput, calls=%fused_computation.6 | convolution fusion | flops 2721447936 | bytes 11215872 | tf_op jit(solution)/shard_map/dot_general | solution.py:499
  81.0 0.6 fusion.23.mod_ref
  81.6 22.1 %shard_map.92 = (bf16[8,72,512]{2,1,0:T(8,128)(2,1)S(1)}, bf16[8,72,512]{2,1,0:T(8,128)(2,1)S(1)}, bf16[8,72,512]{2,1,0:T(8,128)(2,1)S(1)}, bf16[8,72,512]{2,1,0...) custom-call(bf16[512,1152]{1,0:T(8,128)(2,1)S(1)} %fusion.23.mod_ref, ...), custom_call_target="tpu_custom_call" | custom-call | tf_op jit(solution)/shard_map/pallas_call | solution.py:359
  103.7 35.6 %shard_map.93 = (bf16[8,72,512]{2,1,0:T(8,128)(2,1)S(1)}, bf16[8,72,512]{2,1,0:T(8,128)(2,1)S(1)}, bf16[8,72,512]{2,1,0:T(8,128)(2,1)S(1)}, bf16[8,72,512]{2,1,0:T(8,128)(2,1)S(1)}) custom-call(bf16[8,72,512]{2,1,0:T(8,128)(2,1)S(1)} %get-tuple-element.19.refs_0_, bf16[8,72,512]{2,1,0:T(8,128)(2,1)S(1)} %get-tuple-element.20.refs_1_, ...), custom_call_target="tpu_custom_call" | custom-call | tf_op jit(solution)/shard_map/pallas_call | solution.py:300
  139.3 31.9 %shard_map.94 = (bf16[8,72,512]{2,1,0:T(8,128)(2,1)}, bf16[8,72,512]{2,1,0:T(8,128)(2,1)S(1)}, bf16[8,72,512]{2,1,0:T(8,128)(2,1)S(1)}) custom-call(bf16[8,72,512]{2,1,0:T(8,128)(2,1)S(1)} %get-tuple-element.25.refs_0_, bf16[8,72,512]{2,1,0:T(8,128)(2,1)S(1)} %get-tuple-element.26.refs_1_, bf16[8,72,512]{2,1,0:T(8,128)(2,1)S(1)} %get-tuple-element.27.refs_2_, ...), custom_call_target="tpu_custom_call" | custom-call | tf_op jit(solution)/shard_map/pallas_call | solution.py:300
  171.2 3.0 %fusion.18 = bf16[1,512,1152]{2,1,0:T(8,128)(2,1)} fusion(bf16[1,512,1152]{2,1,0:T(8,128)(2,1)S(1)} %copy-done.2, bf16[8,2,72,1152]{3,2,1,0:T(8,128)(2,1)S(1)} %bitcast.60, bf16[512,1152]{1,0:T(8,128)(2,1)S(1)} %get-tuple-element.18, bf16[8,1,72,512]{3,2,0,1:T(8,128)(2,1)S(1)} %bitcast.62, bf16[8,1,72,512]{3,2,0,1:T(8,128)(2,1)S(1)} %bitcast.61), kind=kOutput, calls=%fused_computation.18 | convolution fusion | flops 1362493440 | bytes 7372800 | tf_op jit(solution)/shard_map/phet,pheD->tD/dot_general | solution.py:518
  (21 shorter events, 0.1 us)
Async XLA Ops:
  0.0 171.1 %copy-start = (bf16[1152,1152]{1,0:T(8,128)(2,1)S(1)}, bf16[1152,1152]{1,0:T(8,128)(2,1)}, u32[]{:S(2)}) copy-start(bf16[1152,1152]{1,0:T(8,128)(2,1)} %param.17) | copy-start | bytes 7962628
  0.0 28.7 %copy-start.4 = (bf16[128,1152]{1,0:T(8,128)(2,1)S(1)}, bf16[128,1152]{1,0:T(8,128)(2,1)}, u32[]{:S(2)}) copy-start(bf16[128,1152]{1,0:T(8,128)(2,1)} %param.13) | copy-start | bytes 884740
  30.9 7.5 %copy-start.5 = (f32[3456]{0:T(1024)S(1)}, f32[3456]{0:T(1024)}, u32[]{:S(2)}) copy-start(f32[3456]{0:T(1024)} %param.15) | copy-start | bytes 41476
  30.9 40.3 %all-to-all-start = ((bf16[128,8,1152]{2,1,0:T(8,128)(2,1)}), bf16[128,8,1152]{2,1,0:T(8,128)(2,1)}, u32[]{:S(2)}, u32[]{:S(2)}) async-start(bf16[128,8,1152]{2,1,0:T(8,128)(2,1)} %fusion.11), calls=%async_computation | async-start | bytes 4718592 | tf_op jit(solution)/shard_map/all_to_all | solution.py:488
  56.9 3.6 %copy-start.1 = (bf16[1,512,1152]{2,1,0:T(8,128)(2,1)S(1)}, bf16[1,512,1152]{2,1,0:T(8,128)(2,1)}, u32[]{:S(2)}) copy-start(bf16[1,512,1152]{2,1,0:T(8,128)(2,1)} %param.9) | copy-start | bytes 3538948
  61.3 13.5 %slice-start = ((f32[3456]{0:T(1024)}), f32[2304]{0:T(1024)S(1)}, s32[]{:S(2)}) async-start(f32[3456]{0:T(1024)} %param.15), calls=%async_computation.1 | async-start | bytes 24576 | tf_op jit(solution)/shard_map/slice | solution.py:500
  74.8 6.2 %copy-start.3 = (bf16[512,1152]{1,0:T(8,128)(2,1)}, bf16[512,1152]{1,0:T(8,128)(2,1)S(1)}, u32[]{:S(2)}) copy-start(bf16[512,1152]{1,0:T(8,128)(2,1)S(1)} %select_convert_fusion.act_ref) | copy-start | bytes 3538948
  74.8 6.2 %copy-start.2 = (bf16[1,512,1152]{2,1,0:T(8,128)(2,1)S(1)}, bf16[1,512,1152]{2,1,0:T(8,128)(2,1)}, u32[]{:S(2)}) copy-start(bf16[1,512,1152]{2,1,0:T(8,128)(2,1)} %param.9) | copy-start | bytes 3538948

commit v19 on v17

--- a/solution.py
+++ b/solution.py
@@ -96,7 +96,7 @@
 
 def attend_body(
     qt_ref, kt_ref, vt_ref, o_ref, s_scr, k_ref, inv_root, after_block=None, before_block=None,
-    first=1,
+    first=1, span=None, between=None,
 ):
     blocks, head_dim, q_rows = qt_ref.shape
     for c in range(blocks):
@@ -146,7 +146,12 @@
             after_block(b)
         return carry
 
-    lax.fori_loop(0, blocks, one_block, 0)
+    if between is None:
+        lax.fori_loop(0, blocks, one_block, 0)
+    else:
+        lax.fori_loop(0, span, one_block, 0)
+        between()
+        lax.fori_loop(span, blocks, one_block, 0)
 
 
 def attend_send_kernel(*refs, count, shards, inv_root, stream, pull):
@@ -203,8 +208,16 @@
         first = 0
         qt_ref = q_vmem
     copies = []
-    for a in range(count):
-        copies += start_array(a, sends[a], gots[a], *rest[1:4], shards)
+
+    def launch():
+        for a in range(count):
+            copies.extend(start_array(a, sends[a], gots[a], *rest[1:4], shards))
+
+    between = None
+    if pull:
+        between = launch
+    else:
+        launch()
     after_block = None
     if stream:
         block_send, block_recv, block_local = rest[4:7]
@@ -234,7 +247,8 @@
                 remote_block(b).start()
 
     attend_body(
-        qt_ref, k_ref, vt_ref, o_ref, s_scr, k_scr, inv_root, after_block, before_block, first
+        qt_ref, k_ref, vt_ref, o_ref, s_scr, k_scr, inv_root, after_block, before_block, first,
+        span=1, between=between,
     )
     for copy in copies:
         copy.wait()

time: 176 us -> 175 us (level)
  no operation moved by 1% of the time
where the time goes in v19:
time: 175 us; the launch traced here: 174 us
  Pallas kernels  109 us (62%)
  local copies, waits for them, and re-layouts  29.8 us (17%)
  matrix products  14.9 us (9%)
  waiting for transfers between devices  9.99 us (6%)
  starting transfers between devices  7.47 us (4%)
  other arithmetic  2.43 us (1%)
    pallas_call x2, Pallas kernels, attend_send(): pl.pallas_call(kernel, out_shape=out_shape, in_specs=[any_spec if pull el...  66.6 us
    pallas_call x1, Pallas kernels, project_send(): pl.pallas_call(kernel, out_shape=shapes * pair + [jax.ShapeDtypeStruct((r...  22.9 us
    pallas_call x1, Pallas kernels, exchange_requests(): pl.pallas_call(functools.partial(request_kernel, groups=groups, shards=sh...  19.1 us
    unnamed x13, local copies, waits for them, and re-layouts  11.4 us
    all_to_all x1, waiting for transfers between devices, per_device(): lax.all_to_all(served, ('region', 'ctx'), split_axis=0, concat_axis=0, ti...  9.99 us
    all_to_all x1, starting transfers between devices, per_device(): lax.all_to_all(served, ('region', 'ctx'), split_axis=0, concat_axis=0, ti...  7.47 us
    transpose x1, local copies, waits for them, and re-layouts, per_device(): w_t = w_qkv.reshape(width, 3, shards, pair, head_dim).transpose(1, 3, 2,...  7.1 us
    dot_general x1, matrix products, per_device(): jnp.dot(activated, w_ada[:, :2 * width], preferred_element_type=jnp.float32)  6.17 us
  transfers between devices with their start and end apart: 1, of which 1 were waited for; matrix products, arithmetic and copies ran while one was open for 13% of the time, Pallas kernels for 0%

profile of v19, /device:TPU:0, one launch (start us, length us, event | category | flops | bytes accessed | tf_op | source)
XLA Modules:
  0.0 174.1 jit_solution(2765037159044642082)
XLA Ops:
  0.0 0.8 compare_select_fusion.1
  0.9 3.6 %gather_fusion = s32[512]{0:T(512)S(1)} fusion(s32[16384]{0:T(1024)} %param.11, s32[1024]{0:T(1024)S(1)} %pad_clamp_fusion), kind=kCustom, calls=%fused_computation | custom fusion | bytes 6144 | tf_op jit(solution)/shard_map/gather | solution.py:477
  5.1 0.3 convert_reduce_fusion.1
  5.4 2.4 %scatter_custom_fusion = s32[1024]{0:T(1024)S(1)} fusion(s32[512]{0:T(512)S(1)} %bitcast.68, s32[512]{0:T(512)S(1)} %get-tuple-element.31, s32[]{:T(128)} %constant.41.clone.1), kind=kCustom, calls=%fused_computation.52 | custom fusion | bytes 4100 | tf_op jit(solution)/shard_map/scatter | solution.py:489
  7.9 0.7 reshape.171.req_ref
  8.6 19.1 %shard_map.91 = s32[128,8]{1,0:T(8,128)} custom-call(s32[128,8]{1,0:T(8,128)} %reshape.171.req_ref), custom_call_target="tpu_custom_call" | custom-call | tf_op jit(solution)/shard_map/pallas_call | solution.py:454
  27.7 0.9 eq.49
  28.7 2.2 %fusion.11 = bf16[128,8,1152]{2,1,0:T(8,128)(2,1)} fusion(bf16[128,1152]{1,0:T(8,128)(2,1)S(1)} %copy-done.4, s32[1024]{0:T(1024)S(1)} %eq.49), kind=kOutput, calls=%fused_computation.8 | convolution fusion | flops 303300608 | bytes 2658304 | tf_op jit(solution)/shard_map/dot_general | solution.py:498
  30.9 7.5 %all-to-all-start = ((bf16[128,8,1152]{2,1,0:T(8,128)(2,1)}), bf16[128,8,1152]{2,1,0:T(8,128)(2,1)}, u32[]{:S(2)}, u32[]{:S(2)}) async-start(bf16[128,8,1152]{2,1,0:T(8,128)(2,1)} %fusion.11), calls=%async_computation | async-start | bytes 4718592 | tf_op jit(solution)/shard_map/all_to_all | solution.py:502
  38.4 11.4 %copy.15 = bf16[1152,3456]{0,1:T(8,128)(2,1)} copy(bf16[1152,3456]{1,0:T(8,128)(2,1)} %param.16) | data formatting | bytes 15925248 | tf_op args[7]
  49.8 7.1 %copy.16 = bf16[3,2,8,72,1152]{4,3,2,1,0:T(8,128)(2,1)} copy(bf16[3,2,8,72,1152]{4,3,1,2,0:T(8,128)(2,1)} %bitcast.64) | data formatting | bytes 15925248 | tf_op jit(solution)/shard_map/transpose | solution.py:525
  56.9 3.6 %slice.22.wg_ref = bf16[1152,1152]{1,0:T(8,128)(2,1)} slice(bf16[1152,3456]{1,0:T(8,128)(2,1)} %param.14), slice={[0:1152], [2304:3456]} | slice | bytes 5308416 | tf_op jit(solution)/shard_map/slice | solution.py:517
  60.5 0.2 convert_reduce_fusion
  60.8 0.5 fusion.20
  61.3 0.0 slice-start
  61.3 10.0 %all-to-all-done = bf16[128,8,1152]{2,1,0:T(8,128)(2,1)} async-done(((bf16[128,8,1152]{2,1,0:T(8,128)(2,1)}), bf16[128,8,1152]{2,1,0:T(8,128)(2,1)}, u32[]{:S(2)}, u32[]{:S(2)}) %all-to-all-start) | async-done | bytes 2359328 | tf_op jit(solution)/shard_map/all_to_all | solution.py:502
  71.3 3.5 %select_convert_fusion.act_ref = bf16[512,1152]{1,0:T(8,128)(2,1)S(1)} fusion(bf16[128,8,1152]{2,1,0:T(8,128)(2,1)} %all-to-all-done, pred[512]{0:T(512)(128)(4,1)S(1)} %iota_compare_fusion.5, s32[512]{0:T(512)S(1)} %select_minimum_fusion), kind=kOutput, calls=%fused_computation.27 | convolution fusion | flops 1212022784 | bytes 3541504 | tf_op jit(solution)/shard_map/dot_general | solution.py:506
  74.8 0.0 copy-start.3
  74.8 6.2 %fusion.8 = f32[512,2304]{1,0:T(8,128)S(1)} fusion(bf16[512,1152]{1,0:T(8,128)(2,1)S(1)} %select_convert_fusion.act_ref, bf16[1152,3456]{1,0:T(8,128)(2,1)} %param.14, f32[2304]{0:T(1024)S(1)} %slice-done), kind=kOutput, calls=%fused_computation.6 | convolution fusion | flops 2721447936 | bytes 11215872 | tf_op jit(solution)/shard_map/dot_general | solution.py:513
  81.0 0.6 fusion.23.mod_ref
  81.6 22.9 %shard_map.92 = (bf16[8,72,512]{2,1,0:T(8,128)(2,1)S(1)}, bf16[8,72,512]{2,1,0:T(8,128)(2,1)S(1)}, bf16[8,72,512]{2,1,0:T(8,128)(2,1)S(1)}, bf16[8,72,512]{2,1,0...) custom-call(bf16[512,1152]{1,0:T(8,128)(2,1)S(1)} %fusion.23.mod_ref, ...), custom_call_target="tpu_custom_call" | custom-call | tf_op jit(solution)/shard_map/pallas_call | solution.py:373
  104.5 33.5 %shard_map.93 = (bf16[8,72,512]{2,1,0:T(8,128)(2,1)S(1)}, bf16[8,72,512]{2,1,0:T(8,128)(2,1)S(1)}, bf16[8,72,512]{2,1,0:T(8,128)(2,1)S(1)}, bf16[8,72,512]{2,1,0:T(8,128)(2,1)S(1)}) custom-call(bf16[8,72,512]{2,1,0:T(8,128)(2,1)S(1)} %get-tuple-element.19.refs_0_, bf16[8,72,512]{2,1,0:T(8,128)(2,1)S(1)} %get-tuple-element.20.refs_1_, ...), custom_call_target="tpu_custom_call" | custom-call | tf_op jit(solution)/shard_map/pallas_call | solution.py:314
  138.0 33.1 %shard_map.94 = (bf16[8,72,512]{2,1,0:T(8,128)(2,1)}, bf16[8,72,512]{2,1,0:T(8,128)(2,1)S(1)}, bf16[8,72,512]{2,1,0:T(8,128)(2,1)S(1)}) custom-call(bf16[8,72,512]{2,1,0:T(8,128)(2,1)S(1)} %get-tuple-element.25.refs_0_, bf16[8,72,512]{2,1,0:T(8,128)(2,1)S(1)} %get-tuple-element.26.refs_1_, bf16[8,72,512]{2,1,0:T(8,128)(2,1)S(1)} %get-tuple-element.27.refs_2_, ...), custom_call_target="tpu_custom_call" | custom-call | tf_op jit(solution)/shard_map/pallas_call | solution.py:314
  171.1 3.0 %fusion.18 = bf16[1,512,1152]{2,1,0:T(8,128)(2,1)} fusion(bf16[1,512,1152]{2,1,0:T(8,128)(2,1)S(1)} %copy-done.2, bf16[8,2,72,1152]{3,2,1,0:T(8,128)(2,1)S(1)} %bitcast.60, bf16[512,1152]{1,0:T(8,128)(2,1)S(1)} %get-tuple-element.18, bf16[8,1,72,512]{3,2,0,1:T(8,128)(2,1)S(1)} %bitcast.62, bf16[8,1,72,512]{3,2,0,1:T(8,128)(2,1)S(1)} %bitcast.61), kind=kOutput, calls=%fused_computation.18 | convolution fusion | flops 1362493440 | bytes 7372800 | tf_op jit(solution)/shard_map/phet,pheD->tD/dot_general | solution.py:532
  (21 shorter events, 0.1 us)
Async XLA Ops:
  0.0 171.1 %copy-start = (bf16[1152,1152]{1,0:T(8,128)(2,1)S(1)}, bf16[1152,1152]{1,0:T(8,128)(2,1)}, u32[]{:S(2)}) copy-start(bf16[1152,1152]{1,0:T(8,128)(2,1)} %param.17) | copy-start | bytes 7962628
  0.0 28.6 %copy-start.4 = (bf16[128,1152]{1,0:T(8,128)(2,1)S(1)}, bf16[128,1152]{1,0:T(8,128)(2,1)}, u32[]{:S(2)}) copy-start(bf16[128,1152]{1,0:T(8,128)(2,1)} %param.13) | copy-start | bytes 884740
  30.9 7.5 %copy-start.5 = (f32[3456]{0:T(1024)S(1)}, f32[3456]{0:T(1024)}, u32[]{:S(2)}) copy-start(f32[3456]{0:T(1024)} %param.15) | copy-start | bytes 41476
  30.9 40.4 %all-to-all-start = ((bf16[128,8,1152]{2,1,0:T(8,128)(2,1)}), bf16[128,8,1152]{2,1,0:T(8,128)(2,1)}, u32[]{:S(2)}, u32[]{:S(2)}) async-start(bf16[128,8,1152]{2,1,0:T(8,128)(2,1)} %fusion.11), calls=%async_computation | async-start | bytes 4718592 | tf_op jit(solution)/shard_map/all_to_all | solution.py:502
  56.9 3.6 %copy-start.1 = (bf16[1,512,1152]{2,1,0:T(8,128)(2,1)S(1)}, bf16[1,512,1152]{2,1,0:T(8,128)(2,1)}, u32[]{:S(2)}) copy-start(bf16[1,512,1152]{2,1,0:T(8,128)(2,1)} %param.9) | copy-start | bytes 3538948
  61.3 13.5 %slice-start = ((f32[3456]{0:T(1024)}), f32[2304]{0:T(1024)S(1)}, s32[]{:S(2)}) async-start(f32[3456]{0:T(1024)} %param.15), calls=%async_computation.1 | async-start | bytes 24576 | tf_op jit(solution)/shard_map/slice | solution.py:514
  74.8 6.2 %copy-start.3 = (bf16[512,1152]{1,0:T(8,128)(2,1)}, bf16[512,1152]{1,0:T(8,128)(2,1)S(1)}, u32[]{:S(2)}) copy-start(bf16[512,1152]{1,0:T(8,128)(2,1)S(1)} %select_convert_fusion.act_ref) | copy-start | bytes 3538948
  74.8 6.2 %copy-start.2 = (bf16[1,512,1152]{2,1,0:T(8,128)(2,1)S(1)}, bf16[1,512,1152]{2,1,0:T(8,128)(2,1)}, u32[]{:S(2)}) copy-start(bf16[1,512,1152]{2,1,0:T(8,128)(2,1)} %param.9) | copy-start | bytes 3538948

commit v20 on v19

--- a/solution.py
+++ b/solution.py
@@ -147,11 +147,11 @@
         return carry
 
     if between is None:
-        lax.fori_loop(0, blocks, one_block, 0)
+        lax.fori_loop(0, blocks, one_block, 0, unroll=2)
     else:
         lax.fori_loop(0, span, one_block, 0)
         between()
-        lax.fori_loop(span, blocks, one_block, 0)
+        lax.fori_loop(span, blocks, one_block, 0, unroll=2)
 
 
 def attend_send_kernel(*refs, count, shards, inv_root, stream, pull):

time: 175 us -> 175 us (level)
  no operation moved by 1% of the time
where the time goes in v20:
time: 175 us; the launch traced here: 174 us
  Pallas kernels  109 us (62%)
  local copies, waits for them, and re-layouts  29.8 us (17%)
  matrix products  14.9 us (9%)
  waiting for transfers between devices  9.99 us (6%)
  starting transfers between devices  7.46 us (4%)
  other arithmetic  2.43 us (1%)
    pallas_call x2, Pallas kernels, attend_send(): pl.pallas_call(kernel, out_shape=out_shape, in_specs=[any_spec if pull el...  66.5 us
    pallas_call x1, Pallas kernels, project_send(): pl.pallas_call(kernel, out_shape=shapes * pair + [jax.ShapeDtypeStruct((r...  22.9 us
    pallas_call x1, Pallas kernels, exchange_requests(): pl.pallas_call(functools.partial(request_kernel, groups=groups, shards=sh...  19.1 us
    unnamed x13, local copies, waits for them, and re-layouts  11.4 us
    all_to_all x1, waiting for transfers between devices, per_device(): lax.all_to_all(served, ('region', 'ctx'), split_axis=0, concat_axis=0, ti...  9.99 us
    all_to_all x1, starting transfers between devices, per_device(): lax.all_to_all(served, ('region', 'ctx'), split_axis=0, concat_axis=0, ti...  7.46 us
    transpose x1, local copies, waits for them, and re-layouts, per_device(): w_t = w_qkv.reshape(width, 3, shards, pair, head_dim).transpose(1, 3, 2,...  7.1 us
    dot_general x1, matrix products, per_device(): jnp.dot(activated, w_ada[:, :2 * width], preferred_element_type=jnp.float32)  6.17 us
  transfers between devices with their start and end apart: 1, of which 1 were waited for; matrix products, arithmetic and copies ran while one was open for 13% of the time, Pallas kernels for 0%

profile of v20, /device:TPU:0, one launch (start us, length us, event | category | flops | bytes accessed | tf_op | source)
XLA Modules:
  0.0 174.0 jit_solution(14638900396227664174)
XLA Ops:
  0.0 0.8 compare_select_fusion.1
  0.9 3.6 %gather_fusion = s32[512]{0:T(512)S(1)} fusion(s32[16384]{0:T(1024)} %param.11, s32[1024]{0:T(1024)S(1)} %pad_clamp_fusion), kind=kCustom, calls=%fused_computation | custom fusion | bytes 6144 | tf_op jit(solution)/shard_map/gather | solution.py:477
  5.1 0.3 convert_reduce_fusion.1
  5.4 2.4 %scatter_custom_fusion = s32[1024]{0:T(1024)S(1)} fusion(s32[512]{0:T(512)S(1)} %bitcast.68, s32[512]{0:T(512)S(1)} %get-tuple-element.31, s32[]{:T(128)} %constant.41.clone.1), kind=kCustom, calls=%fused_computation.52 | custom fusion | bytes 4100 | tf_op jit(solution)/shard_map/scatter | solution.py:489
  7.9 0.7 reshape.171.req_ref
  8.6 19.1 %shard_map.91 = s32[128,8]{1,0:T(8,128)} custom-call(s32[128,8]{1,0:T(8,128)} %reshape.171.req_ref), custom_call_target="tpu_custom_call" | custom-call | tf_op jit(solution)/shard_map/pallas_call | solution.py:454
  27.7 0.9 eq.49
  28.7 2.2 %fusion.11 = bf16[128,8,1152]{2,1,0:T(8,128)(2,1)} fusion(bf16[128,1152]{1,0:T(8,128)(2,1)S(1)} %copy-done.4, s32[1024]{0:T(1024)S(1)} %eq.49), kind=kOutput, calls=%fused_computation.8 | convolution fusion | flops 303300608 | bytes 2658304 | tf_op jit(solution)/shard_map/dot_general | solution.py:498
  30.9 7.5 %all-to-all-start = ((bf16[128,8,1152]{2,1,0:T(8,128)(2,1)}), bf16[128,8,1152]{2,1,0:T(8,128)(2,1)}, u32[]{:S(2)}, u32[]{:S(2)}) async-start(bf16[128,8,1152]{2,1,0:T(8,128)(2,1)} %fusion.11), calls=%async_computation | async-start | bytes 4718592 | tf_op jit(solution)/shard_map/all_to_all | solution.py:502
  38.4 11.4 %copy.15 = bf16[1152,3456]{0,1:T(8,128)(2,1)} copy(bf16[1152,3456]{1,0:T(8,128)(2,1)} %param.16) | data formatting | bytes 15925248 | tf_op args[7]
  49.8 7.1 %copy.16 = bf16[3,2,8,72,1152]{4,3,2,1,0:T(8,128)(2,1)} copy(bf16[3,2,8,72,1152]{4,3,1,2,0:T(8,128)(2,1)} %bitcast.64) | data formatting | bytes 15925248 | tf_op jit(solution)/shard_map/transpose | solution.py:525
  56.9 3.6 %slice.22.wg_ref = bf16[1152,1152]{1,0:T(8,128)(2,1)} slice(bf16[1152,3456]{1,0:T(8,128)(2,1)} %param.14), slice={[0:1152], [2304:3456]} | slice | bytes 5308416 | tf_op jit(solution)/shard_map/slice | solution.py:517
  60.5 0.2 convert_reduce_fusion
  60.8 0.5 fusion.20
  61.3 0.0 slice-start
  61.3 10.0 %all-to-all-done = bf16[128,8,1152]{2,1,0:T(8,128)(2,1)} async-done(((bf16[128,8,1152]{2,1,0:T(8,128)(2,1)}), bf16[128,8,1152]{2,1,0:T(8,128)(2,1)}, u32[]{:S(2)}, u32[]{:S(2)}) %all-to-all-start) | async-done | bytes 2359328 | tf_op jit(solution)/shard_map/all_to_all | solution.py:502
  71.3 3.5 %select_convert_fusion.act_ref = bf16[512,1152]{1,0:T(8,128)(2,1)S(1)} fusion(bf16[128,8,1152]{2,1,0:T(8,128)(2,1)} %all-to-all-done, pred[512]{0:T(512)(128)(4,1)S(1)} %iota_compare_fusion.5, s32[512]{0:T(512)S(1)} %select_minimum_fusion), kind=kOutput, calls=%fused_computation.27 | convolution fusion | flops 1212022784 | bytes 3541504 | tf_op jit(solution)/shard_map/dot_general | solution.py:506
  74.8 0.0 copy-start.3
  74.8 6.2 %fusion.8 = f32[512,2304]{1,0:T(8,128)S(1)} fusion(bf16[512,1152]{1,0:T(8,128)(2,1)S(1)} %select_convert_fusion.act_ref, bf16[1152,3456]{1,0:T(8,128)(2,1)} %param.14, f32[2304]{0:T(1024)S(1)} %slice-done), kind=kOutput, calls=%fused_computation.6 | convolution fusion | flops 2721447936 | bytes 11215872 | tf_op jit(solution)/shard_map/dot_general | solution.py:513
  81.0 0.6 fusion.23.mod_ref
  81.6 22.9 %shard_map.92 = (bf16[8,72,512]{2,1,0:T(8,128)(2,1)S(1)}, bf16[8,72,512]{2,1,0:T(8,128)(2,1)S(1)}, bf16[8,72,512]{2,1,0:T(8,128)(2,1)S(1)}, bf16[8,72,512]{2,1,0...) custom-call(bf16[512,1152]{1,0:T(8,128)(2,1)S(1)} %fusion.23.mod_ref, ...), custom_call_target="tpu_custom_call" | custom-call | tf_op jit(solution)/shard_map/pallas_call | solution.py:373
  104.5 33.5 %shard_map.93 = (bf16[8,72,512]{2,1,0:T(8,128)(2,1)S(1)}, bf16[8,72,512]{2,1,0:T(8,128)(2,1)S(1)}, bf16[8,72,512]{2,1,0:T(8,128)(2,1)S(1)}, bf16[8,72,512]{2,1,0:T(8,128)(2,1)S(1)}) custom-call(bf16[8,72,512]{2,1,0:T(8,128)(2,1)S(1)} %get-tuple-element.19.refs_0_, bf16[8,72,512]{2,1,0:T(8,128)(2,1)S(1)} %get-tuple-element.20.refs_1_, ...), custom_call_target="tpu_custom_call" | custom-call | tf_op jit(solution)/shard_map/pallas_call | solution.py:314
  138.0 33.0 %shard_map.94 = (bf16[8,72,512]{2,1,0:T(8,128)(2,1)}, bf16[8,72,512]{2,1,0:T(8,128)(2,1)S(1)}, bf16[8,72,512]{2,1,0:T(8,128)(2,1)S(1)}) custom-call(bf16[8,72,512]{2,1,0:T(8,128)(2,1)S(1)} %get-tuple-element.25.refs_0_, bf16[8,72,512]{2,1,0:T(8,128)(2,1)S(1)} %get-tuple-element.26.refs_1_, bf16[8,72,512]{2,1,0:T(8,128)(2,1)S(1)} %get-tuple-element.27.refs_2_, ...), custom_call_target="tpu_custom_call" | custom-call | tf_op jit(solution)/shard_map/pallas_call | solution.py:314
  171.0 3.0 %fusion.18 = bf16[1,512,1152]{2,1,0:T(8,128)(2,1)} fusion(bf16[1,512,1152]{2,1,0:T(8,128)(2,1)S(1)} %copy-done.2, bf16[8,2,72,1152]{3,2,1,0:T(8,128)(2,1)S(1)} %bitcast.60, bf16[512,1152]{1,0:T(8,128)(2,1)S(1)} %get-tuple-element.18, bf16[8,1,72,512]{3,2,0,1:T(8,128)(2,1)S(1)} %bitcast.62, bf16[8,1,72,512]{3,2,0,1:T(8,128)(2,1)S(1)} %bitcast.61), kind=kOutput, calls=%fused_computation.18 | convolution fusion | flops 1362493440 | bytes 7372800 | tf_op jit(solution)/shard_map/phet,pheD->tD/dot_general | solution.py:532
  (21 shorter events, 0.1 us)
Async XLA Ops:
  0.0 171.0 %copy-start = (bf16[1152,1152]{1,0:T(8,128)(2,1)S(1)}, bf16[1152,1152]{1,0:T(8,128)(2,1)}, u32[]{:S(2)}) copy-start(bf16[1152,1152]{1,0:T(8,128)(2,1)} %param.17) | copy-start | bytes 7962628
  0.0 28.7 %copy-start.4 = (bf16[128,1152]{1,0:T(8,128)(2,1)S(1)}, bf16[128,1152]{1,0:T(8,128)(2,1)}, u32[]{:S(2)}) copy-start(bf16[128,1152]{1,0:T(8,128)(2,1)} %param.13) | copy-start | bytes 884740
  30.9 7.5 %copy-start.5 = (f32[3456]{0:T(1024)S(1)}, f32[3456]{0:T(1024)}, u32[]{:S(2)}) copy-start(f32[3456]{0:T(1024)} %param.15) | copy-start | bytes 41476
  30.9 40.3 %all-to-all-start = ((bf16[128,8,1152]{2,1,0:T(8,128)(2,1)}), bf16[128,8,1152]{2,1,0:T(8,128)(2,1)}, u32[]{:S(2)}, u32[]{:S(2)}) async-start(bf16[128,8,1152]{2,1,0:T(8,128)(2,1)} %fusion.11), calls=%async_computation | async-start | bytes 4718592 | tf_op jit(solution)/shard_map/all_to_all | solution.py:502
  56.9 3.6 %copy-start.1 = (bf16[1,512,1152]{2,1,0:T(8,128)(2,1)S(1)}, bf16[1,512,1152]{2,1,0:T(8,128)(2,1)}, u32[]{:S(2)}) copy-start(bf16[1,512,1152]{2,1,0:T(8,128)(2,1)} %param.9) | copy-start | bytes 3538948
  61.3 13.5 %slice-start = ((f32[3456]{0:T(1024)}), f32[2304]{0:T(1024)S(1)}, s32[]{:S(2)}) async-start(f32[3456]{0:T(1024)} %param.15), calls=%async_computation.1 | async-start | bytes 24576 | tf_op jit(solution)/shard_map/slice | solution.py:514
  74.8 6.2 %copy-start.3 = (bf16[512,1152]{1,0:T(8,128)(2,1)}, bf16[512,1152]{1,0:T(8,128)(2,1)S(1)}, u32[]{:S(2)}) copy-start(bf16[512,1152]{1,0:T(8,128)(2,1)S(1)} %select_convert_fusion.act_ref) | copy-start | bytes 3538948
  74.8 6.2 %copy-start.2 = (bf16[1,512,1152]{2,1,0:T(8,128)(2,1)S(1)}, bf16[1,512,1152]{2,1,0:T(8,128)(2,1)}, u32[]{:S(2)}) copy-start(bf16[1,512,1152]{2,1,0:T(8,128)(2,1)} %param.9) | copy-start | bytes 3538948
